TPU v7x, 32 devices: a whole 2x2x4 slice. The times are simulated.
32 devices in a mesh: region: 8 (over z, x), scen: 4 (over y, core).
Axes of the slice: x: 2, y: 2, z: 4, core: 2. Of those that a mesh axis runs over, the one named last changes fastest.
Arguments:
- inv_blocks: float32 [192, 128, 128], P('region'), may hold values from -0.02 to 3, as said below
- src_amp: float32 [24576], P('region'), may hold values from -5 to 5
- src_phase: float32 [24576], P('region'), may hold values from -3.140625 to 3.140625
- line_a: int32 [8, 256], P('region'), may hold values from 0 to 3071
- line_b: int32 [8, 256], P('region'), may hold values from 0 to 3071
- line_delay: int32 [8, 256], P('region'), may hold values from 2 to 6
- line_yc: float32 [8, 256], P('region'), may hold values from 0.05 to 0.35
- line_atten: float32 [8, 256], P('region'), may hold values from 0.6 to 1
- hist_ua: float32 [8, 6, 128, 256], P('region', None, 'scen'), may hold values from -3 to 3
- hist_ub: float32 [8, 6, 128, 256], P('region', None, 'scen'), may hold values from -3 to 3
- send_node: int32 [8, 8, 64], P('region'), may hold values from -1 to 3071, as said below
- recv_slot: int32 [8, 128], P('region'), may hold values from 0 to 511, as said below
- conv_par: float32 [6, 1024], P(None, 'region'), may hold values from -1.5 to 3, as said below
- conv_state: float32 [2, 128, 1024], P(None, 'scen', 'region'), may hold values from -3 to 3
- fault_node: int32 [128], P('scen'), may hold values from 0 to 24575
- fault_step: int32 [128], P('scen'), may hold values from 0 to 7
- fault_cond: float32 [128], P('scen'), may hold values from 2 to 20
Outputs:
- volts: float32 [128, 24576], P('scen', 'region')
- conv_current: float32 [128, 1024], P('scen', 'region')
- rms_volt: float32 [24576], P('region')
Inputs may be any that keep to these rules, and one draw needn't show every extreme that they name: `send_node`: each region places the same number of converters in every group, and one region places 64 in every group; entries c at or beyond that number are -1, the others are nodes of the region. `recv_slot`: each group's 128 slots name distinct live entries of send_node, and every live entry is named by exactly one slot of its group. `conv_par`: retention lies in 0.5 to 0.98, filter rate in 0.2 to 0.8, current limit in 0.5 to 3. `inv_blocks`: each block is symmetric with a positive diagonal larger than the sum of its row's other magnitudes.
All inputs are finite; a program needn't handle non-finite values.
Results may differ from a plain program's by a relative error of at most 0.0003.
Values sent between devices are 32-bit elements; how exact they have to be, the bound alone decides.
No kernel may reach another device: no remote copies, remote signals or barrier semaphores. Data moves between devices by JAX's collectives and lax.ppermute only.
A program may use at most 64 MiB of HBM per device.

v0:
```python
import functools
from types import SimpleNamespace as Space

import jax
import jax.numpy as jnp
from jax import lax
from jax.experimental import pallas as pl
from jax.experimental.pallas import tpu as pltpu
from jax.sharding import PartitionSpec as P

STEPS = 8
DMIN = 2
LANES = 128
OMEGA = 0.01884955592153876
EPS = 1e-06
F32 = jnp.float32
BF16 = jnp.bfloat16
NN = (((1,), (0,)), ((), ()))
NT = (((1,), (1,)), ((), ()))


def shifted(value, axis, steps):
    count = lax.axis_size(axis)
    pairs = [(source, (source + steps) % count) for source in range(count)]
    return lax.ppermute(value, axis, pairs)


def call(body, name, ins, outs, scratch=(), cost=(1e9, 4e6)):
    leaves, tree = jax.tree.flatten(ins)
    out_names = list(outs)

    def kernel(*refs):
        first, second = len(leaves), len(leaves) + len(out_names)
        i = Space(**jax.tree.unflatten(tree, refs[:first]))
        o = Space(**dict(zip(out_names, refs[first:second])))
        body(i, o, *refs[second:])

    results = pl.pallas_call(
        kernel,
        name=name,
        out_shape=[jax.ShapeDtypeStruct(*outs[key]) for key in out_names],
        in_specs=[pl.BlockSpec(memory_space=pltpu.VMEM)] * len(leaves),
        out_specs=[pl.BlockSpec(memory_space=pltpu.VMEM)] * len(out_names),
        scratch_shapes=list(scratch),
        compiler_params=pltpu.CompilerParams(vmem_limit_bytes=24 << 20),
        cost_estimate=pl.CostEstimate(
            flops=int(cost[0]), bytes_accessed=int(cost[1]), transcendentals=0
        ),
    )(*leaves)
    return Space(**dict(zip(out_names, results)))


def iota(shape, dim):
    return lax.broadcasted_iota(jnp.int32, shape, dim)


def onehot(mask):
    return jnp.where(mask, 1.0, 0.0).astype(BF16)


def dot(left, right, dims=NN):
    return lax.dot_general(left, right, dims, preferred_element_type=F32)


def split2(value):
    high = value.astype(BF16)
    return high, (value - high.astype(F32)).astype(BF16)


def split3(value):
    high, rest = value.astype(BF16), value
    rest = value - high.astype(F32)
    mid = rest.astype(BF16)
    return high, mid, (rest - mid.astype(F32)).astype(BF16)


def product3(left, right_high, right_low, dims=NN):
    rows = left.shape[0]
    high, low = split2(left)
    both = dot(jnp.concatenate([high, low], axis=0), right_high, dims)
    return both[:rows] + both[rows:] + dot(high, right_low, dims)


def as_column(row, size):
    wide = jnp.broadcast_to(row, (size, size))
    return jnp.sum(
        jnp.where(iota((size, size), 0) == iota((size, size), 1), wide, 0.0), axis=1, keepdims=True
    )


def pick(wave, delays, instant, maxd):
    total = None
    for lag in range(DMIN, maxd + 1):
        term = jnp.where(delays == lag, wave(instant - lag), 0.0)
        total = term if total is None else total + term
    return total


def start_body(sizes, i, o):
    regions, cap, half, scen, group, maxd = sizes
    packed = 2 * cap == LANES
    slots = i.slots[...]
    rows = iota((regions * 2 * cap, group), 0)
    if packed:
        target = (slots // cap) * (2 * cap) + slots % cap
        moved = target + cap
    else:
        target = slots
        moved = slots + regions * cap
    left, right = onehot(rows == target), onehot(rows == moved)
    pad = jnp.zeros((half - scen - 6, group), F32)
    upper = jnp.concatenate([i.state[0], i.par[...], pad], axis=0)
    lower = jnp.concatenate([i.state[1], jnp.zeros((half - scen, group), F32)], axis=0)
    buffer = None
    for part, mask in ((upper, left), (lower, right)):
        both = dot(jnp.concatenate(split3(part), axis=0), mask, NT)
        value = both[:half] + both[half : 2 * half] + both[2 * half :]
        buffer = value if buffer is None else buffer + value
    if packed:
        for region in range(regions):
            o.send[region] = buffer[:, region * LANES : (region + 1) * LANES]
    else:
        o.send[...] = buffer
    delays = i.delay[...]
    for step in range(2):
        o.into[step] = pick(lambda t: i.hist[t + maxd], delays, step, maxd)


def model_body(sizes, i, o, spots, base, acc):
    nreg, nblk, lines, width, scen = sizes
    blk = LANES
    points = 2 * lines + width
    whole = points + blk
    spots[...] = jnp.full((1, whole), -1, jnp.int32)
    spots[:, 0:lines] = i.end_a[...]
    spots[:, lines : 2 * lines] = i.end_b[...]
    spots[:, 2 * lines : points] = i.conv[...]
    region = lax.axis_index("region")
    fault = i.fault_node[...] - region * nreg
    fault = jnp.where((fault >= 0) & (fault < nreg), fault, -1)
    spots[:, points : points + scen] = fault
    row = spots[...]
    row_blk, row_in = row >> 7, row & 127
    column = jnp.transpose(jnp.broadcast_to(row.astype(F32), (blk, whole))).astype(jnp.int32)
    column_blk = column >> 7
    o.spots[...] = column[:points]
    o.fault_blk[...] = column_blk[points : points + scen]
    z = i.inv[...].reshape(nreg, blk)
    z_high, z_low = split2(z)
    o.zcat[:, 0:blk] = z_high
    o.zcat[:, blk:] = z_low
    acc[...] = jnp.zeros_like(acc)
    lane = iota((whole, blk), 1)
    span = 2 * blk

    def gather(step, carry):
        start = pl.multiple_of(step * span, span)
        mine = jnp.concatenate(
            [onehot(column == lane + start), onehot(column == lane + (start + blk))], axis=1
        )
        acc[...] += dot(mine, o.zcat[pl.ds(start, span), :])
        return carry

    lax.fori_loop(0, nblk // 2, gather, 0)
    inside = onehot(iota((blk, points), 0) == row_in[:, :points])
    row_blk_p = row_blk[:, :points]

    def between(step, carry):
        start = pl.multiple_of(step * blk, blk)
        rows = acc[pl.ds(start, blk), :].astype(BF16)
        mine = o.spots[pl.ds(start, blk), :][:, 0:1] >> 7
        same = mine == row_blk_p
        both = dot(jnp.concatenate([rows[:, :blk], rows[:, blk:]], axis=0), inside)
        o.m_high[pl.ds(start, blk), :] = jnp.where(same, both[:blk], 0.0).astype(BF16)
        o.m_low[pl.ds(start, blk), :] = jnp.where(same, both[blk:], 0.0).astype(BF16)
        return carry

    lax.fori_loop(0, points // blk, between, 0)
    fault_rows = acc[points : points + scen, :]
    fault_z = fault_rows[:, :blk] + fault_rows[:, blk:]
    o.fault_z[...] = fault_z
    fault_blk = column_blk[points : points + scen]
    both = dot(
        jnp.concatenate([fault_rows[:, :blk], fault_rows[:, blk:]], axis=0).astype(BF16), inside
    )
    o.fault_p[...] = jnp.where(
        fault_blk[:, 0:1] == row_blk_p, both[:scen] + both[scen:], 0.0
    )
    instant = iota((STEPS, nreg), 0).astype(F32)
    source = i.amp[...] * jnp.cos(OMEGA * instant + i.phase[...])
    base[...] = jnp.concatenate(
        [source[:, k * blk : (k + 1) * blk] for k in range(nblk)], axis=0
    )
    for k in range(nblk):
        mine = o.zcat[k * blk : (k + 1) * blk, :]
        o.base[:, k * blk : (k + 1) * blk] = product3(
            base[k * STEPS : (k + 1) * STEPS, :], mine[:, :blk], mine[:, blk:]
        )
    rows = acc[...].astype(BF16)
    spread = product3(base[...], rows[:, :blk], rows[:, blk:], NT)
    at_points = jnp.zeros((STEPS, whole), F32)
    for k in range(nblk):
        at_points = at_points + jnp.where(row_blk == k, spread[k * STEPS : (k + 1) * STEPS], 0.0)
    o.base_p[...] = at_points[:, :points]
    tail = jnp.concatenate(
        [at_points[:, points:], jnp.zeros((blk - STEPS, blk), F32)], axis=0
    )
    o.fault_base[...] = jnp.transpose(tail)[:scen]
    self_imp = jnp.sum(
        jnp.where(iota((scen, blk), 1) == (column[points : points + scen] & 127), fault_z, 0.0),
        axis=1,
        keepdims=True,
    )
    cond = as_column(i.fault_cond[...], scen)
    closes = as_column(i.fault_step[...].astype(F32), scen)
    ratio = cond / (1.0 + cond * self_imp)
    o.fault_ratio[...] = jnp.where(
        closes <= iota((scen, blk), 1).astype(F32), jnp.broadcast_to(ratio, (scen, blk)), 0.0
    )


def advance_body(sizes, pair, i, o):
    lines, width, scen, cap, maxd, packed = sizes
    t0 = 2 * pair
    delays = i.delay[...]
    scale = i.atten[...]
    twice = 2.0 * i.admit[...]
    last = STEPS - 1

    fresh = {}
    if pair:
        for j in range(2):
            fresh[t0 - 2 + j] = scale * (twice * i.far_volts[j] - i.into_prev[j])
            if hasattr(o, "back"):
                o.back[j] = fresh[t0 - 2 + j]

    def back(t):
        if t in fresh:
            return fresh[t]
        if t < 0:
            return i.hist_b[t + maxd]
        return i.backs[t // 2][t % 2]

    made = {}

    def out(t):
        if t in made:
            return made[t]
        if t < 0:
            return i.hist_a[t + maxd]
        return i.made[t // 2][t % 2]

    live = i.conv[...] >= 0
    if packed:
        low = iota((1, LANES), 1) < cap
        params = []
        for row in range(6):
            pieces = []
            for j in range(width // LANES):
                one = i.recv[2 * j][scen + row : scen + row + 1, :]
                two = i.recv[2 * j + 1][scen + row : scen + row + 1, :]
                pieces.append(jnp.where(low, one, pltpu.roll(two, cap, 1)))
            params.append(jnp.concatenate(pieces, axis=1))
    else:
        params = [i.recv[0, scen + row : scen + row + 1, :] for row in range(6)]
    params[5] = jnp.where(live, params[5], 1.0)

    def drive(second):
        return params[5] * jnp.tanh((params[4] + second) / params[5])

    if pair:
        first, second, current = i.state[0], i.state[1], i.current[...]
    else:
        if packed:
            ups, downs = [], []
            for j in range(width // LANES):
                one, two = i.recv[2 * j][:scen], i.recv[2 * j + 1][:scen]
                ups.append(jnp.where(low, one, pltpu.roll(two, cap, 1)))
                downs.append(jnp.where(low, pltpu.roll(one, cap, 1), two))
            first, second = jnp.concatenate(ups, axis=1), jnp.concatenate(downs, axis=1)
        else:
            first, second = i.recv[0, :scen], i.recv[1, :scen]
        current = drive(second)

    fault_p = i.fault_p[...]
    for j in range(2):
        t = t0 + j
        into = pick(back, delays, t, maxd)
        x = jnp.concatenate([into, i.far_in[j], current], axis=1)
        high, low_part = split2(x)
        o.x[j * scen : (j + 1) * scen, :] = high
        o.x[(2 + j) * scen : (3 + j) * scen, :] = low_part
        both = dot(jnp.concatenate([high, low_part], axis=0), i.m_high[...])
        volts = both[:scen] + both[scen:] + dot(high, i.m_low[...])
        volts = volts + i.base_p[t : t + 1, :]
        at_fault = i.fault_base[:, t : t + 1] + jnp.sum(x * fault_p, axis=1, keepdims=True)
        coef = i.fault_ratio[:, t : t + 1] * at_fault
        o.coef[j * scen : (j + 1) * scen, :] = jnp.broadcast_to(coef, (scen, LANES))
        volts = volts - fault_p * coef
        if t <= last - DMIN:
            made[t] = scale * (twice * volts[:, :lines] - into)
            o.ends[j] = volts[:, lines : 2 * lines]
            if hasattr(o, "out"):
                o.out[j] = made[t]
        node = volts[:, 2 * lines :]
        first = params[1] * first + params[2] * (params[0] - node)
        second = second + params[3] * (first - second)
        current = drive(second)
    if hasattr(o, "into"):
        for j in range(2):
            o.into[j] = pick(out, delays, t0 + 2 + j, maxd)
    if hasattr(o, "state"):
        o.state[0] = first
        o.state[1] = second
    if t0 + 2 < STEPS or not packed:
        o.current[...] = current
    else:
        half = scen // 2
        for j in range(width // LANES):
            mine = current[:, j * LANES : (j + 1) * LANES]
            top, bottom = mine[:half], mine[half:]
            o.current[2 * j] = jnp.where(low, top, pltpu.roll(bottom, cap, 1))
            o.current[2 * j + 1] = jnp.where(low, pltpu.roll(top, cap, 1), bottom)


def full_body(sizes, pair, i, o):
    nblk, points, scen = sizes
    blk = LANES
    t0 = 2 * pair
    spots = i.spots
    fault_z = i.fault_z[...]
    fault_blk = i.fault_blk[...]
    x = i.x[...]
    lane = iota((points, blk), 1)
    coef = i.coef[...]

    def step(index, carry):
        start = pl.multiple_of(index * 2 * blk, 2 * blk)
        where = spots[...]
        mine = jnp.concatenate(
            [onehot(where == lane + start), onehot(where == lane + (start + blk))], axis=1
        )
        both = dot(x, mine)
        inject = both[: 2 * scen] + both[2 * scen :]
        for j in range(2):
            here = pl.ds(pl.multiple_of(start + j * blk, blk), blk)
            z = i.zcat[here, :]
            volts = product3(inject[:, j * blk : (j + 1) * blk], z[:, :blk], z[:, blk:])
            base = i.base[:, here]
            volts = volts + jnp.concatenate(
                [
                    jnp.broadcast_to(base[t0 + m : t0 + m + 1, :], (scen, blk))
                    for m in range(2)
                ],
                axis=0,
            )
            column = jnp.where(fault_blk == 2 * index + j, fault_z, 0.0)
            volts = volts - jnp.concatenate([column, column], axis=0) * coef
            total = jnp.sum(volts * volts, axis=0, keepdims=True)
            if hasattr(i, "squares"):
                total = total + i.squares[:, here]
            o.squares[:, here] = total
            if hasattr(o, "volts"):
                o.volts[:, here] = volts[scen:]
        return carry

    lax.fori_loop(0, nblk // 2, step, 0)


def finish_body(sizes, i, o):
    regions, cap, scen, group, count, packed = sizes
    parts = [i.parts[k][...] for k in range(count)]
    while len(parts) > 1:
        parts = [parts[k] + parts[k + 1] for k in range(0, len(parts), 2)]
    o.rms[...] = jnp.sqrt(parts[0] / (scen * count * STEPS) + EPS)
    slots = i.slots[...]
    if packed:
        half = scen // 2
        lane = iota((LANES, group), 0)
        top = bottom = None
        for region in range(regions):
            left = onehot((lane < cap) & (slots == region * cap + lane))
            right = onehot((lane >= cap) & (slots == (region - 1) * cap + lane))
            both = dot(
                jnp.concatenate(split3(i.recv[region]), axis=0),
                jnp.concatenate([left, right], axis=1),
            )
            value = both[:half] + both[half : 2 * half] + both[2 * half :]
            top = value if top is None else top + value
        o.current[:half, :] = top[:, :group]
        o.current[half:, :] = top[:, group:]
    else:
        mask = onehot(iota((regions * cap, group), 0) == slots)
        both = dot(jnp.concatenate(split3(i.recv[...]), axis=0), mask)
        o.current[...] = both[:scen] + both[scen : 2 * scen] + both[2 * scen :]


def per_device(
    inv_blocks,
    src_amp,
    src_phase,
    line_a,
    line_b,
    line_delay,
    line_yc,
    line_atten,
    hist_ua,
    hist_ub,
    send_node,
    recv_slot,
    conv_par,
    conv_state,
    fault_node,
    fault_step,
    fault_cond,
):
    nblk, blk = inv_blocks.shape[0], inv_blocks.shape[1]
    nreg = nblk * blk
    lines = line_a.shape[1]
    maxd, scen = hist_ua.shape[1], hist_ua.shape[2]
    regions, cap = send_node.shape[1], send_node.shape[2]
    group = recv_slot.shape[1]
    width = regions * cap
    points = 2 * lines + width
    count = lax.axis_size("scen")
    packed = 2 * cap == LANES
    half = scen + 8
    hist_a, hist_b = hist_ua[0], hist_ub[0]
    conv = send_node.reshape(1, width)

    send_shape = (regions, half, LANES) if packed else (half, regions * 2 * cap)
    head = call(
        functools.partial(start_body, (regions, cap, half, scen, group, maxd)),
        "start",
        dict(slots=recv_slot, par=conv_par, state=conv_state, hist=hist_a, delay=line_delay),
        dict(send=(send_shape, F32), into=((2, scen, lines), F32)),
    )
    send = head.send
    if packed:
        recv = lax.all_to_all(send, "region", split_axis=0, concat_axis=0, tiled=True)
    else:
        send = send.reshape(half, 2, regions, cap).transpose(2, 1, 0, 3)
        recv = lax.all_to_all(send, "region", split_axis=0, concat_axis=0, tiled=True)
        recv = recv.transpose(1, 2, 0, 3).reshape(2, half, width)
    into = head.into
    far_in = shifted(into, "region", 1)

    model = call(
        functools.partial(model_body, (nreg, nblk, lines, width, scen)),
        "model",
        dict(
            inv=inv_blocks,
            amp=src_amp.reshape(1, nreg),
            phase=src_phase.reshape(1, nreg),
            end_a=line_a,
            end_b=line_b,
            conv=conv,
            fault_node=fault_node.reshape(1, scen),
            fault_step=fault_step.reshape(1, scen),
            fault_cond=fault_cond.reshape(1, scen),
        ),
        dict(
            spots=((points, blk), jnp.int32),
            zcat=((nreg, 2 * blk), BF16),
            m_high=((points, points), BF16),
            m_low=((points, points), BF16),
            base=((STEPS, nreg), F32),
            base_p=((STEPS, points), F32),
            fault_p=((scen, points), F32),
            fault_z=((scen, blk), F32),
            fault_blk=((scen, blk), jnp.int32),
            fault_base=((scen, blk), F32),
            fault_ratio=((scen, blk), F32),
        ),
        scratch=(
            pltpu.VMEM((1, points + blk), jnp.int32),
            pltpu.VMEM((STEPS * nblk, blk), F32),
            pltpu.VMEM((points + blk, 2 * blk), F32),
        ),
        cost=(4e9, 2e7),
    )

    wave = ((2, scen, lines), F32)
    mades, backs, carry = {}, {}, {}
    squares = far_volts = sent = None
    for pair in range(STEPS // 2):
        t0 = 2 * pair
        final = t0 + 2 >= STEPS
        ins = dict(
            delay=line_delay,
            atten=line_atten,
            admit=line_yc,
            conv=conv,
            recv=recv,
            far_in=far_in,
            m_high=model.m_high,
            m_low=model.m_low,
            base_p=model.base_p,
            fault_p=model.fault_p,
            fault_base=model.fault_base,
            fault_ratio=model.fault_ratio,
            **carry,
        )
        if t0 - maxd < 0:
            ins.update(hist_b=hist_b)
        if pair:
            ins.update(far_volts=far_volts, into_prev=sent)
        first = max(0, pair - 3)
        ins.update(backs={k: v for k, v in backs.items() if k >= first})
        if not final:
            ins.update(made={k: v for k, v in mades.items() if k >= pair - 2})
            if t0 + 2 - maxd < 0:
                ins.update(hist_a=hist_a)
        outs = dict(x=((4 * scen, points), BF16), coef=((2 * scen, LANES), F32))
        if not final:
            outs.update(
                ends=wave,
                out=wave,
                into=wave,
                state=((2, scen, width), F32),
                current=((scen, width), F32),
            )
            if pair:
                outs.update(back=wave)
        else:
            shape = (regions, scen // 2, LANES) if packed else (scen, width)
            outs.update(current=(shape, F32))
        made = call(
            functools.partial(advance_body, (lines, width, scen, cap, maxd, packed), pair),
            "advance",
            ins,
            outs,
        )
        if not final:
            sent, into = into, made.into
            far_in = shifted(into, "region", 1)
            far_volts = shifted(made.ends, "region", -1)
            mades[pair] = made.out
            if pair:
                backs[pair - 1] = made.back
            carry = dict(state=made.state, current=made.current)
        else:
            current = made.current
            if packed:
                returned = lax.all_to_all(
                    current, "region", split_axis=0, concat_axis=0, tiled=True
                )
            else:
                current = current.reshape(scen, regions, cap).transpose(1, 0, 2)
                returned = lax.all_to_all(
                    current, "region", split_axis=0, concat_axis=0, tiled=True
                )
                returned = returned.transpose(1, 0, 2).reshape(scen, width)
        ins = dict(
            x=made.x,
            coef=made.coef,
            spots=model.spots,
            zcat=model.zcat,
            base=model.base,
            fault_z=model.fault_z,
            fault_blk=model.fault_blk,
        )
        if pair:
            ins.update(squares=squares)
        outs = dict(squares=((1, nreg), F32))
        if final:
            outs.update(volts=((scen, nreg), F32))
        full = call(
            functools.partial(full_body, (nblk, points, scen), pair),
            "full",
            ins,
            outs,
            cost=(4e9, 1e7),
        )
        squares = full.squares

    parts = [squares]
    for offset in range(1, count):
        pairs = [(source, source ^ offset) for source in range(count)]
        parts.append(lax.ppermute(squares, "scen", pairs))
    tail = call(
        functools.partial(finish_body, (regions, cap, scen, group, count, packed)),
        "finish",
        dict(slots=recv_slot, recv=returned, parts=parts),
        dict(rms=((1, nreg), F32), current=((scen, group), F32)),
    )
    return full.volts, tail.current, tail.rms.reshape(nreg)


def solution(mesh):
    return jax.shard_map(
        per_device,
        mesh=mesh,
        in_specs=(
            P("region", None, None),
            P("region"),
            P("region"),
            P("region", None),
            P("region", None),
            P("region", None),
            P("region", None),
            P("region", None),
            P("region", None, "scen", None),
            P("region", None, "scen", None),
            P("region", None, None),
            P("region", None),
            P(None, "region"),
            P(None, "scen", "region"),
            P("scen"),
            P("scen"),
            P("scen"),
        ),
        out_specs=(P("scen", "region"), P("scen", "region"), P("region")),
        check_vma=False,
    )
```

profile of v0, /device:TPU:0, one launch (start us, length us, event | category | flops | bytes accessed | tf_op | source)
XLA Modules:
  0.0 82.6 jit_solution(8900232889764569753)
XLA Ops:
  5.5 7.3 %all-to-all-start = ((f32[8,40,128]{2,1,0:T(8,128)}), f32[8,40,128]{2,1,0:T(8,128)S(1)}, u32[]{:S(2)}, u32[]{:S(2)}) async-start(f32[8,40,128]{2,1,0:T(8,128)} %get-tuple-element.53), calls=%async_computation | async-start | bytes 327680 | tf_op jit(solution)/shard_map/all_to_all | solution.py:440
  12.7 2.0 %collective-permute-start = (f32[2,32,256]{2,1,0:T(8,128)S(1)}, f32[2,32,256]{2,1,0:T(8,128)S(1)}, u32[]{:S(2)}, u32[]{:S(2)}) collective-permute-start(f32[2,32,256]{2,1,0:T(8,128)S(1)} %get-tuple-element.47.refs_13_), channel_id=1, source_target_pairs={{0,4},{4,8},{8,12},{12,16},{16,20},{20,24},{24,28},{28,0},{1,5},{5... | collective-permute-start | bytes 196616 | tf_op jit(solution)/shard_map/ppermute | solution.py:25
  14.9 1.4 %copy-done.10 = f32[24,128,128]{2,1,0:T(8,128)S(1)} copy-done((f32[24,128,128]{2,1,0:T(8,128)S(1)}, f32[24,128,128]{2,1,0:T(8,128)}, u32[]{:S(2)}) %copy-start.10) | copy-done | bytes 1572888
  16.3 8.0 %model.1 = (s32[1024,128]{1,0:T(8,128)S(1)}, bf16[3072,256]{1,0:T(8,128)(2,1)S(1)}, bf16[1024,1024]{1,0:T(8,128)(2,1)S(1)}, bf16[1024,1024]{1,0:T(8,128)(2,1)S(1...) custom-call(f32[1,3072]{1,0:T(1,128)S(1)} %bitcast.14, ...), custom_call_target="tpu_custom_call" | custom-call | flops 4000000000 | bytes 20000000 | tf_op jit(solution)/shard_map/model/pallas_call | solution.py:38
  24.4 1.3 %copy-done = bf16[1024,1024]{1,0:T(8,128)(2,1)} copy-done((bf16[1024,1024]{1,0:T(8,128)(2,1)}, bf16[1024,1024]{1,0:T(8,128)(2,1)S(1)}, u32[]{:S(2)}) %copy-start) | copy-done | bytes 2097176
  25.7 1.2 %copy-done.22 = bf16[3072,256]{1,0:T(8,128)(2,1)} copy-done((bf16[3072,256]{1,0:T(8,128)(2,1)}, bf16[3072,256]{1,0:T(8,128)(2,1)S(1)}, u32[]{:S(2)}) %copy-start.22) | copy-done | bytes 1572888
  28.4 1.6 %copy-done.1 = bf16[1024,1024]{1,0:T(8,128)(2,1)S(1)} copy-done((bf16[1024,1024]{1,0:T(8,128)(2,1)S(1)}, bf16[1024,1024]{1,0:T(8,128)(2,1)}, u32[]{:S(2)}) %copy-start.1) | copy-done | bytes 2097176
  29.9 1.6 %advance.4 = (bf16[128,1024]{1,0:T(8,128)(2,1)S(1)}, f32[64,128]{1,0:T(8,128)S(1)}, f32[2,32,256]{2,1,0:T(8,128)S(1)}, f32[2,32,256]{2,1,0:T(8,128)S(1)}, f32[2,...) custom-call(f32[1,256]{1,0:T(1,128)S(1)} %copy-done.6, f32[1,256]{1,0:T(1,128)S(1)} %copy-done.7, ...), custom_call_target="tpu_custom_call" | custom-call | flops 1000000000 | bytes 4000000 | tf_op jit(solution)/shard_map/advance/pallas_call | solution.py:38
  31.6 2.8 %collective-permute-start.2 = (f32[2,32,256]{2,1,0:T(8,128)S(1)}, f32[2,32,256]{2,1,0:T(8,128)S(1)}, u32[]{:S(2)}, u32[]{:S(2)}) collective-permute-start(f32[2,32,256]{2,1,0:T(8,128)S(1)} %get-tuple-element.56), channel_id=1, source_target_pairs={{0,28},{4,0},{8,4},{12,8},{16,12},{20,16},{24,20},{28,24},{1,29},{... | collective-permute-start | bytes 196616 | tf_op jit(solution)/shard_map/ppermute | solution.py:25
  34.4 5.4 %full.4.refs_5_ = f32[1,3072]{1,0:T(1,128)S(1)} custom-call(f32[8,3072]{1,0:T(8,128)S(1)} %copy-done.28, f32[64,128]{1,0:T(8,128)S(1)} %get-tuple-element.76.refs_1_, s32[32,128]{1,0:T(8,128)S(1)} %get-tuple-element.71.refs_2_, f32[32,128]{1,0:T(8,128)S(1)} %get-tuple-element.72.refs_3_, s32[1024,128]{1,0:T(8,128)S(1)} %copy-done.26, ...), custom_call_target="tpu_custom_call" | custom-call | flops 4000000000 | bytes 10000000 | tf_op jit(solution)/shard_map/full/pallas_call | solution.py:38
  39.8 1.5 %collective-permute-done.1.refs_6_ = f32[2,32,256]{2,1,0:T(8,128)S(1)} collective-permute-done((f32[2,32,256]{2,1,0:T(8,128)S(1)}, f32[2,32,256]{2,1,0:T(8,128)S(1)}, u32[]{:S(2)}, u32[]{:S(2)}) %collective-permute-start.1) | collective-permute-done | bytes 65568 | tf_op jit(solution)/shard_map/ppermute | solution.py:25
  41.3 1.6 %advance.5 = (bf16[128,1024]{1,0:T(8,128)(2,1)S(1)}, f32[64,128]{1,0:T(8,128)S(1)}, f32[2,32,256]{2,1,0:T(8,128)S(1)}, f32[2,32,256]{2,1,0:T(8,128)S(1)}, f32[2,...) custom-call(f32[1,256]{1,0:T(1,128)S(1)} %copy-done.6, ...), custom_call_target="tpu_custom_call" | custom-call | flops 1000000000 | bytes 4000000 | tf_op jit(solution)/shard_map/advance/pallas_call | solution.py:38
  43.0 3.3 %collective-permute-start.4 = (f32[2,32,256]{2,1,0:T(8,128)S(1)}, f32[2,32,256]{2,1,0:T(8,128)S(1)}, u32[]{:S(2)}, u32[]{:S(2)}) collective-permute-start(f32[2,32,256]{2,1,0:T(8,128)S(1)} %get-tuple-element.62), channel_id=1, source_target_pairs={{0,28},{4,0},{8,4},{12,8},{16,12},{20,16},{24,20},{28,24},{1,29},{... | collective-permute-start | bytes 196616 | tf_op jit(solution)/shard_map/ppermute | solution.py:25
  46.3 5.4 %full.5.refs_5_ = f32[1,3072]{1,0:T(1,128)S(1)} custom-call(f32[8,3072]{1,0:T(8,128)S(1)} %copy-done.28, f32[64,128]{1,0:T(8,128)S(1)} %get-tuple-element.75.refs_1_, s32[32,128]{1,0:T(8,128)S(1)} %get-tuple-element.71.refs_2_, f32[32,128]{1,0:T(8,128)S(1)} %get-tuple-element.72.refs_3_, s32[1024,128]{1,0:T(8,128)S(1)} %copy-done.26, ...), custom_call_target="tpu_custom_call" | custom-call | flops 4000000000 | bytes 10000000 | tf_op jit(solution)/shard_map/full/pallas_call | solution.py:38
  51.7 1.5 %collective-permute-done.3.refs_7_ = f32[2,32,256]{2,1,0:T(8,128)S(1)} collective-permute-done((f32[2,32,256]{2,1,0:T(8,128)S(1)}, f32[2,32,256]{2,1,0:T(8,128)S(1)}, u32[]{:S(2)}, u32[]{:S(2)}) %collective-permute-start.3) | collective-permute-done | bytes 65568 | tf_op jit(solution)/shard_map/ppermute | solution.py:25
  53.2 2.1 %advance.6 = (bf16[128,1024]{1,0:T(8,128)(2,1)S(1)}, f32[64,128]{1,0:T(8,128)S(1)}, f32[2,32,256]{2,1,0:T(8,128)S(1)}, f32[2,32,256]{2,1,0:T(8,128)}, f32[2,32,2...) custom-call(f32[1,256]{1,0:T(1,128)S(1)} %copy-done.6, ...), custom_call_target="tpu_custom_call" | custom-call | flops 1000000000 | bytes 4000000 | tf_op jit(solution)/shard_map/advance/pallas_call | solution.py:38
  55.3 4.7 %collective-permute-start.6 = (f32[2,32,256]{2,1,0:T(8,128)S(1)}, f32[2,32,256]{2,1,0:T(8,128)S(1)}, u32[]{:S(2)}, u32[]{:S(2)}) collective-permute-start(f32[2,32,256]{2,1,0:T(8,128)S(1)} %get-tuple-element.68), channel_id=1, source_target_pairs={{0,28},{4,0},{8,4},{12,8},{16,12},{20,16},{24,20},{28,24},{1,29},{... | collective-permute-start | bytes 196616 | tf_op jit(solution)/shard_map/ppermute | solution.py:25
  60.1 5.4 %full.6.refs_5_ = f32[1,3072]{1,0:T(1,128)S(1)} custom-call(f32[8,3072]{1,0:T(8,128)S(1)} %copy-done.28, f32[64,128]{1,0:T(8,128)S(1)} %get-tuple-element.74.refs_1_, s32[32,128]{1,0:T(8,128)S(1)} %get-tuple-element.71.refs_2_, f32[32,128]{1,0:T(8,128)S(1)} %get-tuple-element.72.refs_3_, s32[1024,128]{1,0:T(8,128)S(1)} %copy-done.26, ...), custom_call_target="tpu_custom_call" | custom-call | flops 4000000000 | bytes 10000000 | tf_op jit(solution)/shard_map/full/pallas_call | solution.py:38
  65.5 1.6 %advance.7 = (bf16[128,1024]{1,0:T(8,128)(2,1)S(1)}, f32[64,128]{1,0:T(8,128)S(1)}, f32[8,16,128]{2,1,0:T(8,128)}) custom-call(f32[1,256]{1,0:T(1,128)S(1)} %copy-done.6, f32[1,256]{1,0:T(1,128)S(1)} %copy-done.7, f32[2,32,256]{2,1,0:T(8,128)S(1)} %get-tuple-element.59.refs_2_, f32[2,32,256]{2,1,0:T(8,128)S(1)} %get-tuple-element.65.refs_3_, ...), custom_call_target="tpu_custom_call" | custom-call | flops 1000000000 | bytes 4000000 | tf_op jit(solution)/shard_map/advance/pallas_call | solution.py:38
  67.1 3.3 %all-to-all-start.1 = ((f32[8,16,128]{2,1,0:T(8,128)}), f32[8,16,128]{2,1,0:T(8,128)S(1)}, u32[]{:S(2)}, u32[]{:S(2)}) async-start(f32[8,16,128]{2,1,0:T(8,128)} %get-tuple-element.84), calls=%async_computation.1 | async-start | bytes 131072 | tf_op jit(solution)/shard_map/all_to_all | solution.py:545
  70.5 1.4 %copy-done.24 = bf16[3072,256]{1,0:T(8,128)(2,1)S(1)} copy-done((bf16[3072,256]{1,0:T(8,128)(2,1)S(1)}, bf16[3072,256]{1,0:T(8,128)(2,1)}, u32[]{:S(2)}) %copy-start.24) | copy-done | bytes 1572888
  71.9 6.2 %full.7 = (f32[1,3072]{1,0:T(1,128)S(1)}, f32[32,3072]{1,0:T(8,128)}) custom-call(f32[8,3072]{1,0:T(8,128)S(1)} %copy-done.29, f32[64,128]{1,0:T(8,128)S(1)} %get-tuple-element.70.refs_1_, s32[32,128]{1,0:T(8,128)S(1)} %get-tuple-element.71.refs_2_, f32[32,128]{1,0:T(8,128)S(1)} %get-tuple-element.72.refs_3_, s32[1024,128]{1,0:T(8,128)S(1)} %copy-done.26, ...), custom_call_target="tpu_custom_call" | custom-call | flops 4000000000 | bytes 10000000 | tf_op jit(solution)/shard_map/full/pallas_call | solution.py:38
  78.1 1.5 %collective-permute-start.8 = (f32[1,3072]{1,0:T(1,128)S(1)}, f32[1,3072]{1,0:T(1,128)S(1)}, u32[]{:S(2)}, u32[]{:S(2)}) collective-permute-start(f32[1,3072]{1,0:T(1,128)S(1)} %get-tuple-element.83.refs_0_), channel_id=1, source_target_pairs={{0,2},{1,3},{2,0},{3,1},{4,6},{5,7},{6,4},{7,5},{8,10},{9,11},{10,... | collective-permute-start | bytes 36872 | tf_op jit(solution)/shard_map/ppermute | solution.py:580
  79.9 1.3 %collective-permute-done.9.refs_3_ = f32[1,3072]{1,0:T(1,128)S(1)} collective-permute-done((f32[1,3072]{1,0:T(1,128)S(1)}, f32[1,3072]{1,0:T(1,128)S(1)}, u32[]{:S(2)}, u32[]{:S(2)}) %collective-permute-start.9) | collective-permute-done | bytes 12320 | tf_op jit(solution)/shard_map/ppermute | solution.py:580
  (74 shorter events, 8.1 us)
Async XLA Ops:
  0.6 14.2 %copy-start.17 = (f32[32]{0:T(128)S(1)}, f32[32]{0:T(128)}, u32[]{:S(2)}) copy-start(f32[32]{0:T(128)} %param.33) | copy-start | bytes 388
  0.6 14.2 %copy-start.15 = (s32[1,256]{1,0:T(1,128)S(1)}, s32[1,256]{1,0:T(1,128)}, u32[]{:S(2)}) copy-start(s32[1,256]{1,0:T(1,128)} %refs_2_.2) | copy-start | bytes 3076
  4.4 10.5 %copy-start.12 = (f32[3072]{0:T(1024)S(1)}, f32[3072]{0:T(1024)}, u32[]{:S(2)}) copy-start(f32[3072]{0:T(1024)} %param.18) | copy-start | bytes 36868
  4.4 10.5 %copy-start.13 = (f32[3072]{0:T(1024)S(1)}, f32[3072]{0:T(1024)}, u32[]{:S(2)}) copy-start(f32[3072]{0:T(1024)} %param.19) | copy-start | bytes 36868
  4.4 10.5 %copy-start.16 = (s32[1,256]{1,0:T(1,128)S(1)}, s32[1,256]{1,0:T(1,128)}, u32[]{:S(2)}) copy-start(s32[1,256]{1,0:T(1,128)} %refs_3_.2) | copy-start | bytes 3076
  4.4 10.5 %copy-start.18 = (s32[32]{0:T(128)S(1)}, s32[32]{0:T(128)}, u32[]{:S(2)}) copy-start(s32[32]{0:T(128)} %param.31) | copy-start | bytes 388
  4.4 10.5 %copy-start.19 = (s32[32]{0:T(128)S(1)}, s32[32]{0:T(128)}, u32[]{:S(2)}) copy-start(s32[32]{0:T(128)} %param.32) | copy-start | bytes 388
  5.5 22.8 %all-to-all-start = ((f32[8,40,128]{2,1,0:T(8,128)}), f32[8,40,128]{2,1,0:T(8,128)S(1)}, u32[]{:S(2)}, u32[]{:S(2)}) async-start(f32[8,40,128]{2,1,0:T(8,128)} %get-tuple-element.53), calls=%async_computation | async-start | bytes 327680 | tf_op jit(solution)/shard_map/all_to_all | solution.py:440
  12.7 15.6 %collective-permute-start = (f32[2,32,256]{2,1,0:T(8,128)S(1)}, f32[2,32,256]{2,1,0:T(8,128)S(1)}, u32[]{:S(2)}, u32[]{:S(2)}) collective-permute-start(f32[2,32,256]{2,1,0:T(8,128)S(1)} %get-tuple-element.47.refs_13_), channel_id=1, source_target_pairs={{0,4},{4,8},{8,12},{12,16},{16,20},{20,24},{24,28},{28,0},{1,5},{5... | collective-permute-start | bytes 196616 | tf_op jit(solution)/shard_map/ppermute | solution.py:25
  16.3 12.0 %copy-start.3 = (f32[1,6,32,256]{3,2,1,0:T(8,128)S(1)}, f32[1,6,32,256]{3,2,1,0:T(8,128)}, u32[]{:S(2)}) copy-start(f32[1,6,32,256]{3,2,1,0:T(8,128)} %param.26) | copy-start | bytes 589828
  16.3 12.0 %copy-start.5 = (f32[1,6,32,256]{3,2,1,0:T(8,128)S(1)}, f32[1,6,32,256]{3,2,1,0:T(8,128)}, u32[]{:S(2)}) copy-start(f32[1,6,32,256]{3,2,1,0:T(8,128)} %param.25) | copy-start | bytes 589828
  16.3 12.0 %copy-start.6 = (f32[1,256]{1,0:T(1,128)S(1)}, f32[1,256]{1,0:T(1,128)}, u32[]{:S(2)}) copy-start(f32[1,256]{1,0:T(1,128)} %refs_0_.9) | copy-start | bytes 3076
  16.3 12.0 %copy-start.7 = (f32[1,256]{1,0:T(1,128)S(1)}, f32[1,256]{1,0:T(1,128)}, u32[]{:S(2)}) copy-start(f32[1,256]{1,0:T(1,128)} %refs_1_.7) | copy-start | bytes 3076
  16.3 12.0 %copy-start.9 = (s32[1,256]{1,0:T(1,128)S(1)}, s32[1,256]{1,0:T(1,128)}, u32[]{:S(2)}) copy-start(s32[1,256]{1,0:T(1,128)} %refs_7_.3) | copy-start | bytes 3076
  31.6 8.2 %collective-permute-start.2 = (f32[2,32,256]{2,1,0:T(8,128)S(1)}, f32[2,32,256]{2,1,0:T(8,128)S(1)}, u32[]{:S(2)}, u32[]{:S(2)}) collective-permute-start(f32[2,32,256]{2,1,0:T(8,128)S(1)} %get-tuple-element.56), channel_id=1, source_target_pairs={{0,28},{4,0},{8,4},{12,8},{16,12},{20,16},{24,20},{28,24},{1,29},{... | collective-permute-start | bytes 196616 | tf_op jit(solution)/shard_map/ppermute | solution.py:25
  34.4 7.0 %collective-permute-start.1 = (f32[2,32,256]{2,1,0:T(8,128)S(1)}, f32[2,32,256]{2,1,0:T(8,128)S(1)}, u32[]{:S(2)}, u32[]{:S(2)}) collective-permute-start(f32[2,32,256]{2,1,0:T(8,128)S(1)} %get-tuple-element.55.refs_13_), channel_id=1, source_target_pairs={{0,4},{4,8},{8,12},{12,16},{16,20},{20,24},{24,28},{28,0},{1,5},{5... | collective-permute-start | bytes 196616 | tf_op jit(solution)/shard_map/ppermute | solution.py:25
  43.0 8.7 %collective-permute-start.4 = (f32[2,32,256]{2,1,0:T(8,128)S(1)}, f32[2,32,256]{2,1,0:T(8,128)S(1)}, u32[]{:S(2)}, u32[]{:S(2)}) collective-permute-start(f32[2,32,256]{2,1,0:T(8,128)S(1)} %get-tuple-element.62), channel_id=1, source_target_pairs={{0,28},{4,0},{8,4},{12,8},{16,12},{20,16},{24,20},{28,24},{1,29},{... | collective-permute-start | bytes 196616 | tf_op jit(solution)/shard_map/ppermute | solution.py:25
  46.3 7.0 %collective-permute-start.3 = (f32[2,32,256]{2,1,0:T(8,128)S(1)}, f32[2,32,256]{2,1,0:T(8,128)S(1)}, u32[]{:S(2)}, u32[]{:S(2)}) collective-permute-start(f32[2,32,256]{2,1,0:T(8,128)S(1)} %get-tuple-element.61.refs_13_), channel_id=1, source_target_pairs={{0,4},{4,8},{8,12},{12,16},{16,20},{20,24},{24,28},{28,0},{1,5},{5... | collective-permute-start | bytes 196616 | tf_op jit(solution)/shard_map/ppermute | solution.py:25
  55.3 10.2 %collective-permute-start.5 = (f32[2,32,256]{2,1,0:T(8,128)S(1)}, f32[2,32,256]{2,1,0:T(8,128)S(1)}, u32[]{:S(2)}, u32[]{:S(2)}) collective-permute-start(f32[2,32,256]{2,1,0:T(8,128)S(1)} %get-tuple-element.67), channel_id=1, source_target_pairs={{0,4},{4,8},{8,12},{12,16},{16,20},{20,24},{24,28},{28,0},{1,5},{5... | collective-permute-start | bytes 196616 | tf_op jit(solution)/shard_map/ppermute | solution.py:25
  55.3 10.2 %collective-permute-start.6 = (f32[2,32,256]{2,1,0:T(8,128)S(1)}, f32[2,32,256]{2,1,0:T(8,128)S(1)}, u32[]{:S(2)}, u32[]{:S(2)}) collective-permute-start(f32[2,32,256]{2,1,0:T(8,128)S(1)} %get-tuple-element.68), channel_id=1, source_target_pairs={{0,28},{4,0},{8,4},{12,8},{16,12},{20,16},{24,20},{28,24},{1,29},{... | collective-permute-start | bytes 196616 | tf_op jit(solution)/shard_map/ppermute | solution.py:25
  67.1 14.6 %all-to-all-start.1 = ((f32[8,16,128]{2,1,0:T(8,128)}), f32[8,16,128]{2,1,0:T(8,128)S(1)}, u32[]{:S(2)}, u32[]{:S(2)}) async-start(f32[8,16,128]{2,1,0:T(8,128)} %get-tuple-element.84), calls=%async_computation.1 | async-start | bytes 131072 | tf_op jit(solution)/shard_map/all_to_all | solution.py:545
  78.1 3.2 %collective-permute-start.9 = (f32[1,3072]{1,0:T(1,128)S(1)}, f32[1,3072]{1,0:T(1,128)S(1)}, u32[]{:S(2)}, u32[]{:S(2)}) collective-permute-start(f32[1,3072]{1,0:T(1,128)S(1)} %get-tuple-element.83.refs_0_), channel_id=1, source_target_pairs={{0,3},{1,2},{2,1},{3,0},{4,7},{5,6},{6,5},{7,4},{8,11},{9,10},{10,... | collective-permute-start | bytes 36872 | tf_op jit(solution)/shard_map/ppermute | solution.py:580
  78.1 3.7 %collective-permute-start.8 = (f32[1,3072]{1,0:T(1,128)S(1)}, f32[1,3072]{1,0:T(1,128)S(1)}, u32[]{:S(2)}, u32[]{:S(2)}) collective-permute-start(f32[1,3072]{1,0:T(1,128)S(1)} %get-tuple-element.83.refs_0_), channel_id=1, source_target_pairs={{0,2},{1,3},{2,0},{3,1},{4,6},{5,7},{6,4},{7,5},{8,10},{9,11},{10,... | collective-permute-start | bytes 36872 | tf_op jit(solution)/shard_map/ppermute | solution.py:580
  79.6 2.2 %collective-permute-start.7 = (f32[1,3072]{1,0:T(1,128)S(1)}, f32[1,3072]{1,0:T(1,128)S(1)}, u32[]{:S(2)}, u32[]{:S(2)}) collective-permute-start(f32[1,3072]{1,0:T(1,128)S(1)} %get-tuple-element.83.refs_0_), channel_id=1, source_target_pairs={{0,1},{1,0},{2,3},{3,2},{4,5},{5,4},{6,7},{7,6},{8,9},{9,8},{10,11... | collective-permute-start | bytes 36872 | tf_op jit(solution)/shard_map/ppermute | solution.py:580
  (19 other events, 57.6 us)
where the time goes:
time: 83.1 us; the launch traced here: 82.6 us
  Pallas kernels  39.3 us (47%)
  starting transfers between devices  25.3 us (30%)
  local copies, waits for them, and re-layouts  12.2 us (15%)
  waiting for transfers between devices  4.89 us (6%)
  between operations  0.92 us (1%)
    pallas_call x11, Pallas kernels, call(): pl.pallas_call(kernel, name=name, out_shape=[jax.ShapeDtypeStruct(*outs[k...  39.3 us
    ppermute x7, starting transfers between devices, shifted(): return lax.ppermute(value, axis, pairs)  12.8 us
    unnamed x62, local copies, waits for them, and re-layouts  12.1 us
    all_to_all x1, starting transfers between devices, per_device(): lax.all_to_all(send, 'region', split_axis=0, concat_axis=0, tiled=True)  7.28 us
    all_to_all x1, starting transfers between devices, per_device(): lax.all_to_all(current, 'region', split_axis=0, concat_axis=0, tiled=True)  3.35 us
    ppermute x7, waiting for transfers between devices, shifted(): return lax.ppermute(value, axis, pairs)  3.04 us
    ppermute x3, starting transfers between devices, per_device(): parts.append(lax.ppermute(squares, 'scen', pairs))  1.86 us
    ppermute x3, waiting for transfers between devices, per_device(): parts.append(lax.ppermute(squares, 'scen', pairs))  1.84 us
  transfers between devices with their start and end apart: 12, of which 4 were waited for; matrix products, arithmetic and copies ran while one was open for 0% of the time, Pallas kernels for 37%

commit v1 on v0

--- a/solution.py
+++ b/solution.py
@@ -11,6 +11,8 @@
 STEPS = 8
 DMIN = 2
 LANES = 128
+VMEM = 67043328
+ROOM = 1600 << 10
 OMEGA = 0.01884955592153876
 EPS = 1e-06
 F32 = jnp.float32
@@ -25,29 +27,71 @@
     return lax.ppermute(value, axis, pairs)
 
 
-def call(body, name, ins, outs, scratch=(), cost=(1e9, 4e6)):
+def swapped(value, axis, first):
+    count = lax.axis_size(axis)
+    pairs = []
+    for left in range(first, count, 2):
+        right = (left + 1) % count
+        pairs += [(left, right), (right, left)]
+    return lax.ppermute(value, axis, pairs)
+
+
+def call(body, name, ins, outs, scratch=(), hbm=None, hbm_outs=None, limit=20 << 20, cost=None):
     leaves, tree = jax.tree.flatten(ins)
-    out_names = list(outs)
+    far, far_outs = dict(hbm or {}), dict(hbm_outs or {})
+    names = [list(far), list(outs), list(far_outs)]
+    sizes = [len(leaves)] + [len(group) for group in names] + [len(far), len(far_outs)]
+    ends = [sum(sizes[:k]) for k in range(len(sizes) + 1)]
+    count = len(far) + len(far_outs)
 
     def kernel(*refs):
-        first, second = len(leaves), len(leaves) + len(out_names)
-        i = Space(**jax.tree.unflatten(tree, refs[:first]))
-        o = Space(**dict(zip(out_names, refs[first:second])))
-        body(i, o, *refs[second:])
-
+        near, sources, near_outs, targets, held, made = [
+            refs[ends[k] : ends[k + 1]] for k in range(len(sizes))
+        ]
+        rest = refs[ends[-1] :]
+        arriving, leaving, pending = {}, {}, []
+        if count:
+            sems, rest = rest[0], rest[1:]
+            for k, key in enumerate(far):
+                arriving[key] = pltpu.make_async_copy(sources[k], held[k], sems.at[k])
+                arriving[key].start()
+            for k, key in enumerate(far_outs):
+                leaving[key] = pltpu.make_async_copy(made[k], targets[k], sems.at[len(far) + k])
+        i = Space(**jax.tree.unflatten(tree, near), **dict(zip(far, held)))
+        o = Space(**dict(zip(outs, near_outs)), **dict(zip(far_outs, made)))
+
+        def flush(key):
+            pending.append(leaving.pop(key))
+            pending[-1].start()
+
+        i.ready = lambda *keys: [arriving.pop(key).wait() for key in keys]
+        o.flush = flush
+        body(i, o, *rest)
+        for key in list(leaving):
+            flush(key)
+        for copy in pending:
+            copy.wait()
+
+    buffers = [pltpu.VMEM(value.shape, value.dtype) for value in far.values()]
+    buffers += [pltpu.VMEM(*shape) for shape in far_outs.values()]
+    if count:
+        buffers.append(pltpu.SemaphoreType.DMA((count,)))
+    every = list(outs.values()) + list(far_outs.values())
+    near_spec, far_spec = (pl.BlockSpec(memory_space=space) for space in (pltpu.VMEM, pltpu.HBM))
+    flops, moved = cost or (1e9, 4e6)
     results = pl.pallas_call(
         kernel,
         name=name,
-        out_shape=[jax.ShapeDtypeStruct(*outs[key]) for key in out_names],
-        in_specs=[pl.BlockSpec(memory_space=pltpu.VMEM)] * len(leaves),
-        out_specs=[pl.BlockSpec(memory_space=pltpu.VMEM)] * len(out_names),
-        scratch_shapes=list(scratch),
-        compiler_params=pltpu.CompilerParams(vmem_limit_bytes=24 << 20),
+        out_shape=[jax.ShapeDtypeStruct(*shape) for shape in every],
+        in_specs=[near_spec] * len(leaves) + [far_spec] * len(far),
+        out_specs=[near_spec] * len(outs) + [far_spec] * len(far_outs),
+        scratch_shapes=buffers + list(scratch),
+        compiler_params=pltpu.CompilerParams(vmem_limit_bytes=limit),
         cost_estimate=pl.CostEstimate(
-            flops=int(cost[0]), bytes_accessed=int(cost[1]), transcendentals=0
+            flops=int(flops), bytes_accessed=int(moved), transcendentals=0
         ),
-    )(*leaves)
-    return Space(**dict(zip(out_names, results)))
+    )(*leaves, *far.values())
+    return Space(**dict(zip(names[1] + names[2], results)))
 
 
 def iota(shape, dim):
@@ -99,6 +143,7 @@
 def start_body(sizes, i, o):
     regions, cap, half, scen, group, maxd = sizes
     packed = 2 * cap == LANES
+    i.ready("slots", "par", "state")
     slots = i.slots[...]
     rows = iota((regions * 2 * cap, group), 0)
     if packed:
@@ -121,83 +166,53 @@
             o.send[region] = buffer[:, region * LANES : (region + 1) * LANES]
     else:
         o.send[...] = buffer
+    o.flush("send")
+    i.ready("hist", "delay")
     delays = i.delay[...]
     for step in range(2):
-        o.into[step] = pick(lambda t: i.hist[t + maxd], delays, step, maxd)
-
-
-def model_body(sizes, i, o, spots, base, acc):
-    nreg, nblk, lines, width, scen = sizes
+        o.into[step] = pick(lambda t: i.hist[0, t + maxd], delays, step, maxd)
+
+
+def sources(amp, phase):
+    instant = iota((STEPS, amp.shape[1]), 0).astype(F32)
+    return amp * jnp.cos(OMEGA * instant + phase)
+
+
+def rows_body(sizes, i, o, place, source_rows):
+    nreg, nblk, lines, regions, cap, scen = sizes
     blk = LANES
+    width = regions * cap
     points = 2 * lines + width
     whole = points + blk
-    spots[...] = jnp.full((1, whole), -1, jnp.int32)
-    spots[:, 0:lines] = i.end_a[...]
-    spots[:, lines : 2 * lines] = i.end_b[...]
-    spots[:, 2 * lines : points] = i.conv[...]
+    i.ready("end_a", "end_b", "conv", "fault_node")
+    o.row[...] = jnp.full((1, whole), -1, jnp.int32)
+    o.row[:, 0:lines] = i.end_a[...]
+    o.row[:, lines : 2 * lines] = i.end_b[...]
+    for group in range(regions):
+        start = 2 * lines + group * cap
+        o.row[:, start : start + cap] = i.conv[0, group : group + 1, :]
     region = lax.axis_index("region")
     fault = i.fault_node[...] - region * nreg
     fault = jnp.where((fault >= 0) & (fault < nreg), fault, -1)
-    spots[:, points : points + scen] = fault
-    row = spots[...]
-    row_blk, row_in = row >> 7, row & 127
+    o.row[:, points : points + scen] = fault
+    row = o.row[...]
     column = jnp.transpose(jnp.broadcast_to(row.astype(F32), (blk, whole))).astype(jnp.int32)
-    column_blk = column >> 7
-    o.spots[...] = column[:points]
-    o.fault_blk[...] = column_blk[points : points + scen]
-    z = i.inv[...].reshape(nreg, blk)
-    z_high, z_low = split2(z)
+    o.column[...] = column
+    lane = iota((whole, blk), 1)
+    for k in range(nblk):
+        place[:, k * blk : (k + 1) * blk] = onehot(o.column[...] == lane + k * blk)
+    i.ready("inv")
+    z_high, z_low = split2(i.inv[...].reshape(nreg, blk))
     o.zcat[:, 0:blk] = z_high
     o.zcat[:, blk:] = z_low
-    acc[...] = jnp.zeros_like(acc)
-    lane = iota((whole, blk), 1)
-    span = 2 * blk
-
-    def gather(step, carry):
-        start = pl.multiple_of(step * span, span)
-        mine = jnp.concatenate(
-            [onehot(column == lane + start), onehot(column == lane + (start + blk))], axis=1
-        )
-        acc[...] += dot(mine, o.zcat[pl.ds(start, span), :])
-        return carry
-
-    lax.fori_loop(0, nblk // 2, gather, 0)
-    inside = onehot(iota((blk, points), 0) == row_in[:, :points])
-    row_blk_p = row_blk[:, :points]
-
-    def between(step, carry):
-        start = pl.multiple_of(step * blk, blk)
-        rows = acc[pl.ds(start, blk), :].astype(BF16)
-        mine = o.spots[pl.ds(start, blk), :][:, 0:1] >> 7
-        same = mine == row_blk_p
-        both = dot(jnp.concatenate([rows[:, :blk], rows[:, blk:]], axis=0), inside)
-        o.m_high[pl.ds(start, blk), :] = jnp.where(same, both[:blk], 0.0).astype(BF16)
-        o.m_low[pl.ds(start, blk), :] = jnp.where(same, both[blk:], 0.0).astype(BF16)
-        return carry
-
-    lax.fori_loop(0, points // blk, between, 0)
-    fault_rows = acc[points : points + scen, :]
-    fault_z = fault_rows[:, :blk] + fault_rows[:, blk:]
-    o.fault_z[...] = fault_z
-    fault_blk = column_blk[points : points + scen]
-    both = dot(
-        jnp.concatenate([fault_rows[:, :blk], fault_rows[:, blk:]], axis=0).astype(BF16), inside
-    )
-    o.fault_p[...] = jnp.where(
-        fault_blk[:, 0:1] == row_blk_p, both[:scen] + both[scen:], 0.0
-    )
-    instant = iota((STEPS, nreg), 0).astype(F32)
-    source = i.amp[...] * jnp.cos(OMEGA * instant + i.phase[...])
-    base[...] = jnp.concatenate(
-        [source[:, k * blk : (k + 1) * blk] for k in range(nblk)], axis=0
-    )
+    o.flush("zcat")
+    o.rows[...] = dot(place[...], o.zcat[...]).astype(BF16)
+    i.ready("amp", "phase")
+    source = sources(i.amp[...], i.phase[...])
     for k in range(nblk):
-        mine = o.zcat[k * blk : (k + 1) * blk, :]
-        o.base[:, k * blk : (k + 1) * blk] = product3(
-            base[k * STEPS : (k + 1) * STEPS, :], mine[:, :blk], mine[:, blk:]
-        )
-    rows = acc[...].astype(BF16)
-    spread = product3(base[...], rows[:, :blk], rows[:, blk:], NT)
+        source_rows[k * STEPS : (k + 1) * STEPS, :] = source[:, k * blk : (k + 1) * blk]
+    spread = product3(source_rows[...], o.rows[:, :blk], o.rows[:, blk:], NT)
+    row_blk = row >> 7
     at_points = jnp.zeros((STEPS, whole), F32)
     for k in range(nblk):
         at_points = at_points + jnp.where(row_blk == k, spread[k * STEPS : (k + 1) * STEPS], 0.0)
@@ -206,17 +221,39 @@
         [at_points[:, points:], jnp.zeros((blk - STEPS, blk), F32)], axis=0
     )
     o.fault_base[...] = jnp.transpose(tail)[:scen]
+    fault_rows = o.rows[points : points + scen, :].astype(F32)
+    fault_z = fault_rows[:, :blk] + fault_rows[:, blk:]
+    o.fault_z[...] = fault_z
     self_imp = jnp.sum(
         jnp.where(iota((scen, blk), 1) == (column[points : points + scen] & 127), fault_z, 0.0),
         axis=1,
         keepdims=True,
     )
+    i.ready("fault_cond", "fault_step")
     cond = as_column(i.fault_cond[...], scen)
     closes = as_column(i.fault_step[...].astype(F32), scen)
     ratio = cond / (1.0 + cond * self_imp)
     o.fault_ratio[...] = jnp.where(
         closes <= iota((scen, blk), 1).astype(F32), jnp.broadcast_to(ratio, (scen, blk)), 0.0
     )
+
+
+def between_body(sizes, i, o):
+    points, scen = sizes
+    blk = LANES
+    row = i.row[:, :points]
+    row_blk = row >> 7
+    inside = onehot(iota((blk, points), 0) == (row & 127))
+    for k in range(points // blk):
+        here = slice(k * blk, (k + 1) * blk)
+        same = (i.column[here, 0:1] >> 7) == row_blk
+        both = dot(jnp.concatenate([i.rows[here, :blk], i.rows[here, blk:]], axis=0), inside)
+        o.m_high[here, :] = jnp.where(same, both[:blk], 0.0).astype(BF16)
+        o.m_low[here, :] = jnp.where(same, both[blk:], 0.0).astype(BF16)
+    here = slice(points, points + scen)
+    both = dot(jnp.concatenate([i.rows[here, :blk], i.rows[here, blk:]], axis=0), inside)
+    same = (i.column[here, 0:1] >> 7) == row_blk
+    o.fault_p[...] = jnp.where(same, both[:scen] + both[scen:], 0.0)
 
 
 def advance_body(sizes, pair, i, o):
@@ -227,18 +264,23 @@
     twice = 2.0 * i.admit[...]
     last = STEPS - 1
 
+    even = lax.rem(lax.axis_index("region"), 2) == 0
     fresh = {}
     if pair:
+        far_in = [jnp.where(even, i.swap_b[j], i.swap_a[j]) for j in range(2)]
         for j in range(2):
-            fresh[t0 - 2 + j] = scale * (twice * i.far_volts[j] - i.into_prev[j])
+            far_volts = jnp.where(even, i.swap_a[j], i.swap_b[j])
+            fresh[t0 - 2 + j] = scale * (twice * far_volts - i.into_prev[j])
             if hasattr(o, "back"):
                 o.back[j] = fresh[t0 - 2 + j]
+    else:
+        far_in = [i.far_in[j] for j in range(2)]
 
     def back(t):
         if t in fresh:
             return fresh[t]
         if t < 0:
-            return i.hist_b[t + maxd]
+            return i.hist_b[0, t + maxd]
         return i.backs[t // 2][t % 2]
 
     made = {}
@@ -247,10 +289,10 @@
         if t in made:
             return made[t]
         if t < 0:
-            return i.hist_a[t + maxd]
+            return i.hist_a[0, t + maxd]
         return i.made[t // 2][t % 2]
 
-    live = i.conv[...] >= 0
+    live = i.row[:, 2 * lines : 2 * lines + width] >= 0
     if packed:
         low = iota((1, LANES), 1) < cap
         params = []
@@ -283,23 +325,32 @@
         current = drive(second)
 
     fault_p = i.fault_p[...]
+    ends = 2 * lines
+    sides = []
+    arrivals = [pick(back, delays, t0 + j, maxd) for j in range(2)]
+    waves = [jnp.concatenate([arrivals[j], far_in[j]], axis=1) for j in range(2)]
+    pairs = split2(jnp.concatenate(waves, axis=0))
+    for part in range(2):
+        o.x[part * 2 * scen : (part + 1) * 2 * scen, :ends] = pairs[part]
+    both = dot(jnp.concatenate(pairs, axis=0), i.m_high[:ends, :])
+    of_lines = both[: 2 * scen] + both[2 * scen :] + dot(pairs[0], i.m_low[:ends, :])
     for j in range(2):
         t = t0 + j
-        into = pick(back, delays, t, maxd)
-        x = jnp.concatenate([into, i.far_in[j], current], axis=1)
-        high, low_part = split2(x)
-        o.x[j * scen : (j + 1) * scen, :] = high
-        o.x[(2 + j) * scen : (3 + j) * scen, :] = low_part
-        both = dot(jnp.concatenate([high, low_part], axis=0), i.m_high[...])
-        volts = both[:scen] + both[scen:] + dot(high, i.m_low[...])
-        volts = volts + i.base_p[t : t + 1, :]
+        into = arrivals[j]
+        x = jnp.concatenate([waves[j], current], axis=1)
+        high, low_part = split2(current)
+        o.x[j * scen : (j + 1) * scen, ends:] = high
+        o.x[(2 + j) * scen : (3 + j) * scen, ends:] = low_part
+        both = dot(jnp.concatenate([high, low_part], axis=0), i.m_high[ends:, :])
+        volts = both[:scen] + both[scen:] + dot(high, i.m_low[ends:, :])
+        volts = volts + of_lines[j * scen : (j + 1) * scen] + i.base_p[t : t + 1, :]
         at_fault = i.fault_base[:, t : t + 1] + jnp.sum(x * fault_p, axis=1, keepdims=True)
         coef = i.fault_ratio[:, t : t + 1] * at_fault
         o.coef[j * scen : (j + 1) * scen, :] = jnp.broadcast_to(coef, (scen, LANES))
         volts = volts - fault_p * coef
         if t <= last - DMIN:
             made[t] = scale * (twice * volts[:, :lines] - into)
-            o.ends[j] = volts[:, lines : 2 * lines]
+            sides.append(volts[:, lines : 2 * lines])
             if hasattr(o, "out"):
                 o.out[j] = made[t]
         node = volts[:, 2 * lines :]
@@ -308,7 +359,10 @@
         current = drive(second)
     if hasattr(o, "into"):
         for j in range(2):
-            o.into[j] = pick(out, delays, t0 + 2 + j, maxd)
+            onward = pick(out, delays, t0 + 2 + j, maxd)
+            o.into[j] = onward
+            o.swap_a[j] = jnp.where(even, onward, sides[j])
+            o.swap_b[j] = jnp.where(even, sides[j], onward)
     if hasattr(o, "state"):
         o.state[0] = first
         o.state[1] = second
@@ -327,34 +381,36 @@
     nblk, points, scen = sizes
     blk = LANES
     t0 = 2 * pair
-    spots = i.spots
     fault_z = i.fault_z[...]
-    fault_blk = i.fault_blk[...]
+    fault_blk = i.column[points : points + scen, :] >> 7
     x = i.x[...]
+    coef = i.coef[...]
     lane = iota((points, blk), 1)
-    coef = i.coef[...]
-
-    def step(index, carry):
-        start = pl.multiple_of(index * 2 * blk, 2 * blk)
-        where = spots[...]
+    if pair:
+        all_base = i.base
+    else:
+        all_base = o.base
+        source = sources(i.amp[...], i.phase[...])
+        for k in range(nblk):
+            here = slice(k * blk, (k + 1) * blk)
+            z = i.zcat[here, :]
+            o.base[:, here] = product3(source[:, here], z[:, :blk], z[:, blk:])
+    for k in range(0, nblk, 2):
         mine = jnp.concatenate(
-            [onehot(where == lane + start), onehot(where == lane + (start + blk))], axis=1
+            [onehot(i.column[:points, :] == lane + (k + j) * blk) for j in range(2)], axis=1
         )
         both = dot(x, mine)
         inject = both[: 2 * scen] + both[2 * scen :]
         for j in range(2):
-            here = pl.ds(pl.multiple_of(start + j * blk, blk), blk)
+            here = slice((k + j) * blk, (k + j + 1) * blk)
             z = i.zcat[here, :]
             volts = product3(inject[:, j * blk : (j + 1) * blk], z[:, :blk], z[:, blk:])
-            base = i.base[:, here]
-            volts = volts + jnp.concatenate(
-                [
-                    jnp.broadcast_to(base[t0 + m : t0 + m + 1, :], (scen, blk))
-                    for m in range(2)
-                ],
-                axis=0,
-            )
-            column = jnp.where(fault_blk == 2 * index + j, fault_z, 0.0)
+            base = [
+                jnp.broadcast_to(all_base[t0 + m : t0 + m + 1, here], (scen, blk))
+                for m in range(2)
+            ]
+            column = jnp.where(fault_blk == k + j, fault_z, 0.0)
+            volts = volts + jnp.concatenate(base, axis=0)
             volts = volts - jnp.concatenate([column, column], axis=0) * coef
             total = jnp.sum(volts * volts, axis=0, keepdims=True)
             if hasattr(i, "squares"):
@@ -362,9 +418,6 @@
             o.squares[:, here] = total
             if hasattr(o, "volts"):
                 o.volts[:, here] = volts[scen:]
-        return carry
-
-    lax.fori_loop(0, nblk // 2, step, 0)
 
 
 def finish_body(sizes, i, o):
@@ -425,15 +478,16 @@
     count = lax.axis_size("scen")
     packed = 2 * cap == LANES
     half = scen + 8
-    hist_a, hist_b = hist_ua[0], hist_ub[0]
-    conv = send_node.reshape(1, width)
 
     send_shape = (regions, half, LANES) if packed else (half, regions * 2 * cap)
     head = call(
         functools.partial(start_body, (regions, cap, half, scen, group, maxd)),
         "start",
-        dict(slots=recv_slot, par=conv_par, state=conv_state, hist=hist_a, delay=line_delay),
-        dict(send=(send_shape, F32), into=((2, scen, lines), F32)),
+        {},
+        {},
+        hbm_outs=dict(send=(send_shape, F32), into=((2, scen, lines), F32)),
+        limit=VMEM,
+        hbm=dict(slots=recv_slot, par=conv_par, state=conv_state, hist=hist_ua, delay=line_delay),
     )
     send = head.send
     if packed:
@@ -445,44 +499,50 @@
     into = head.into
     far_in = shifted(into, "region", 1)
 
+    whole = points + blk
     model = call(
-        functools.partial(model_body, (nreg, nblk, lines, width, scen)),
-        "model",
+        functools.partial(rows_body, (nreg, nblk, lines, regions, cap, scen)),
+        "rows",
+        {},
         dict(
+            row=((1, whole), jnp.int32),
+            column=((whole, blk), jnp.int32),
+            rows=((whole, 2 * blk), BF16),
+            base_p=((STEPS, points), F32),
+            fault_z=((scen, blk), F32),
+            fault_base=((scen, blk), F32),
+            fault_ratio=((scen, blk), F32),
+        ),
+        hbm_outs=dict(zcat=((nreg, 2 * blk), BF16)),
+        hbm=dict(
+            end_a=line_a,
+            end_b=line_b,
+            conv=send_node,
+            fault_node=fault_node.reshape(1, scen),
             inv=inv_blocks,
             amp=src_amp.reshape(1, nreg),
             phase=src_phase.reshape(1, nreg),
-            end_a=line_a,
-            end_b=line_b,
-            conv=conv,
-            fault_node=fault_node.reshape(1, scen),
             fault_step=fault_step.reshape(1, scen),
             fault_cond=fault_cond.reshape(1, scen),
         ),
+        scratch=(pltpu.VMEM((whole, nreg), BF16), pltpu.VMEM((STEPS * nblk, blk), F32)),
+        limit=VMEM - ROOM,
+        cost=(4e9, 2e7),
+    )
+    matrix = call(
+        functools.partial(between_body, (points, scen)),
+        "between",
+        dict(row=model.row, column=model.column, rows=model.rows, recv=recv),
         dict(
-            spots=((points, blk), jnp.int32),
-            zcat=((nreg, 2 * blk), BF16),
             m_high=((points, points), BF16),
             m_low=((points, points), BF16),
-            base=((STEPS, nreg), F32),
-            base_p=((STEPS, points), F32),
             fault_p=((scen, points), F32),
-            fault_z=((scen, blk), F32),
-            fault_blk=((scen, blk), jnp.int32),
-            fault_base=((scen, blk), F32),
-            fault_ratio=((scen, blk), F32),
         ),
-        scratch=(
-            pltpu.VMEM((1, points + blk), jnp.int32),
-            pltpu.VMEM((STEPS * nblk, blk), F32),
-            pltpu.VMEM((points + blk, 2 * blk), F32),
-        ),
-        cost=(4e9, 2e7),
     )
 
     wave = ((2, scen, lines), F32)
     mades, backs, carry = {}, {}, {}
-    squares = far_volts = sent = None
+    squares = swap_a = swap_b = sent = base = None
     for pair in range(STEPS // 2):
         t0 = 2 * pair
         final = t0 + 2 >= STEPS
@@ -490,31 +550,33 @@
             delay=line_delay,
             atten=line_atten,
             admit=line_yc,
-            conv=conv,
+            row=model.row,
             recv=recv,
-            far_in=far_in,
-            m_high=model.m_high,
-            m_low=model.m_low,
+            m_high=matrix.m_high,
+            m_low=matrix.m_low,
             base_p=model.base_p,
-            fault_p=model.fault_p,
+            fault_p=matrix.fault_p,
             fault_base=model.fault_base,
             fault_ratio=model.fault_ratio,
             **carry,
         )
         if t0 - maxd < 0:
-            ins.update(hist_b=hist_b)
+            ins.update(hist_b=hist_ub)
         if pair:
-            ins.update(far_volts=far_volts, into_prev=sent)
+            ins.update(swap_a=swap_a, swap_b=swap_b, into_prev=sent)
+        else:
+            ins.update(far_in=far_in)
         first = max(0, pair - 3)
         ins.update(backs={k: v for k, v in backs.items() if k >= first})
         if not final:
             ins.update(made={k: v for k, v in mades.items() if k >= pair - 2})
             if t0 + 2 - maxd < 0:
-                ins.update(hist_a=hist_a)
+                ins.update(hist_a=hist_ua)
         outs = dict(x=((4 * scen, points), BF16), coef=((2 * scen, LANES), F32))
         if not final:
             outs.update(
-                ends=wave,
+                swap_a=wave,
+                swap_b=wave,
                 out=wave,
                 into=wave,
                 state=((2, scen, width), F32),
@@ -533,8 +595,8 @@
         )
         if not final:
             sent, into = into, made.into
-            far_in = shifted(into, "region", 1)
-            far_volts = shifted(made.ends, "region", -1)
+            swap_a = swapped(made.swap_a, "region", 0)
+            swap_b = swapped(made.swap_b, "region", 1)
             mades[pair] = made.out
             if pair:
                 backs[pair - 1] = made.back
@@ -542,29 +604,27 @@
         else:
             current = made.current
             if packed:
-                returned = lax.all_to_all(
-                    current, "region", split_axis=0, concat_axis=0, tiled=True
-                )
+                returned = lax.all_to_all(current, "region", split_axis=0, concat_axis=0, tiled=True)
             else:
                 current = current.reshape(scen, regions, cap).transpose(1, 0, 2)
-                returned = lax.all_to_all(
-                    current, "region", split_axis=0, concat_axis=0, tiled=True
-                )
+                returned = lax.all_to_all(current, "region", split_axis=0, concat_axis=0, tiled=True)
                 returned = returned.transpose(1, 0, 2).reshape(scen, width)
         ins = dict(
             x=made.x,
             coef=made.coef,
-            spots=model.spots,
+            column=model.column,
             zcat=model.zcat,
-            base=model.base,
             fault_z=model.fault_z,
-            fault_blk=model.fault_blk,
         )
         if pair:
-            ins.update(squares=squares)
+            ins.update(squares=squares, base=base)
+        else:
+            ins.update(amp=src_amp.reshape(1, nreg), phase=src_phase.reshape(1, nreg))
         outs = dict(squares=((1, nreg), F32))
         if final:
             outs.update(volts=((scen, nreg), F32))
+        if not pair:
+            outs.update(base=((STEPS, nreg), F32))
         full = call(
             functools.partial(full_body, (nblk, points, scen), pair),
             "full",
@@ -573,6 +633,8 @@
             cost=(4e9, 1e7),
         )
         squares = full.squares
+        if not pair:
+            base = full.base
 
     parts = [squares]
     for offset in range(1, count):

time: 83.1 us -> 67.1 us (0.81)
  Pallas kernels: 39.3 us -> 31.2 us
  local copies, waits for them, and re-layouts: 12.2 us -> 4.38 us
  waiting for transfers between devices: 4.89 us -> 2.8 us
  starting transfers between devices: 25.3 us -> 27.3 us
    ppermute x0 -> x6, starting transfers between devices: none -> 11.6 us  [swapped(): return lax.ppermute(value, axis, pairs)]
    ppermute x7 -> x1, starting transfers between devices: 12.8 us -> 2.02 us  [shifted(): return lax.ppermute(value, axis, pairs)]
    pallas_call x11 -> x12, Pallas kernels: 39.3 us -> 31.2 us  [call(): pl.pallas_call(kernel, name=name, out_shape=[jax.ShapeDtypeStruct(*shape)...]
    unnamed x62 -> x40, local copies, waits for them, and re-layouts: 12.1 us -> 4.38 us
    ppermute x7 -> x1, waiting for transfers between devices: 3.04 us -> 0.01 us  [shifted(): return lax.ppermute(value, axis, pairs)]
    all_to_all x1, starting transfers between devices: 3.35 us -> 4.53 us  [per_device(): lax.all_to_all(current, 'region', split_axis=0, concat_axis=0, tiled=True)]
    ppermute x0 -> x6, waiting for transfers between devices: none -> 0.95 us  [swapped(): return lax.ppermute(value, axis, pairs)]
  transfers between devices with their start and end apart: 12 -> 12, of which waited for: 4 -> 4; matrix products, arithmetic and copies ran while one was open for 0% -> 0% of each run, Pallas kernels for 37% -> 34%
where the time goes in v1:
time: 67.1 us; the launch traced here: 66.6 us
  Pallas kernels  31.2 us (46%)
  starting transfers between devices  27.3 us (41%)
  local copies, waits for them, and re-layouts  4.38 us (7%)
  waiting for transfers between devices  2.8 us (4%)
  between operations  0.92 us (1%)
    pallas_call x12, Pallas kernels, call(): pl.pallas_call(kernel, name=name, out_shape=[jax.ShapeDtypeStruct(*shape)...  31.2 us
    ppermute x6, starting transfers between devices, swapped(): return lax.ppermute(value, axis, pairs)  11.6 us
    all_to_all x1, starting transfers between devices, per_device(): lax.all_to_all(send, 'region', split_axis=0, concat_axis=0, tiled=True)  7.29 us
    all_to_all x1, starting transfers between devices, per_device(): lax.all_to_all(current, 'region', split_axis=0, concat_axis=0, tiled=True)  4.53 us
    unnamed x40, local copies, waits for them, and re-layouts  4.38 us
    ppermute x1, starting transfers between devices, shifted(): return lax.ppermute(value, axis, pairs)  2.02 us
    ppermute x3, starting transfers between devices, per_device(): parts.append(lax.ppermute(squares, 'scen', pairs))  1.86 us
    ppermute x3, waiting for transfers between devices, per_device(): parts.append(lax.ppermute(squares, 'scen', pairs))  1.84 us
  transfers between devices with their start and end apart: 12, of which 4 were waited for; matrix products, arithmetic and copies ran while one was open for 0% of the time, Pallas kernels for 34%

profile of v1, /device:TPU:0, one launch (start us, length us, event | category | flops | bytes accessed | tf_op | source)
XLA Modules:
  0.0 66.6 jit_solution(18411328831625145969)
XLA Ops:
  0.6 1.9 %start.1 = (f32[8,40,128]{2,1,0:T(8,128)}, f32[2,32,256]{2,1,0:T(8,128)}) custom-call(s32[1,128]{1,0:T(1,128)} %refs_5_.3, f32[6,128]{1,0:T(8,128)} %refs_1_.7, f32[2,32,128]{2,1,0:T(8,128)} %refs_2_.3, f32[1,6,32,256]{3,2,1,0:T(8,128)} %refs_8_.3, s32[1,256]{1,0:T(1,128)} %refs_6_.1), custom_call_target="tpu_custom_call" | custom-call | flops 1000000000 | bytes 4000000 | tf_op jit(solution)/shard_map/start/pallas_call | solution.py:82
  2.5 7.3 %all-to-all-start = ((f32[8,40,128]{2,1,0:T(8,128)}), f32[8,40,128]{2,1,0:T(8,128)S(1)}, u32[]{:S(2)}, u32[]{:S(2)}) async-start(f32[8,40,128]{2,1,0:T(8,128)} %get-tuple-element.53), calls=%async_computation | async-start | bytes 327680 | tf_op jit(solution)/shard_map/all_to_all | solution.py:494
  9.8 2.0 %collective-permute-start = (f32[2,32,256]{2,1,0:T(8,128)}, f32[2,32,256]{2,1,0:T(8,128)S(1)}, u32[]{:S(2)}, u32[]{:S(2)}) collective-permute-start(f32[2,32,256]{2,1,0:T(8,128)} %get-tuple-element.50.refs_10_), channel_id=1, source_target_pairs={{0,4},{4,8},{8,12},{12,16},{16,20},{20,24},{24,28},{28,0},{1,5},{5... | collective-permute-start | bytes 196616 | tf_op jit(solution)/shard_map/ppermute | solution.py:27
  11.9 7.2 %rows.1 = (s32[1,1152]{1,0:T(1,128)}, s32[1152,128]{1,0:T(8,128)}, bf16[1152,256]{1,0:T(8,128)(2,1)}, f32[8,1024]{1,0:T(8,128)}, f32[32,128]{1,0:T(8,128)}, /*in...) custom-call(s32[1,256]{1,0:T(1,128)} %refs_0_.6, s32[1,256]{1,0:T(1,128)} %refs_1_.6, ...), custom_call_target="tpu_custom_call" | custom-call | flops 4000000000 | bytes 20000000 | tf_op jit(solution)/shard_map/rows/pallas_call | solution.py:82
  20.0 1.1 %copy-done.14 = s32[1152,128]{1,0:T(8,128)S(1)} copy-done((s32[1152,128]{1,0:T(8,128)S(1)}, s32[1152,128]{1,0:T(8,128)}, u32[]{:S(2)}) %copy-start.14) | copy-done | bytes 589848
  21.0 1.1 %copy-done.16 = bf16[1152,256]{1,0:T(8,128)(2,1)S(1)} copy-done((bf16[1152,256]{1,0:T(8,128)(2,1)S(1)}, bf16[1152,256]{1,0:T(8,128)(2,1)}, u32[]{:S(2)}) %copy-start.16) | copy-done | bytes 589848
  22.1 1.3 %between.1 = (bf16[1024,1024]{1,0:T(8,128)(2,1)S(1)}, bf16[1024,1024]{1,0:T(8,128)(2,1)S(1)}, f32[32,1024]{1,0:T(8,128)S(1)}) custom-call(s32[1152,128]{1,0:T(8,128)S(1)} %copy-done.14, f32[8,40,128]{2,1,0:T(8,128)S(1)} %all-to-all-done.refs_1_.refs_12_.refs_14_.refs_15_.refs_13_, s32[1,1152]{1,0:T(1,128)S(1)} %copy-done.5, bf16[1152,256]{1,0:T(8,128)(2,1)S(1)} %copy-done.16), custom_call_target="tpu_custom_call" | custom-call | flops 1000000000 | bytes 4000000 | tf_op jit(solution)/shard_map/between/pallas_call | solution.py:82
  23.5 1.3 %advance.4 = (bf16[128,1024]{1,0:T(8,128)(2,1)S(1)}, f32[64,128]{1,0:T(8,128)S(1)}, f32[2,32,256]{2,1,0:T(8,128)S(1)}, f32[2,32,256]{2,1,0:T(8,128)S(1)}, f32[2,...) custom-call(f32[1,256]{1,0:T(1,128)S(1)} %copy-done.8, ...), custom_call_target="tpu_custom_call" | custom-call | flops 1000000000 | bytes 4000000 | tf_op jit(solution)/shard_map/advance/pallas_call | solution.py:82
  24.8 1.5 %collective-permute-start.1 = (f32[2,32,256]{2,1,0:T(8,128)S(1)}, f32[2,32,256]{2,1,0:T(8,128)S(1)}, u32[]{:S(2)}, u32[]{:S(2)}) collective-permute-start(f32[2,32,256]{2,1,0:T(8,128)S(1)} %get-tuple-element.68), channel_id=1, source_target_pairs={{0,4},{4,0},{8,12},{12,8},{16,20},{20,16},{24,28},{28,24},{1,5},{5... | collective-permute-start | bytes 196616 | tf_op jit(solution)/shard_map/ppermute | solution.py:36
  26.4 3.3 %collective-permute-start.2 = (f32[2,32,256]{2,1,0:T(8,128)S(1)}, f32[2,32,256]{2,1,0:T(8,128)S(1)}, u32[]{:S(2)}, u32[]{:S(2)}) collective-permute-start(f32[2,32,256]{2,1,0:T(8,128)S(1)} %get-tuple-element.69), channel_id=1, source_target_pairs={{4,8},{8,4},{12,16},{16,12},{20,24},{24,20},{28,0},{0,28},{5,9},{9... | collective-permute-start | bytes 196616 | tf_op jit(solution)/shard_map/ppermute | solution.py:36
  29.7 3.6 %full.4 = (f32[1,3072]{1,0:T(1,128)S(1)}, f32[8,3072]{1,0:T(8,128)S(1)}) custom-call(f32[1,3072]{1,0:T(1,128)S(1)} %bitcast.7, f32[64,128]{1,0:T(8,128)S(1)} %get-tuple-element.60.refs_1_, s32[1152,128]{1,0:T(8,128)S(1)} %copy-done.15, f32[32,128]{1,0:T(8,128)S(1)} %copy-done.19, f32[1,3072]{1,0:T(1,128)S(1)} %bitcast.9, ...), custom_call_target="tpu_custom_call" | custom-call | flops 4000000000 | bytes 10000000 | tf_op jit(solution)/shard_map/full/pallas_call | solution.py:82
  33.3 1.3 %advance.5 = (bf16[128,1024]{1,0:T(8,128)(2,1)S(1)}, f32[64,128]{1,0:T(8,128)S(1)}, f32[2,32,256]{2,1,0:T(8,128)S(1)}, f32[2,32,256]{2,1,0:T(8,128)S(1)}, f32[2,...) custom-call(f32[1,256]{1,0:T(1,128)S(1)} %copy-done.8, ...), custom_call_target="tpu_custom_call" | custom-call | flops 1000000000 | bytes 4000000 | tf_op jit(solution)/shard_map/advance/pallas_call | solution.py:82
  34.8 3.3 %collective-permute-start.4 = (f32[2,32,256]{2,1,0:T(8,128)S(1)}, f32[2,32,256]{2,1,0:T(8,128)S(1)}, u32[]{:S(2)}, u32[]{:S(2)}) collective-permute-start(f32[2,32,256]{2,1,0:T(8,128)S(1)} %get-tuple-element.76), channel_id=1, source_target_pairs={{4,8},{8,4},{12,16},{16,12},{20,24},{24,20},{28,0},{0,28},{5,9},{9... | collective-permute-start | bytes 196616 | tf_op jit(solution)/shard_map/ppermute | solution.py:36
  38.1 3.3 %full.5.refs_4_ = f32[1,3072]{1,0:T(1,128)S(1)} custom-call(f32[8,3072]{1,0:T(8,128)S(1)} %get-tuple-element.64.refs_0_, f32[64,128]{1,0:T(8,128)S(1)} %get-tuple-element.85.refs_1_, s32[1152,128]{1,0:T(8,128)S(1)} %copy-done.15, f32[32,128]{1,0:T(8,128)S(1)} %copy-done.19, f32[1,3072]{1,0:T(1,128)S(1)} %get-tuple-element.86.refs_4_, ...), custom_call_target="tpu_custom_call" | custom-call | flops 4000000000 | bytes 10000000 | tf_op jit(solution)/shard_map/full/pallas_call | solution.py:82
  41.8 1.9 %advance.6 = (bf16[128,1024]{1,0:T(8,128)(2,1)S(1)}, f32[64,128]{1,0:T(8,128)S(1)}, f32[2,32,256]{2,1,0:T(8,128)S(1)}, f32[2,32,256]{2,1,0:T(8,128)S(1)}, f32[2,...) custom-call(f32[1,256]{1,0:T(1,128)S(1)} %copy-done.8, ...), custom_call_target="tpu_custom_call" | custom-call | flops 1000000000 | bytes 4000000 | tf_op jit(solution)/shard_map/advance/pallas_call | solution.py:82
  43.8 3.3 %collective-permute-start.6 = (f32[2,32,256]{2,1,0:T(8,128)S(1)}, f32[2,32,256]{2,1,0:T(8,128)S(1)}, u32[]{:S(2)}, u32[]{:S(2)}) collective-permute-start(f32[2,32,256]{2,1,0:T(8,128)S(1)} %get-tuple-element.82), channel_id=1, source_target_pairs={{4,8},{8,4},{12,16},{16,12},{20,24},{24,20},{28,0},{0,28},{5,9},{9... | collective-permute-start | bytes 196616 | tf_op jit(solution)/shard_map/ppermute | solution.py:36
  47.1 3.1 %full.6.refs_4_ = f32[1,3072]{1,0:T(1,128)S(1)} custom-call(f32[8,3072]{1,0:T(8,128)S(1)} %get-tuple-element.64.refs_0_, f32[64,128]{1,0:T(8,128)S(1)} %get-tuple-element.84.refs_1_, s32[1152,128]{1,0:T(8,128)S(1)} %copy-done.15, f32[32,128]{1,0:T(8,128)S(1)} %copy-done.19, f32[1,3072]{1,0:T(1,128)S(1)} %full.5.refs_4_, ...), custom_call_target="tpu_custom_call" | custom-call | flops 4000000000 | bytes 10000000 | tf_op jit(solution)/shard_map/full/pallas_call | solution.py:82
  50.8 1.5 %advance.7 = (bf16[128,1024]{1,0:T(8,128)(2,1)S(1)}, f32[64,128]{1,0:T(8,128)S(1)}, f32[8,16,128]{2,1,0:T(8,128)}) custom-call(f32[1,256]{1,0:T(1,128)S(1)} %copy-done.8, f32[1,256]{1,0:T(1,128)S(1)} %copy-done.9, f32[2,32,256]{2,1,0:T(8,128)S(1)} %get-tuple-element.70.refs_2_, f32[2,32,256]{2,1,0:T(8,128)S(1)} %get-tuple-element.77.refs_3_, ...), custom_call_target="tpu_custom_call" | custom-call | flops 1000000000 | bytes 4000000 | tf_op jit(solution)/shard_map/advance/pallas_call | solution.py:82
  52.3 4.5 %all-to-all-start.1 = ((f32[8,16,128]{2,1,0:T(8,128)}), f32[8,16,128]{2,1,0:T(8,128)S(1)}, u32[]{:S(2)}, u32[]{:S(2)}) async-start(f32[8,16,128]{2,1,0:T(8,128)} %get-tuple-element.92), calls=%async_computation.1 | async-start | bytes 131072 | tf_op jit(solution)/shard_map/all_to_all | solution.py:607
  56.8 1.4 %copy-done.18 = bf16[3072,256]{1,0:T(8,128)(2,1)S(1)} copy-done((bf16[3072,256]{1,0:T(8,128)(2,1)S(1)}, bf16[3072,256]{1,0:T(8,128)(2,1)}, u32[]{:S(2)}) %copy-start.18) | copy-done | bytes 1572888
  58.2 3.9 %full.7 = (f32[1,3072]{1,0:T(1,128)S(1)}, f32[32,3072]{1,0:T(8,128)}) custom-call(f32[8,3072]{1,0:T(8,128)S(1)} %get-tuple-element.64.refs_0_, f32[64,128]{1,0:T(8,128)S(1)} %get-tuple-element.83.refs_1_, s32[1152,128]{1,0:T(8,128)S(1)} %copy-done.15, f32[32,128]{1,0:T(8,128)S(1)} %copy-done.19, f32[1,3072]{1,0:T(1,128)S(1)} %full.6.refs_4_, ...), custom_call_target="tpu_custom_call" | custom-call | flops 4000000000 | bytes 10000000 | tf_op jit(solution)/shard_map/full/pallas_call | solution.py:82
  62.1 1.5 %collective-permute-start.8 = (f32[1,3072]{1,0:T(1,128)S(1)}, f32[1,3072]{1,0:T(1,128)S(1)}, u32[]{:S(2)}, u32[]{:S(2)}) collective-permute-start(f32[1,3072]{1,0:T(1,128)S(1)} %get-tuple-element.91.refs_0_), channel_id=1, source_target_pairs={{0,2},{1,3},{2,0},{3,1},{4,6},{5,7},{6,4},{7,5},{8,10},{9,11},{10,... | collective-permute-start | bytes 36872 | tf_op jit(solution)/shard_map/ppermute | solution.py:642
  64.0 1.3 %collective-permute-done.9.refs_3_ = f32[1,3072]{1,0:T(1,128)S(1)} collective-permute-done((f32[1,3072]{1,0:T(1,128)S(1)}, f32[1,3072]{1,0:T(1,128)S(1)}, u32[]{:S(2)}, u32[]{:S(2)}) %collective-permute-start.9) | collective-permute-done | bytes 12320 | tf_op jit(solution)/shard_map/ppermute | solution.py:642
  65.8 0.8 %finish.1 = (f32[1,3072]{1,0:T(1,128)}, f32[32,128]{1,0:T(8,128)}) custom-call(f32[1,3072]{1,0:T(1,128)S(1)} %get-tuple-element.91.refs_0_, f32[1,3072]{1,0:T(1,128)S(1)} %collective-permute-done.7.refs_1_, f32[1,3072]{1,0:T(1,128)S(1)} %collective-permute-done.8.refs_2_, f32[1,3072]{1,0:T(1,128)S(1)} %collective-permute-done.9.refs_3_, ...), custom_call_target="tpu_custom_call" | custom-call | flops 1000000000 | bytes 4000000 | tf_op jit(solution)/shard_map/finish/pallas_call | solution.py:82
  (52 shorter events, 2.9 us)
Async XLA Ops:
  2.5 16.6 %all-to-all-start = ((f32[8,40,128]{2,1,0:T(8,128)}), f32[8,40,128]{2,1,0:T(8,128)S(1)}, u32[]{:S(2)}, u32[]{:S(2)}) async-start(f32[8,40,128]{2,1,0:T(8,128)} %get-tuple-element.53), calls=%async_computation | async-start | bytes 327680 | tf_op jit(solution)/shard_map/all_to_all | solution.py:494
  9.8 13.5 %collective-permute-start = (f32[2,32,256]{2,1,0:T(8,128)}, f32[2,32,256]{2,1,0:T(8,128)S(1)}, u32[]{:S(2)}, u32[]{:S(2)}) collective-permute-start(f32[2,32,256]{2,1,0:T(8,128)} %get-tuple-element.50.refs_10_), channel_id=1, source_target_pairs={{0,4},{4,8},{8,12},{12,16},{16,20},{20,24},{24,28},{28,0},{1,5},{5... | collective-permute-start | bytes 196616 | tf_op jit(solution)/shard_map/ppermute | solution.py:27
  11.9 11.5 %copy-start.8 = (f32[1,256]{1,0:T(1,128)S(1)}, f32[1,256]{1,0:T(1,128)}, u32[]{:S(2)}) copy-start(f32[1,256]{1,0:T(1,128)} %refs_0_.11) | copy-start | bytes 3076
  11.9 11.5 %copy-start.9 = (f32[1,256]{1,0:T(1,128)S(1)}, f32[1,256]{1,0:T(1,128)}, u32[]{:S(2)}) copy-start(f32[1,256]{1,0:T(1,128)} %refs_1_.11) | copy-start | bytes 3076
  11.9 11.5 %copy-start.10 = (s32[1,256]{1,0:T(1,128)S(1)}, s32[1,256]{1,0:T(1,128)}, u32[]{:S(2)}) copy-start(s32[1,256]{1,0:T(1,128)} %refs_6_.1) | copy-start | bytes 3076
  19.1 4.3 %copy-start = (f32[1,6,32,256]{3,2,1,0:T(8,128)S(1)}, f32[1,6,32,256]{3,2,1,0:T(8,128)}, u32[]{:S(2)}) copy-start(f32[1,6,32,256]{3,2,1,0:T(8,128)} %refs_9_.5) | copy-start | bytes 589828
  19.1 4.3 %copy-start.1 = (f32[1,6,32,256]{3,2,1,0:T(8,128)S(1)}, f32[1,6,32,256]{3,2,1,0:T(8,128)}, u32[]{:S(2)}) copy-start(f32[1,6,32,256]{3,2,1,0:T(8,128)} %refs_8_.3) | copy-start | bytes 589828
  19.1 4.3 %copy-start.2 = (f32[8,1024]{1,0:T(8,128)S(1)}, f32[8,1024]{1,0:T(8,128)}, u32[]{:S(2)}) copy-start(f32[8,1024]{1,0:T(8,128)} %get-tuple-element.49.refs_2_.refs_3_.refs_4_) | copy-start | bytes 98308
  23.5 6.2 %copy-start.11 = (f32[3072]{0:T(1024)S(1)}, f32[3072]{0:T(1024)}, u32[]{:S(2)}) copy-start(f32[3072]{0:T(1024)} %param.18) | copy-start | bytes 36868
  23.5 6.2 %copy-start.12 = (f32[3072]{0:T(1024)S(1)}, f32[3072]{0:T(1024)}, u32[]{:S(2)}) copy-start(f32[3072]{0:T(1024)} %param.19) | copy-start | bytes 36868
  23.5 6.2 %copy-start.15 = (s32[1152,128]{1,0:T(8,128)S(1)}, s32[1152,128]{1,0:T(8,128)}, u32[]{:S(2)}) copy-start(s32[1152,128]{1,0:T(8,128)} %get-tuple-element.52.refs_0_.refs_2_) | copy-start | bytes 1769476
  23.5 6.2 %copy-start.17 = (bf16[3072,256]{1,0:T(8,128)(2,1)S(1)}, bf16[3072,256]{1,0:T(8,128)(2,1)}, u32[]{:S(2)}) copy-start(bf16[3072,256]{1,0:T(8,128)(2,1)} %get-tuple-element.63.refs_6_) | copy-start | bytes 4718596
  23.5 6.2 %copy-start.19 = (f32[32,128]{1,0:T(8,128)S(1)}, f32[32,128]{1,0:T(8,128)}, u32[]{:S(2)}) copy-start(f32[32,128]{1,0:T(8,128)} %get-tuple-element.61.refs_3_) | copy-start | bytes 49156
  24.8 8.4 %collective-permute-start.1 = (f32[2,32,256]{2,1,0:T(8,128)S(1)}, f32[2,32,256]{2,1,0:T(8,128)S(1)}, u32[]{:S(2)}, u32[]{:S(2)}) collective-permute-start(f32[2,32,256]{2,1,0:T(8,128)S(1)} %get-tuple-element.68), channel_id=1, source_target_pairs={{0,4},{4,0},{8,12},{12,8},{16,20},{20,16},{24,28},{28,24},{1,5},{5... | collective-permute-start | bytes 196616 | tf_op jit(solution)/shard_map/ppermute | solution.py:36
  26.4 7.0 %collective-permute-start.2 = (f32[2,32,256]{2,1,0:T(8,128)S(1)}, f32[2,32,256]{2,1,0:T(8,128)S(1)}, u32[]{:S(2)}, u32[]{:S(2)}) collective-permute-start(f32[2,32,256]{2,1,0:T(8,128)S(1)} %get-tuple-element.69), channel_id=1, source_target_pairs={{4,8},{8,4},{12,16},{16,12},{20,24},{24,20},{28,0},{0,28},{5,9},{9... | collective-permute-start | bytes 196616 | tf_op jit(solution)/shard_map/ppermute | solution.py:36
  34.7 6.7 %collective-permute-start.3 = (f32[2,32,256]{2,1,0:T(8,128)S(1)}, f32[2,32,256]{2,1,0:T(8,128)S(1)}, u32[]{:S(2)}, u32[]{:S(2)}) collective-permute-start(f32[2,32,256]{2,1,0:T(8,128)S(1)} %get-tuple-element.75), channel_id=1, source_target_pairs={{0,4},{4,0},{8,12},{12,8},{16,20},{20,16},{24,28},{28,24},{1,5},{5... | collective-permute-start | bytes 196616 | tf_op jit(solution)/shard_map/ppermute | solution.py:36
  34.8 7.0 %collective-permute-start.4 = (f32[2,32,256]{2,1,0:T(8,128)S(1)}, f32[2,32,256]{2,1,0:T(8,128)S(1)}, u32[]{:S(2)}, u32[]{:S(2)}) collective-permute-start(f32[2,32,256]{2,1,0:T(8,128)S(1)} %get-tuple-element.76), channel_id=1, source_target_pairs={{4,8},{8,4},{12,16},{16,12},{20,24},{24,20},{28,0},{0,28},{5,9},{9... | collective-permute-start | bytes 196616 | tf_op jit(solution)/shard_map/ppermute | solution.py:36
  43.6 6.6 %collective-permute-start.5 = (f32[2,32,256]{2,1,0:T(8,128)S(1)}, f32[2,32,256]{2,1,0:T(8,128)S(1)}, u32[]{:S(2)}, u32[]{:S(2)}) collective-permute-start(f32[2,32,256]{2,1,0:T(8,128)S(1)} %get-tuple-element.81), channel_id=1, source_target_pairs={{0,4},{4,0},{8,12},{12,8},{16,20},{20,16},{24,28},{28,24},{1,5},{5... | collective-permute-start | bytes 196616 | tf_op jit(solution)/shard_map/ppermute | solution.py:36
  43.8 7.0 %collective-permute-start.6 = (f32[2,32,256]{2,1,0:T(8,128)S(1)}, f32[2,32,256]{2,1,0:T(8,128)S(1)}, u32[]{:S(2)}, u32[]{:S(2)}) collective-permute-start(f32[2,32,256]{2,1,0:T(8,128)S(1)} %get-tuple-element.82), channel_id=1, source_target_pairs={{4,8},{8,4},{12,16},{16,12},{20,24},{24,20},{28,0},{0,28},{5,9},{9... | collective-permute-start | bytes 196616 | tf_op jit(solution)/shard_map/ppermute | solution.py:36
  52.3 13.5 %all-to-all-start.1 = ((f32[8,16,128]{2,1,0:T(8,128)}), f32[8,16,128]{2,1,0:T(8,128)S(1)}, u32[]{:S(2)}, u32[]{:S(2)}) async-start(f32[8,16,128]{2,1,0:T(8,128)} %get-tuple-element.92), calls=%async_computation.1 | async-start | bytes 131072 | tf_op jit(solution)/shard_map/all_to_all | solution.py:607
  58.2 7.6 %copy-start.13 = (s32[1,128]{1,0:T(1,128)S(1)}, s32[1,128]{1,0:T(1,128)}, u32[]{:S(2)}) copy-start(s32[1,128]{1,0:T(1,128)} %refs_5_.3) | copy-start | bytes 1540
  62.1 3.2 %collective-permute-start.9 = (f32[1,3072]{1,0:T(1,128)S(1)}, f32[1,3072]{1,0:T(1,128)S(1)}, u32[]{:S(2)}, u32[]{:S(2)}) collective-permute-start(f32[1,3072]{1,0:T(1,128)S(1)} %get-tuple-element.91.refs_0_), channel_id=1, source_target_pairs={{0,3},{1,2},{2,1},{3,0},{4,7},{5,6},{6,5},{7,4},{8,11},{9,10},{10,... | collective-permute-start | bytes 36872 | tf_op jit(solution)/shard_map/ppermute | solution.py:642
  62.1 3.7 %collective-permute-start.8 = (f32[1,3072]{1,0:T(1,128)S(1)}, f32[1,3072]{1,0:T(1,128)S(1)}, u32[]{:S(2)}, u32[]{:S(2)}) collective-permute-start(f32[1,3072]{1,0:T(1,128)S(1)} %get-tuple-element.91.refs_0_), channel_id=1, source_target_pairs={{0,2},{1,3},{2,0},{3,1},{4,6},{5,7},{6,4},{7,5},{8,10},{9,11},{10,... | collective-permute-start | bytes 36872 | tf_op jit(solution)/shard_map/ppermute | solution.py:642
  63.6 2.2 %collective-permute-start.7 = (f32[1,3072]{1,0:T(1,128)S(1)}, f32[1,3072]{1,0:T(1,128)S(1)}, u32[]{:S(2)}, u32[]{:S(2)}) collective-permute-start(f32[1,3072]{1,0:T(1,128)S(1)} %get-tuple-element.91.refs_0_), channel_id=1, source_target_pairs={{0,1},{1,0},{2,3},{3,2},{4,5},{5,4},{6,7},{7,6},{8,9},{9,8},{10,11... | collective-permute-start | bytes 36872 | tf_op jit(solution)/shard_map/ppermute | solution.py:642
  (8 other events, 20.2 us)

commit v2 on v1

--- a/solution.py
+++ b/solution.py
@@ -12,7 +12,8 @@
 DMIN = 2
 LANES = 128
 VMEM = 67043328
-ROOM = 1600 << 10
+ROOM = 30000 << 10
+WIDE = 4
 OMEGA = 0.01884955592153876
 EPS = 1e-06
 F32 = jnp.float32
@@ -102,6 +103,14 @@
     return jnp.where(mask, 1.0, 0.0).astype(BF16)
 
 
+def owned(mark, k):
+    return jnp.where(mark == jnp.asarray(k, BF16), jnp.asarray(1, BF16), jnp.asarray(0, BF16))
+
+
+def owner_of(mark):
+    return jnp.max(mark.astype(F32), axis=1, keepdims=True)
+
+
 def dot(left, right, dims=NN):
     return lax.dot_general(left, right, dims, preferred_element_type=F32)
 
@@ -141,7 +150,7 @@
 
 
 def start_body(sizes, i, o):
-    regions, cap, half, scen, group, maxd = sizes
+    regions, cap, half, scen, group, maxd, lines, nreg = sizes
     packed = 2 * cap == LANES
     i.ready("slots", "par", "state")
     slots = i.slots[...]
@@ -171,6 +180,23 @@
     delays = i.delay[...]
     for step in range(2):
         o.into[step] = pick(lambda t: i.hist[0, t + maxd], delays, step, maxd)
+    o.flush("into")
+    i.ready("end_a", "end_b", "conv", "fault_node", "fault_step", "fault_cond", "amp", "phase")
+    pack = o.pack
+    pack[0:1, :] = i.amp[...]
+    pack[1:2, :] = i.phase[...]
+    pack[2:3, 0:scen] = i.fault_step[...].astype(F32)
+    pack[3:4, 0:scen] = i.fault_cond[...]
+    points = 2 * lines + regions * cap
+    pack[4:5, 0 : points + LANES] = jnp.full((1, points + LANES), -1.0, F32)
+    pack[4:5, 0:lines] = i.end_a[...].astype(F32)
+    pack[4:5, lines : 2 * lines] = i.end_b[...].astype(F32)
+    for index in range(regions):
+        first = 2 * lines + index * cap
+        pack[4:5, first : first + cap] = i.conv[0, index : index + 1, :].astype(F32)
+    fault = i.fault_node[...] - lax.axis_index("region") * nreg
+    fault = jnp.where((fault >= 0) & (fault < nreg), fault, -1)
+    pack[4:5, points : points + scen] = fault.astype(F32)
 
 
 def sources(amp, phase):
@@ -178,37 +204,26 @@
     return amp * jnp.cos(OMEGA * instant + phase)
 
 
-def rows_body(sizes, i, o, place, source_rows):
+def rows_body(sizes, i, o, place, zcat, source_rows):
     nreg, nblk, lines, regions, cap, scen = sizes
     blk = LANES
     width = regions * cap
     points = 2 * lines + width
     whole = points + blk
-    i.ready("end_a", "end_b", "conv", "fault_node")
-    o.row[...] = jnp.full((1, whole), -1, jnp.int32)
-    o.row[:, 0:lines] = i.end_a[...]
-    o.row[:, lines : 2 * lines] = i.end_b[...]
-    for group in range(regions):
-        start = 2 * lines + group * cap
-        o.row[:, start : start + cap] = i.conv[0, group : group + 1, :]
-    region = lax.axis_index("region")
-    fault = i.fault_node[...] - region * nreg
-    fault = jnp.where((fault >= 0) & (fault < nreg), fault, -1)
-    o.row[:, points : points + scen] = fault
-    row = o.row[...]
-    column = jnp.transpose(jnp.broadcast_to(row.astype(F32), (blk, whole))).astype(jnp.int32)
-    o.column[...] = column
-    lane = iota((whole, blk), 1)
+    whole_row = i.pack[4:5, 0:whole]
+    row = whole_row.astype(jnp.int32)
+    o.row[...] = row
+    column = jnp.transpose(jnp.broadcast_to(whole_row, (blk, whole))).astype(jnp.int32)
+    here = (column & 127) == iota((whole, blk), 1)
+    o.mark[...] = jnp.where(here, (column >> 7).astype(F32), -1.0).astype(BF16)
     for k in range(nblk):
-        place[:, k * blk : (k + 1) * blk] = onehot(o.column[...] == lane + k * blk)
+        place[:, k * blk : (k + 1) * blk] = owned(o.mark[...], k)
     i.ready("inv")
     z_high, z_low = split2(i.inv[...].reshape(nreg, blk))
-    o.zcat[:, 0:blk] = z_high
-    o.zcat[:, blk:] = z_low
-    o.flush("zcat")
-    o.rows[...] = dot(place[...], o.zcat[...]).astype(BF16)
-    i.ready("amp", "phase")
-    source = sources(i.amp[...], i.phase[...])
+    zcat[:, 0:blk] = z_high
+    zcat[:, blk:] = z_low
+    o.rows[...] = dot(place[...], zcat[...]).astype(BF16)
+    source = sources(i.pack[0:1, :], i.pack[1:2, :])
     for k in range(nblk):
         source_rows[k * STEPS : (k + 1) * STEPS, :] = source[:, k * blk : (k + 1) * blk]
     spread = product3(source_rows[...], o.rows[:, :blk], o.rows[:, blk:], NT)
@@ -229,30 +244,28 @@
         axis=1,
         keepdims=True,
     )
-    i.ready("fault_cond", "fault_step")
-    cond = as_column(i.fault_cond[...], scen)
-    closes = as_column(i.fault_step[...].astype(F32), scen)
+    cond = as_column(i.pack[3:4, 0:scen], scen)
+    closes = as_column(i.pack[2:3, 0:scen], scen)
     ratio = cond / (1.0 + cond * self_imp)
     o.fault_ratio[...] = jnp.where(
         closes <= iota((scen, blk), 1).astype(F32), jnp.broadcast_to(ratio, (scen, blk)), 0.0
     )
 
 
-def between_body(sizes, i, o):
-    points, scen = sizes
+def between_body(points, scen, i, o):
     blk = LANES
     row = i.row[:, :points]
-    row_blk = row >> 7
+    row_blk = (row >> 7).astype(F32)
     inside = onehot(iota((blk, points), 0) == (row & 127))
     for k in range(points // blk):
         here = slice(k * blk, (k + 1) * blk)
-        same = (i.column[here, 0:1] >> 7) == row_blk
+        same = owner_of(i.mark[here, :]) == row_blk
         both = dot(jnp.concatenate([i.rows[here, :blk], i.rows[here, blk:]], axis=0), inside)
         o.m_high[here, :] = jnp.where(same, both[:blk], 0.0).astype(BF16)
         o.m_low[here, :] = jnp.where(same, both[blk:], 0.0).astype(BF16)
     here = slice(points, points + scen)
     both = dot(jnp.concatenate([i.rows[here, :blk], i.rows[here, blk:]], axis=0), inside)
-    same = (i.column[here, 0:1] >> 7) == row_blk
+    same = owner_of(i.mark[here, :]) == row_blk
     o.fault_p[...] = jnp.where(same, both[:scen] + both[scen:], 0.0)
 
 
@@ -267,9 +280,9 @@
     even = lax.rem(lax.axis_index("region"), 2) == 0
     fresh = {}
     if pair:
-        far_in = [jnp.where(even, i.swap_b[j], i.swap_a[j]) for j in range(2)]
+        far_in = [jnp.where(even, i.swap_far[j], i.swap_near[j]) for j in range(2)]
         for j in range(2):
-            far_volts = jnp.where(even, i.swap_a[j], i.swap_b[j])
+            far_volts = jnp.where(even, i.swap_near[j], i.swap_far[j])
             fresh[t0 - 2 + j] = scale * (twice * far_volts - i.into_prev[j])
             if hasattr(o, "back"):
                 o.back[j] = fresh[t0 - 2 + j]
@@ -292,6 +305,10 @@
             return i.hist_a[0, t + maxd]
         return i.made[t // 2][t % 2]
 
+    points = 2 * lines + width
+    known = i if pair else o
+    if not pair:
+        between_body(points, scen, i, o)
     live = i.row[:, 2 * lines : 2 * lines + width] >= 0
     if packed:
         low = iota((1, LANES), 1) < cap
@@ -324,45 +341,60 @@
             first, second = i.recv[0, :scen], i.recv[1, :scen]
         current = drive(second)
 
-    fault_p = i.fault_p[...]
+    fault_p = known.fault_p[...]
     ends = 2 * lines
-    sides = []
     arrivals = [pick(back, delays, t0 + j, maxd) for j in range(2)]
-    waves = [jnp.concatenate([arrivals[j], far_in[j]], axis=1) for j in range(2)]
-    pairs = split2(jnp.concatenate(waves, axis=0))
+    waves = jnp.concatenate(
+        [jnp.concatenate([arrivals[j], far_in[j]], axis=1) for j in range(2)], axis=0
+    )
+    pairs = split2(waves)
     for part in range(2):
         o.x[part * 2 * scen : (part + 1) * 2 * scen, :ends] = pairs[part]
-    both = dot(jnp.concatenate(pairs, axis=0), i.m_high[:ends, :])
-    of_lines = both[: 2 * scen] + both[2 * scen :] + dot(pairs[0], i.m_low[:ends, :])
+    both = dot(jnp.concatenate(pairs, axis=0), known.m_high[:ends, :])
+    volts = both[: 2 * scen] + both[2 * scen :] + dot(pairs[0], known.m_low[:ends, :])
+    base = [jnp.broadcast_to(i.base_p[t0 + j : t0 + j + 1, :], (scen, points)) for j in range(2)]
+    volts = volts + jnp.concatenate(base, axis=0)
+    fault_ends, fault_conv = fault_p[:, :ends], fault_p[:, ends:]
+    wave_fault = jnp.sum(
+        waves * jnp.concatenate([fault_ends, fault_ends], axis=0), axis=1, keepdims=True
+    )
+    highs, lows, coefs = [], [], []
     for j in range(2):
-        t = t0 + j
-        into = arrivals[j]
-        x = jnp.concatenate([waves[j], current], axis=1)
+        here = slice(j * scen, (j + 1) * scen)
         high, low_part = split2(current)
+        highs.append(high)
+        lows.append(low_part)
         o.x[j * scen : (j + 1) * scen, ends:] = high
         o.x[(2 + j) * scen : (3 + j) * scen, ends:] = low_part
-        both = dot(jnp.concatenate([high, low_part], axis=0), i.m_high[ends:, :])
-        volts = both[:scen] + both[scen:] + dot(high, i.m_low[ends:, :])
-        volts = volts + of_lines[j * scen : (j + 1) * scen] + i.base_p[t : t + 1, :]
-        at_fault = i.fault_base[:, t : t + 1] + jnp.sum(x * fault_p, axis=1, keepdims=True)
-        coef = i.fault_ratio[:, t : t + 1] * at_fault
-        o.coef[j * scen : (j + 1) * scen, :] = jnp.broadcast_to(coef, (scen, LANES))
-        volts = volts - fault_p * coef
-        if t <= last - DMIN:
-            made[t] = scale * (twice * volts[:, :lines] - into)
-            sides.append(volts[:, lines : 2 * lines])
-            if hasattr(o, "out"):
-                o.out[j] = made[t]
-        node = volts[:, 2 * lines :]
+        both = dot(jnp.concatenate([high, low_part], axis=0), known.m_high[ends:, ends:])
+        node = both[:scen] + both[scen:] + dot(high, known.m_low[ends:, ends:])
+        at_fault = i.fault_base[:, t0 + j : t0 + j + 1] + wave_fault[here]
+        at_fault = at_fault + jnp.sum(current * fault_conv, axis=1, keepdims=True)
+        coef = i.fault_ratio[:, t0 + j : t0 + j + 1] * at_fault
+        coefs.append(coef)
+        o.coef[here, :] = jnp.broadcast_to(coef, (scen, LANES))
+        node = node + volts[here, ends:] - fault_conv * coef
         first = params[1] * first + params[2] * (params[0] - node)
         second = second + params[3] * (first - second)
         current = drive(second)
+    sides = []
+    if t0 <= last - DMIN:
+        both = dot(jnp.concatenate(highs + lows, axis=0), known.m_high[ends:, :ends])
+        more = both[: 2 * scen] + both[2 * scen :]
+        more = more + dot(jnp.concatenate(highs, axis=0), known.m_low[ends:, :ends])
+        for j in range(2):
+            here = slice(j * scen, (j + 1) * scen)
+            line = volts[here, :ends] + more[here] - fault_ends * coefs[j]
+            made[t0 + j] = scale * (twice * line[:, :lines] - arrivals[j])
+            sides.append(line[:, lines:])
+            if hasattr(o, "out"):
+                o.out[j] = made[t0 + j]
     if hasattr(o, "into"):
         for j in range(2):
             onward = pick(out, delays, t0 + 2 + j, maxd)
             o.into[j] = onward
-            o.swap_a[j] = jnp.where(even, onward, sides[j])
-            o.swap_b[j] = jnp.where(even, sides[j], onward)
+            o.swap_near[j] = jnp.where(even, onward, sides[j])
+            o.swap_far[j] = jnp.where(even, sides[j], onward)
     if hasattr(o, "state"):
         o.state[0] = first
         o.state[1] = second
@@ -382,36 +414,32 @@
     blk = LANES
     t0 = 2 * pair
     fault_z = i.fault_z[...]
-    fault_blk = i.column[points : points + scen, :] >> 7
+    fault_blk = owner_of(i.mark[points : points + scen, :])
     x = i.x[...]
     coef = i.coef[...]
-    lane = iota((points, blk), 1)
+    i.ready("inv")
     if pair:
         all_base = i.base
     else:
         all_base = o.base
-        source = sources(i.amp[...], i.phase[...])
+        source = sources(i.pack[0:1, :], i.pack[1:2, :])
         for k in range(nblk):
             here = slice(k * blk, (k + 1) * blk)
-            z = i.zcat[here, :]
-            o.base[:, here] = product3(source[:, here], z[:, :blk], z[:, blk:])
-    for k in range(0, nblk, 2):
-        mine = jnp.concatenate(
-            [onehot(i.column[:points, :] == lane + (k + j) * blk) for j in range(2)], axis=1
-        )
+            o.base[:, here] = product3(source[:, here], *split2(i.inv[k]))
+    for k in range(0, nblk, WIDE):
+        mine = jnp.concatenate([owned(i.mark[:points], k + j) for j in range(WIDE)], axis=1)
         both = dot(x, mine)
         inject = both[: 2 * scen] + both[2 * scen :]
-        for j in range(2):
+        for j in range(WIDE):
             here = slice((k + j) * blk, (k + j + 1) * blk)
-            z = i.zcat[here, :]
-            volts = product3(inject[:, j * blk : (j + 1) * blk], z[:, :blk], z[:, blk:])
+            volts = product3(inject[:, j * blk : (j + 1) * blk], *split2(i.inv[k + j]))
             base = [
                 jnp.broadcast_to(all_base[t0 + m : t0 + m + 1, here], (scen, blk))
                 for m in range(2)
             ]
-            column = jnp.where(fault_blk == k + j, fault_z, 0.0)
+            zcol = jnp.where(fault_blk == k + j, fault_z, 0.0)
             volts = volts + jnp.concatenate(base, axis=0)
-            volts = volts - jnp.concatenate([column, column], axis=0) * coef
+            volts = volts - jnp.concatenate([zcol, zcol], axis=0) * coef
             total = jnp.sum(volts * volts, axis=0, keepdims=True)
             if hasattr(i, "squares"):
                 total = total + i.squares[:, here]
@@ -481,13 +509,29 @@
 
     send_shape = (regions, half, LANES) if packed else (half, regions * 2 * cap)
     head = call(
-        functools.partial(start_body, (regions, cap, half, scen, group, maxd)),
+        functools.partial(start_body, (regions, cap, half, scen, group, maxd, lines, nreg)),
         "start",
         {},
         {},
-        hbm_outs=dict(send=(send_shape, F32), into=((2, scen, lines), F32)),
+        hbm_outs=dict(
+            send=(send_shape, F32), into=((2, scen, lines), F32), pack=((8, nreg), F32)
+        ),
         limit=VMEM,
-        hbm=dict(slots=recv_slot, par=conv_par, state=conv_state, hist=hist_ua, delay=line_delay),
+        hbm=dict(
+            slots=recv_slot,
+            par=conv_par,
+            state=conv_state,
+            hist=hist_ua,
+            delay=line_delay,
+            end_a=line_a,
+            end_b=line_b,
+            conv=send_node,
+            amp=src_amp.reshape(1, nreg),
+            phase=src_phase.reshape(1, nreg),
+            fault_node=fault_node.reshape(1, scen),
+            fault_step=fault_step.reshape(1, scen),
+            fault_cond=fault_cond.reshape(1, scen),
+        ),
     )
     send = head.send
     if packed:
@@ -503,46 +547,28 @@
     model = call(
         functools.partial(rows_body, (nreg, nblk, lines, regions, cap, scen)),
         "rows",
-        {},
+        dict(pack=head.pack),
         dict(
             row=((1, whole), jnp.int32),
-            column=((whole, blk), jnp.int32),
+            mark=((whole, blk), BF16),
             rows=((whole, 2 * blk), BF16),
             base_p=((STEPS, points), F32),
             fault_z=((scen, blk), F32),
             fault_base=((scen, blk), F32),
             fault_ratio=((scen, blk), F32),
         ),
-        hbm_outs=dict(zcat=((nreg, 2 * blk), BF16)),
-        hbm=dict(
-            end_a=line_a,
-            end_b=line_b,
-            conv=send_node,
-            fault_node=fault_node.reshape(1, scen),
-            inv=inv_blocks,
-            amp=src_amp.reshape(1, nreg),
-            phase=src_phase.reshape(1, nreg),
-            fault_step=fault_step.reshape(1, scen),
-            fault_cond=fault_cond.reshape(1, scen),
+        hbm=dict(inv=inv_blocks),
+        scratch=(
+            pltpu.VMEM((whole, nreg), BF16),
+            pltpu.VMEM((nreg, 2 * blk), BF16),
+            pltpu.VMEM((STEPS * nblk, blk), F32),
         ),
-        scratch=(pltpu.VMEM((whole, nreg), BF16), pltpu.VMEM((STEPS * nblk, blk), F32)),
         limit=VMEM - ROOM,
         cost=(4e9, 2e7),
     )
-    matrix = call(
-        functools.partial(between_body, (points, scen)),
-        "between",
-        dict(row=model.row, column=model.column, rows=model.rows, recv=recv),
-        dict(
-            m_high=((points, points), BF16),
-            m_low=((points, points), BF16),
-            fault_p=((scen, points), F32),
-        ),
-    )
-
     wave = ((2, scen, lines), F32)
     mades, backs, carry = {}, {}, {}
-    squares = swap_a = swap_b = sent = base = None
+    squares = swap_near = swap_far = sent = base = None
     for pair in range(STEPS // 2):
         t0 = 2 * pair
         final = t0 + 2 >= STEPS
@@ -550,12 +576,8 @@
             delay=line_delay,
             atten=line_atten,
             admit=line_yc,
-            row=model.row,
             recv=recv,
-            m_high=matrix.m_high,
-            m_low=matrix.m_low,
             base_p=model.base_p,
-            fault_p=matrix.fault_p,
             fault_base=model.fault_base,
             fault_ratio=model.fault_ratio,
             **carry,
@@ -563,9 +585,11 @@
         if t0 - maxd < 0:
             ins.update(hist_b=hist_ub)
         if pair:
-            ins.update(swap_a=swap_a, swap_b=swap_b, into_prev=sent)
+            ins.update(swap_near=swap_near, swap_far=swap_far, into_prev=sent, row=model.row)
+            ins.update(m_high=matrix.m_high, m_low=matrix.m_low, fault_p=matrix.fault_p)
         else:
             ins.update(far_in=far_in)
+            ins.update(row=model.row, mark=model.mark, rows=model.rows)
         first = max(0, pair - 3)
         ins.update(backs={k: v for k, v in backs.items() if k >= first})
         if not final:
@@ -575,15 +599,22 @@
         outs = dict(x=((4 * scen, points), BF16), coef=((2 * scen, LANES), F32))
         if not final:
             outs.update(
-                swap_a=wave,
-                swap_b=wave,
-                out=wave,
+                swap_far=wave,
+                swap_near=wave,
                 into=wave,
                 state=((2, scen, width), F32),
                 current=((scen, width), F32),
             )
+            if t0 + 4 < STEPS:
+                outs.update(out=wave)
             if pair:
                 outs.update(back=wave)
+            else:
+                outs.update(
+                    m_high=((points, points), BF16),
+                    m_low=((points, points), BF16),
+                    fault_p=((scen, points), F32),
+                )
         else:
             shape = (regions, scen // 2, LANES) if packed else (scen, width)
             outs.update(current=(shape, F32))
@@ -593,11 +624,14 @@
             ins,
             outs,
         )
+        if not pair:
+            matrix = made
         if not final:
             sent, into = into, made.into
-            swap_a = swapped(made.swap_a, "region", 0)
-            swap_b = swapped(made.swap_b, "region", 1)
-            mades[pair] = made.out
+            swap_far = swapped(made.swap_far, "region", 1)
+            swap_near = swapped(made.swap_near, "region", 0)
+            if t0 + 4 < STEPS:
+                mades[pair] = made.out
             if pair:
                 backs[pair - 1] = made.back
             carry = dict(state=made.state, current=made.current)
@@ -612,14 +646,13 @@
         ins = dict(
             x=made.x,
             coef=made.coef,
-            column=model.column,
-            zcat=model.zcat,
+            mark=model.mark,
             fault_z=model.fault_z,
         )
         if pair:
             ins.update(squares=squares, base=base)
         else:
-            ins.update(amp=src_amp.reshape(1, nreg), phase=src_phase.reshape(1, nreg))
+            ins.update(pack=head.pack)
         outs = dict(squares=((1, nreg), F32))
         if final:
             outs.update(volts=((scen, nreg), F32))
@@ -630,6 +663,7 @@
             "full",
             ins,
             outs,
+            hbm=dict(inv=inv_blocks),
             cost=(4e9, 1e7),
         )
         squares = full.squares

time: 67.1 us -> 61.8 us (0.921)
  starting transfers between devices: 27.3 us -> 22.5 us
  waiting for transfers between devices: 2.8 us -> 6.5 us
  local copies, waits for them, and re-layouts: 4.38 us -> 2.34 us
  Pallas kernels: 31.2 us -> 29.2 us
    ppermute x6, starting transfers between devices: 11.6 us -> 7.79 us  [swapped(): return lax.ppermute(value, axis, pairs)]
    ppermute x6, waiting for transfers between devices: 0.95 us -> 4.58 us  [swapped(): return lax.ppermute(value, axis, pairs)]
    unnamed x40 -> x22, local copies, waits for them, and re-layouts: 4.38 us -> 2.34 us
    pallas_call x12 -> x11, Pallas kernels: 31.2 us -> 29.2 us  [call(): pl.pallas_call(kernel, name=name, out_shape=[jax.ShapeDtypeStruct(*shape)...]
    all_to_all x1, starting transfers between devices: 4.53 us -> 3.51 us  [per_device(): lax.all_to_all(current, 'region', split_axis=0, concat_axis=0, tiled=True)]
  transfers between devices with their start and end apart: 12 -> 12, of which waited for: 4 -> 8; matrix products, arithmetic and copies ran while one was open for 0% -> 0% of each run, Pallas kernels for 34% -> 32%
where the time goes in v2:
time: 61.8 us; the launch traced here: 61.4 us
  Pallas kernels  29.2 us (47%)
  starting transfers between devices  22.5 us (36%)
  waiting for transfers between devices  6.5 us (11%)
  local copies, waits for them, and re-layouts  2.34 us (4%)
  between operations  0.81 us (1%)
    pallas_call x11, Pallas kernels, call(): pl.pallas_call(kernel, name=name, out_shape=[jax.ShapeDtypeStruct(*shape)...  29.2 us
    ppermute x6, starting transfers between devices, swapped(): return lax.ppermute(value, axis, pairs)  7.79 us
    all_to_all x1, starting transfers between devices, per_device(): lax.all_to_all(send, 'region', split_axis=0, concat_axis=0, tiled=True)  7.29 us
    ppermute x6, waiting for transfers between devices, swapped(): return lax.ppermute(value, axis, pairs)  4.58 us
    all_to_all x1, starting transfers between devices, per_device(): lax.all_to_all(current, 'region', split_axis=0, concat_axis=0, tiled=True)  3.51 us
    unnamed x22, local copies, waits for them, and re-layouts  2.34 us
    ppermute x1, starting transfers between devices, shifted(): return lax.ppermute(value, axis, pairs)  2.02 us
    ppermute x3, starting transfers between devices, per_device(): parts.append(lax.ppermute(squares, 'scen', pairs))  1.92 us
  transfers between devices with their start and end apart: 12, of which 8 were waited for; matrix products, arithmetic and copies ran while one was open for 0% of the time, Pallas kernels for 32%

profile of v2, /device:TPU:0, one launch (start us, length us, event | category | flops | bytes accessed | tf_op | source)
XLA Modules:
  0.0 61.4 jit_solution(719917475791642122)
XLA Ops:
  0.6 2.1 %start.1 = (f32[8,40,128]{2,1,0:T(8,128)}, f32[2,32,256]{2,1,0:T(8,128)}, f32[8,3072]{1,0:T(8,128)}) custom-call(s32[1,128]{1,0:T(1,128)} %refs_5_.7, f32[6,128]{1,0:T(8,128)} %refs_1_.6, f32[2,32,128]{2,1,0:T(8,128)} %refs_2_.1, f32[1,6,32,256]{3,2,1,0:T(8,128)} %refs_8_.3, s32[1,256]{1,0:T(1,128)} %refs_6_.6, s32[1,256]{1,0:T(1,128)} %refs_5_.4, ...), custom_call_target="tpu_custom_call" | custom-call | flops 1000000000 | bytes 4000000 | tf_op jit(solution)/shard_map/start/pallas_call | solution.py:83
  2.7 7.3 %all-to-all-start = ((f32[8,40,128]{2,1,0:T(8,128)}), f32[8,40,128]{2,1,0:T(8,128)S(1)}, u32[]{:S(2)}, u32[]{:S(2)}) async-start(f32[8,40,128]{2,1,0:T(8,128)} %get-tuple-element.55), calls=%async_computation | async-start | bytes 327680 | tf_op jit(solution)/shard_map/all_to_all | solution.py:538
  10.0 2.0 %collective-permute-start = (f32[2,32,256]{2,1,0:T(8,128)}, f32[2,32,256]{2,1,0:T(8,128)S(1)}, u32[]{:S(2)}, u32[]{:S(2)}) collective-permute-start(f32[2,32,256]{2,1,0:T(8,128)} %get-tuple-element.51.refs_10_), channel_id=1, source_target_pairs={{0,4},{4,8},{8,12},{12,16},{16,20},{20,24},{24,28},{28,0},{1,5},{5... | collective-permute-start | bytes 196616 | tf_op jit(solution)/shard_map/ppermute | solution.py:28
  12.0 1.4 %copy-done.6 = f32[24,128,128]{2,1,0:T(8,128)S(1)} copy-done((f32[24,128,128]{2,1,0:T(8,128)S(1)}, f32[24,128,128]{2,1,0:T(8,128)}, u32[]{:S(2)}) %copy-start.6) | copy-done | bytes 1572888
  13.4 0.9 %copy-done.9 = f32[8,3072]{1,0:T(8,128)S(1)} copy-done((f32[8,3072]{1,0:T(8,128)S(1)}, f32[8,3072]{1,0:T(8,128)}, u32[]{:S(2)}) %copy-start.9) | copy-done | bytes 98328
  14.3 5.6 %rows.1 = (s32[1,1152]{1,0:T(1,128)S(1)}, bf16[1152,128]{1,0:T(8,128)(2,1)S(1)}, bf16[1152,256]{1,0:T(8,128)(2,1)S(1)}, f32[8,1024]{1,0:T(8,128)S(1)}, f32[32,12...) custom-call(f32[8,3072]{1,0:T(8,128)S(1)} %copy-done.9, f32[24,128,128]{2,1,0:T(8,128)S(1)} %copy-done.6), custom_call_target="tpu_custom_call" | custom-call | flops 4000000000 | bytes 20000000 | tf_op jit(solution)/shard_map/rows/pallas_call | solution.py:83
  20.0 2.4 %advance.4 = (bf16[128,1024]{1,0:T(8,128)(2,1)S(1)}, f32[64,128]{1,0:T(8,128)S(1)}, f32[2,32,256]{2,1,0:T(8,128)S(1)}, f32[2,32,256]{2,1,0:T(8,128)S(1)}, f32[2,...) custom-call(f32[1,256]{1,0:T(1,128)S(1)} %copy-done.3, ...), custom_call_target="tpu_custom_call" | custom-call | flops 1000000000 | bytes 4000000 | tf_op jit(solution)/shard_map/advance/pallas_call | solution.py:83
  22.4 2.8 %collective-permute-start.1 = (f32[2,32,256]{2,1,0:T(8,128)S(1)}, f32[2,32,256]{2,1,0:T(8,128)S(1)}, u32[]{:S(2)}, u32[]{:S(2)}) collective-permute-start(f32[2,32,256]{2,1,0:T(8,128)S(1)} %get-tuple-element.68), channel_id=1, source_target_pairs={{4,8},{8,4},{12,16},{16,12},{20,24},{24,20},{28,0},{0,28},{5,9},{9... | collective-permute-start | bytes 196616 | tf_op jit(solution)/shard_map/ppermute | solution.py:37
  25.4 3.6 %full.4 = (f32[1,3072]{1,0:T(1,128)S(1)}, f32[8,3072]{1,0:T(8,128)S(1)}) custom-call(f32[64,128]{1,0:T(8,128)S(1)} %get-tuple-element.58.refs_0_, f32[32,128]{1,0:T(8,128)S(1)} %get-tuple-element.59.refs_1_.refs_2_, bf16[1152,128]{1,0:T(8,128)(2,1)S(1)} %get-tuple-element.54.refs_9_.refs_2_.refs_3_, f32[8,3072]{1,0:T(8,128)S(1)} %copy-done.10, ...), custom_call_target="tpu_custom_call" | custom-call | flops 4000000000 | bytes 10000000 | tf_op jit(solution)/shard_map/full/pallas_call | solution.py:83
  29.5 0.6 %collective-permute-done.2.refs_18_ = f32[2,32,256]{2,1,0:T(8,128)S(1)} collective-permute-done((f32[2,32,256]{2,1,0:T(8,128)S(1)}, f32[2,32,256]{2,1,0:T(8,128)S(1)}, u32[]{:S(2)}, u32[]{:S(2)}) %collective-permute-start.2) | collective-permute-done | bytes 65568 | tf_op jit(solution)/shard_map/ppermute | solution.py:37
  30.2 1.2 %advance.5 = (bf16[128,1024]{1,0:T(8,128)(2,1)S(1)}, f32[64,128]{1,0:T(8,128)S(1)}, f32[2,32,256]{2,1,0:T(8,128)S(1)}, f32[2,32,256]{2,1,0:T(8,128)S(1)}, f32[2,...) custom-call(f32[1,256]{1,0:T(1,128)S(1)} %copy-done.3, ...), custom_call_target="tpu_custom_call" | custom-call | flops 1000000000 | bytes 4000000 | tf_op jit(solution)/shard_map/advance/pallas_call | solution.py:83
  31.3 2.3 %collective-permute-start.3 = (f32[2,32,256]{2,1,0:T(8,128)S(1)}, f32[2,32,256]{2,1,0:T(8,128)S(1)}, u32[]{:S(2)}, u32[]{:S(2)}) collective-permute-start(f32[2,32,256]{2,1,0:T(8,128)S(1)} %get-tuple-element.75), channel_id=1, source_target_pairs={{4,8},{8,4},{12,16},{16,12},{20,24},{24,20},{28,0},{0,28},{5,9},{9... | collective-permute-start | bytes 196616 | tf_op jit(solution)/shard_map/ppermute | solution.py:37
  33.6 3.3 %full.5.refs_4_ = f32[1,3072]{1,0:T(1,128)S(1)} custom-call(f32[8,3072]{1,0:T(8,128)S(1)} %get-tuple-element.61.refs_0_, f32[64,128]{1,0:T(8,128)S(1)} %get-tuple-element.85.refs_1_, f32[32,128]{1,0:T(8,128)S(1)} %get-tuple-element.59.refs_1_.refs_2_, bf16[1152,128]{1,0:T(8,128)(2,1)S(1)} %get-tuple-element.54.refs_9_.refs_2_.refs_3_, ...), custom_call_target="tpu_custom_call" | custom-call | flops 4000000000 | bytes 10000000 | tf_op jit(solution)/shard_map/full/pallas_call | solution.py:83
  36.9 1.5 %collective-permute-done.3.refs_18_ = f32[2,32,256]{2,1,0:T(8,128)S(1)} collective-permute-done((f32[2,32,256]{2,1,0:T(8,128)S(1)}, f32[2,32,256]{2,1,0:T(8,128)S(1)}, u32[]{:S(2)}, u32[]{:S(2)}) %collective-permute-start.3) | collective-permute-done | bytes 65568 | tf_op jit(solution)/shard_map/ppermute | solution.py:37
  38.6 1.8 %advance.6 = (bf16[128,1024]{1,0:T(8,128)(2,1)S(1)}, f32[64,128]{1,0:T(8,128)S(1)}, f32[2,32,256]{2,1,0:T(8,128)S(1)}, f32[2,32,256]{2,1,0:T(8,128)S(1)}, f32[2,...) custom-call(f32[1,256]{1,0:T(1,128)S(1)} %copy-done.3, ...), custom_call_target="tpu_custom_call" | custom-call | flops 1000000000 | bytes 4000000 | tf_op jit(solution)/shard_map/advance/pallas_call | solution.py:83
  40.4 2.5 %collective-permute-start.5 = (f32[2,32,256]{2,1,0:T(8,128)S(1)}, f32[2,32,256]{2,1,0:T(8,128)S(1)}, u32[]{:S(2)}, u32[]{:S(2)}) collective-permute-start(f32[2,32,256]{2,1,0:T(8,128)S(1)} %get-tuple-element.81), channel_id=1, source_target_pairs={{4,8},{8,4},{12,16},{16,12},{20,24},{24,20},{28,0},{0,28},{5,9},{9... | collective-permute-start | bytes 196616 | tf_op jit(solution)/shard_map/ppermute | solution.py:37
  42.9 3.1 %full.6.refs_4_ = f32[1,3072]{1,0:T(1,128)S(1)} custom-call(f32[8,3072]{1,0:T(8,128)S(1)} %get-tuple-element.61.refs_0_, f32[64,128]{1,0:T(8,128)S(1)} %get-tuple-element.84.refs_1_, f32[32,128]{1,0:T(8,128)S(1)} %get-tuple-element.59.refs_1_.refs_2_, bf16[1152,128]{1,0:T(8,128)(2,1)S(1)} %get-tuple-element.54.refs_9_.refs_2_.refs_3_, ...), custom_call_target="tpu_custom_call" | custom-call | flops 4000000000 | bytes 10000000 | tf_op jit(solution)/shard_map/full/pallas_call | solution.py:83
  46.0 1.5 %collective-permute-done.5.refs_16_ = f32[2,32,256]{2,1,0:T(8,128)S(1)} collective-permute-done((f32[2,32,256]{2,1,0:T(8,128)S(1)}, f32[2,32,256]{2,1,0:T(8,128)S(1)}, u32[]{:S(2)}, u32[]{:S(2)}) %collective-permute-start.5) | collective-permute-done | bytes 65568 | tf_op jit(solution)/shard_map/ppermute | solution.py:37
  47.9 1.5 %advance.7 = (bf16[128,1024]{1,0:T(8,128)(2,1)S(1)}, f32[64,128]{1,0:T(8,128)S(1)}, f32[8,16,128]{2,1,0:T(8,128)}) custom-call(f32[1,256]{1,0:T(1,128)S(1)} %copy-done.3, f32[1,256]{1,0:T(1,128)S(1)} %copy-done.4, f32[2,32,256]{2,1,0:T(8,128)S(1)} %get-tuple-element.70.refs_2_, f32[2,32,256]{2,1,0:T(8,128)S(1)} %get-tuple-element.77.refs_3_, ...), custom_call_target="tpu_custom_call" | custom-call | flops 1000000000 | bytes 4000000 | tf_op jit(solution)/shard_map/advance/pallas_call | solution.py:83
  49.4 3.5 %all-to-all-start.1 = ((f32[8,16,128]{2,1,0:T(8,128)}), f32[8,16,128]{2,1,0:T(8,128)S(1)}, u32[]{:S(2)}, u32[]{:S(2)}) async-start(f32[8,16,128]{2,1,0:T(8,128)} %get-tuple-element.92), calls=%async_computation.1 | async-start | bytes 131072 | tf_op jit(solution)/shard_map/all_to_all | solution.py:641
  52.9 3.8 %full.7 = (f32[1,3072]{1,0:T(1,128)S(1)}, f32[32,3072]{1,0:T(8,128)}) custom-call(f32[8,3072]{1,0:T(8,128)S(1)} %get-tuple-element.61.refs_0_, f32[64,128]{1,0:T(8,128)S(1)} %get-tuple-element.83.refs_1_, f32[32,128]{1,0:T(8,128)S(1)} %get-tuple-element.59.refs_1_.refs_2_, bf16[1152,128]{1,0:T(8,128)(2,1)S(1)} %get-tuple-element.54.refs_9_.refs_2_.refs_3_, ...), custom_call_target="tpu_custom_call" | custom-call | flops 4000000000 | bytes 10000000 | tf_op jit(solution)/shard_map/full/pallas_call | solution.py:83
  56.8 1.6 %collective-permute-start.8 = (f32[1,3072]{1,0:T(1,128)S(1)}, f32[1,3072]{1,0:T(1,128)S(1)}, u32[]{:S(2)}, u32[]{:S(2)}) collective-permute-start(f32[1,3072]{1,0:T(1,128)S(1)} %get-tuple-element.91.refs_0_), channel_id=1, source_target_pairs={{0,2},{1,3},{2,0},{3,1},{4,6},{5,7},{6,4},{7,5},{8,10},{9,11},{10,... | collective-permute-start | bytes 36872 | tf_op jit(solution)/shard_map/ppermute | solution.py:676
  58.7 1.3 %collective-permute-done.9.refs_3_ = f32[1,3072]{1,0:T(1,128)S(1)} collective-permute-done((f32[1,3072]{1,0:T(1,128)S(1)}, f32[1,3072]{1,0:T(1,128)S(1)}, u32[]{:S(2)}, u32[]{:S(2)}) %collective-permute-start.9) | collective-permute-done | bytes 12320 | tf_op jit(solution)/shard_map/ppermute | solution.py:676
  60.6 0.8 %finish.1 = (f32[1,3072]{1,0:T(1,128)}, f32[32,128]{1,0:T(8,128)}) custom-call(f32[1,3072]{1,0:T(1,128)S(1)} %get-tuple-element.91.refs_0_, f32[1,3072]{1,0:T(1,128)S(1)} %collective-permute-done.7.refs_1_, f32[1,3072]{1,0:T(1,128)S(1)} %collective-permute-done.8.refs_2_, f32[1,3072]{1,0:T(1,128)S(1)} %collective-permute-done.9.refs_3_, ...), custom_call_target="tpu_custom_call" | custom-call | flops 1000000000 | bytes 4000000 | tf_op jit(solution)/shard_map/finish/pallas_call | solution.py:83
  (33 shorter events, 2.2 us)
Async XLA Ops:
  2.7 17.2 %all-to-all-start = ((f32[8,40,128]{2,1,0:T(8,128)}), f32[8,40,128]{2,1,0:T(8,128)S(1)}, u32[]{:S(2)}, u32[]{:S(2)}) async-start(f32[8,40,128]{2,1,0:T(8,128)} %get-tuple-element.55), calls=%async_computation | async-start | bytes 327680 | tf_op jit(solution)/shard_map/all_to_all | solution.py:538
  10.0 9.9 %collective-permute-start = (f32[2,32,256]{2,1,0:T(8,128)}, f32[2,32,256]{2,1,0:T(8,128)S(1)}, u32[]{:S(2)}, u32[]{:S(2)}) collective-permute-start(f32[2,32,256]{2,1,0:T(8,128)} %get-tuple-element.51.refs_10_), channel_id=1, source_target_pairs={{0,4},{4,8},{8,12},{12,16},{16,20},{20,24},{24,28},{28,0},{1,5},{5... | collective-permute-start | bytes 196616 | tf_op jit(solution)/shard_map/ppermute | solution.py:28
  12.0 1.4 %copy-start.6 = (f32[24,128,128]{2,1,0:T(8,128)S(1)}, f32[24,128,128]{2,1,0:T(8,128)}, u32[]{:S(2)}) copy-start(f32[24,128,128]{2,1,0:T(8,128)} %refs_6_.9) | copy-start | bytes 4718596
  13.4 0.9 %copy-start.9 = (f32[8,3072]{1,0:T(8,128)S(1)}, f32[8,3072]{1,0:T(8,128)}, u32[]{:S(2)}) copy-start(f32[8,3072]{1,0:T(8,128)} %get-tuple-element.49.refs_0_.refs_3_) | copy-start | bytes 294916
  14.3 5.6 %copy-start = (f32[1,6,32,256]{3,2,1,0:T(8,128)S(1)}, f32[1,6,32,256]{3,2,1,0:T(8,128)}, u32[]{:S(2)}) copy-start(f32[1,6,32,256]{3,2,1,0:T(8,128)} %refs_9_.3) | copy-start | bytes 589828
  14.3 5.6 %copy-start.1 = (f32[1,6,32,256]{3,2,1,0:T(8,128)S(1)}, f32[1,6,32,256]{3,2,1,0:T(8,128)}, u32[]{:S(2)}) copy-start(f32[1,6,32,256]{3,2,1,0:T(8,128)} %refs_8_.3) | copy-start | bytes 589828
  14.3 5.7 %copy-start.3 = (f32[1,256]{1,0:T(1,128)S(1)}, f32[1,256]{1,0:T(1,128)}, u32[]{:S(2)}) copy-start(f32[1,256]{1,0:T(1,128)} %refs_0_.9) | copy-start | bytes 3076
  14.3 5.7 %copy-start.4 = (f32[1,256]{1,0:T(1,128)S(1)}, f32[1,256]{1,0:T(1,128)}, u32[]{:S(2)}) copy-start(f32[1,256]{1,0:T(1,128)} %refs_1_.11) | copy-start | bytes 3076
  14.3 5.7 %copy-start.5 = (s32[1,256]{1,0:T(1,128)S(1)}, s32[1,256]{1,0:T(1,128)}, u32[]{:S(2)}) copy-start(s32[1,256]{1,0:T(1,128)} %refs_6_.6) | copy-start | bytes 3076
  19.9 5.5 %copy-start.7 = (f32[24,128,128]{2,1,0:T(8,128)S(1)}, f32[24,128,128]{2,1,0:T(8,128)}, u32[]{:S(2)}) copy-start(f32[24,128,128]{2,1,0:T(8,128)} %refs_6_.9) | copy-start | bytes 4718596
  19.9 5.5 %copy-start.10 = (f32[8,3072]{1,0:T(8,128)S(1)}, f32[8,3072]{1,0:T(8,128)}, u32[]{:S(2)}) copy-start(f32[8,3072]{1,0:T(8,128)} %get-tuple-element.49.refs_0_.refs_3_) | copy-start | bytes 294916
  22.4 7.1 %collective-permute-start.1 = (f32[2,32,256]{2,1,0:T(8,128)S(1)}, f32[2,32,256]{2,1,0:T(8,128)S(1)}, u32[]{:S(2)}, u32[]{:S(2)}) collective-permute-start(f32[2,32,256]{2,1,0:T(8,128)S(1)} %get-tuple-element.68), channel_id=1, source_target_pairs={{4,8},{8,4},{12,16},{16,12},{20,24},{24,20},{28,0},{0,28},{5,9},{9... | collective-permute-start | bytes 196616 | tf_op jit(solution)/shard_map/ppermute | solution.py:37
  25.2 4.9 %collective-permute-start.2 = (f32[2,32,256]{2,1,0:T(8,128)S(1)}, f32[2,32,256]{2,1,0:T(8,128)S(1)}, u32[]{:S(2)}, u32[]{:S(2)}) collective-permute-start(f32[2,32,256]{2,1,0:T(8,128)S(1)} %get-tuple-element.69), channel_id=1, source_target_pairs={{0,4},{4,0},{8,12},{12,8},{16,20},{20,16},{24,28},{28,24},{1,5},{5... | collective-permute-start | bytes 196616 | tf_op jit(solution)/shard_map/ppermute | solution.py:37
  25.4 4.7 %copy-start.2 = (f32[2,32,256]{2,1,0:T(8,128)S(1)}, f32[2,32,256]{2,1,0:T(8,128)}, u32[]{:S(2)}) copy-start(f32[2,32,256]{2,1,0:T(8,128)} %get-tuple-element.51.refs_10_) | copy-start | bytes 196612
  31.3 7.1 %collective-permute-start.3 = (f32[2,32,256]{2,1,0:T(8,128)S(1)}, f32[2,32,256]{2,1,0:T(8,128)S(1)}, u32[]{:S(2)}, u32[]{:S(2)}) collective-permute-start(f32[2,32,256]{2,1,0:T(8,128)S(1)} %get-tuple-element.75), channel_id=1, source_target_pairs={{4,8},{8,4},{12,16},{16,12},{20,24},{24,20},{28,0},{0,28},{5,9},{9... | collective-permute-start | bytes 196616 | tf_op jit(solution)/shard_map/ppermute | solution.py:37
  33.6 5.0 %collective-permute-start.4 = (f32[2,32,256]{2,1,0:T(8,128)S(1)}, f32[2,32,256]{2,1,0:T(8,128)S(1)}, u32[]{:S(2)}, u32[]{:S(2)}) collective-permute-start(f32[2,32,256]{2,1,0:T(8,128)S(1)} %get-tuple-element.76), channel_id=1, source_target_pairs={{0,4},{4,0},{8,12},{12,8},{16,20},{20,16},{24,28},{28,24},{1,5},{5... | collective-permute-start | bytes 196616 | tf_op jit(solution)/shard_map/ppermute | solution.py:37
  40.4 7.1 %collective-permute-start.5 = (f32[2,32,256]{2,1,0:T(8,128)S(1)}, f32[2,32,256]{2,1,0:T(8,128)S(1)}, u32[]{:S(2)}, u32[]{:S(2)}) collective-permute-start(f32[2,32,256]{2,1,0:T(8,128)S(1)} %get-tuple-element.81), channel_id=1, source_target_pairs={{4,8},{8,4},{12,16},{16,12},{20,24},{24,20},{28,0},{0,28},{5,9},{9... | collective-permute-start | bytes 196616 | tf_op jit(solution)/shard_map/ppermute | solution.py:37
  42.9 5.0 %collective-permute-start.6 = (f32[2,32,256]{2,1,0:T(8,128)S(1)}, f32[2,32,256]{2,1,0:T(8,128)S(1)}, u32[]{:S(2)}, u32[]{:S(2)}) collective-permute-start(f32[2,32,256]{2,1,0:T(8,128)S(1)} %get-tuple-element.82), channel_id=1, source_target_pairs={{0,4},{4,0},{8,12},{12,8},{16,20},{20,16},{24,28},{28,24},{1,5},{5... | collective-permute-start | bytes 196616 | tf_op jit(solution)/shard_map/ppermute | solution.py:37
  49.4 11.2 %all-to-all-start.1 = ((f32[8,16,128]{2,1,0:T(8,128)}), f32[8,16,128]{2,1,0:T(8,128)S(1)}, u32[]{:S(2)}, u32[]{:S(2)}) async-start(f32[8,16,128]{2,1,0:T(8,128)} %get-tuple-element.92), calls=%async_computation.1 | async-start | bytes 131072 | tf_op jit(solution)/shard_map/all_to_all | solution.py:641
  52.9 7.7 %copy-start.8 = (s32[1,128]{1,0:T(1,128)S(1)}, s32[1,128]{1,0:T(1,128)}, u32[]{:S(2)}) copy-start(s32[1,128]{1,0:T(1,128)} %refs_5_.7) | copy-start | bytes 1540
  56.7 3.3 %collective-permute-start.9 = (f32[1,3072]{1,0:T(1,128)S(1)}, f32[1,3072]{1,0:T(1,128)S(1)}, u32[]{:S(2)}, u32[]{:S(2)}) collective-permute-start(f32[1,3072]{1,0:T(1,128)S(1)} %get-tuple-element.91.refs_0_), channel_id=1, source_target_pairs={{0,3},{1,2},{2,1},{3,0},{4,7},{5,6},{6,5},{7,4},{8,11},{9,10},{10,... | collective-permute-start | bytes 36872 | tf_op jit(solution)/shard_map/ppermute | solution.py:676
  56.8 3.8 %collective-permute-start.8 = (f32[1,3072]{1,0:T(1,128)S(1)}, f32[1,3072]{1,0:T(1,128)S(1)}, u32[]{:S(2)}, u32[]{:S(2)}) collective-permute-start(f32[1,3072]{1,0:T(1,128)S(1)} %get-tuple-element.91.refs_0_), channel_id=1, source_target_pairs={{0,2},{1,3},{2,0},{3,1},{4,6},{5,7},{6,4},{7,5},{8,10},{9,11},{10,... | collective-permute-start | bytes 36872 | tf_op jit(solution)/shard_map/ppermute | solution.py:676
  58.4 2.2 %collective-permute-start.7 = (f32[1,3072]{1,0:T(1,128)S(1)}, f32[1,3072]{1,0:T(1,128)S(1)}, u32[]{:S(2)}, u32[]{:S(2)}) collective-permute-start(f32[1,3072]{1,0:T(1,128)S(1)} %get-tuple-element.91.refs_0_), channel_id=1, source_target_pairs={{0,1},{1,0},{2,3},{3,2},{4,5},{5,4},{6,7},{7,6},{8,9},{9,8},{10,11... | collective-permute-start | bytes 36872 | tf_op jit(solution)/shard_map/ppermute | solution.py:676

commit v3 on v2

--- a/solution.py
+++ b/solution.py
@@ -11,9 +11,8 @@
 STEPS = 8
 DMIN = 2
 LANES = 128
-VMEM = 67043328
-ROOM = 30000 << 10
 WIDE = 4
+PAIR = "pair"
 OMEGA = 0.01884955592153876
 EPS = 1e-06
 F32 = jnp.float32
@@ -26,6 +25,11 @@
     count = lax.axis_size(axis)
     pairs = [(source, (source + steps) % count) for source in range(count)]
     return lax.ppermute(value, axis, pairs)
+
+
+def mirrored(value, axis, offset):
+    count = lax.axis_size(axis)
+    return lax.ppermute(value, axis, [(source, source ^ offset) for source in range(count)])
 
 
 def swapped(value, axis, first):
@@ -37,16 +41,30 @@
     return lax.ppermute(value, axis, pairs)
 
 
-def call(body, name, ins, outs, scratch=(), hbm=None, hbm_outs=None, limit=20 << 20, cost=None):
+def call(
+    body,
+    name,
+    ins,
+    outs,
+    scratch=(),
+    hbm=None,
+    hbm_outs=None,
+    relays=None,
+    scalar=(),
+    limit=20 << 20,
+    cost=None,
+):
     leaves, tree = jax.tree.flatten(ins)
     far, far_outs = dict(hbm or {}), dict(hbm_outs or {})
-    names = [list(far), list(outs), list(far_outs)]
+    far = {key: pltpu.with_memory_space_constraint(far[key], pltpu.HBM) for key in far}
+    relays = dict(relays or {})
+    names = [list(far), list(outs), list(far_outs), list(relays)]
     sizes = [len(leaves)] + [len(group) for group in names] + [len(far), len(far_outs)]
     ends = [sum(sizes[:k]) for k in range(len(sizes) + 1)]
-    count = len(far) + len(far_outs)
+    count = len(far) + len(far_outs) + len(relays)
 
     def kernel(*refs):
-        near, sources, near_outs, targets, held, made = [
+        near, sources, near_outs, targets, relayed, held, made = [
             refs[ends[k] : ends[k + 1]] for k in range(len(sizes))
         ]
         rest = refs[ends[-1] :]
@@ -60,6 +78,10 @@
                 leaving[key] = pltpu.make_async_copy(made[k], targets[k], sems.at[len(far) + k])
         i = Space(**jax.tree.unflatten(tree, near), **dict(zip(far, held)))
         o = Space(**dict(zip(outs, near_outs)), **dict(zip(far_outs, made)))
+        for k, key in enumerate(relays):
+            copy = pltpu.make_async_copy(getattr(i, key), relayed[k], sems.at[count - 1 - k])
+            copy.start()
+            pending.append(copy)
 
         def flush(key):
             pending.append(leaving.pop(key))
@@ -73,11 +95,14 @@
         for copy in pending:
             copy.wait()
 
-    buffers = [pltpu.VMEM(value.shape, value.dtype) for value in far.values()]
+    buffers = [
+        (pltpu.SMEM if key in scalar else pltpu.VMEM)(value.shape, value.dtype)
+        for key, value in far.items()
+    ]
     buffers += [pltpu.VMEM(*shape) for shape in far_outs.values()]
     if count:
         buffers.append(pltpu.SemaphoreType.DMA((count,)))
-    every = list(outs.values()) + list(far_outs.values())
+    every = list(outs.values()) + list(far_outs.values()) + list(relays.values())
     near_spec, far_spec = (pl.BlockSpec(memory_space=space) for space in (pltpu.VMEM, pltpu.HBM))
     flops, moved = cost or (1e9, 4e6)
     results = pl.pallas_call(
@@ -85,14 +110,14 @@
         name=name,
         out_shape=[jax.ShapeDtypeStruct(*shape) for shape in every],
         in_specs=[near_spec] * len(leaves) + [far_spec] * len(far),
-        out_specs=[near_spec] * len(outs) + [far_spec] * len(far_outs),
+        out_specs=[near_spec] * len(outs) + [far_spec] * (len(far_outs) + len(relays)),
         scratch_shapes=buffers + list(scratch),
         compiler_params=pltpu.CompilerParams(vmem_limit_bytes=limit),
         cost_estimate=pl.CostEstimate(
             flops=int(flops), bytes_accessed=int(moved), transcendentals=0
         ),
     )(*leaves, *far.values())
-    return Space(**dict(zip(names[1] + names[2], results)))
+    return Space(**dict(zip(names[1] + names[2] + names[3], results)))
 
 
 def iota(shape, dim):
@@ -101,10 +126,6 @@
 
 def onehot(mask):
     return jnp.where(mask, 1.0, 0.0).astype(BF16)
-
-
-def owned(mark, k):
-    return jnp.where(mark == jnp.asarray(k, BF16), jnp.asarray(1, BF16), jnp.asarray(0, BF16))
 
 
 def owner_of(mark):
@@ -150,17 +171,18 @@
 
 
 def start_body(sizes, i, o):
-    regions, cap, half, scen, group, maxd, lines, nreg = sizes
+    regions, cap, half, scen, group, maxd = sizes
     packed = 2 * cap == LANES
     i.ready("slots", "par", "state")
     slots = i.slots[...]
     rows = iota((regions * 2 * cap, group), 0)
+    away = jnp.bitwise_xor(slots // cap, lax.axis_index("region"))
     if packed:
-        target = (slots // cap) * (2 * cap) + slots % cap
+        target = away * (2 * cap) + slots % cap
         moved = target + cap
     else:
-        target = slots
-        moved = slots + regions * cap
+        target = away * cap + slots % cap
+        moved = target + regions * cap
     left, right = onehot(rows == target), onehot(rows == moved)
     pad = jnp.zeros((half - scen - 6, group), F32)
     upper = jnp.concatenate([i.state[0], i.par[...], pad], axis=0)
@@ -171,32 +193,21 @@
         value = both[:half] + both[half : 2 * half] + both[2 * half :]
         buffer = value if buffer is None else buffer + value
     if packed:
-        for region in range(regions):
-            o.send[region] = buffer[:, region * LANES : (region + 1) * LANES]
+        for index in range(regions):
+            slot = buffer[:, index * LANES : (index + 1) * LANES]
+            (o.odd if index % 2 else o.even)[index // 2] = slot
     else:
         o.send[...] = buffer
-    o.flush("send")
     i.ready("hist", "delay")
     delays = i.delay[...]
     for step in range(2):
         o.into[step] = pick(lambda t: i.hist[0, t + maxd], delays, step, maxd)
-    o.flush("into")
-    i.ready("end_a", "end_b", "conv", "fault_node", "fault_step", "fault_cond", "amp", "phase")
-    pack = o.pack
-    pack[0:1, :] = i.amp[...]
-    pack[1:2, :] = i.phase[...]
-    pack[2:3, 0:scen] = i.fault_step[...].astype(F32)
-    pack[3:4, 0:scen] = i.fault_cond[...]
-    points = 2 * lines + regions * cap
-    pack[4:5, 0 : points + LANES] = jnp.full((1, points + LANES), -1.0, F32)
-    pack[4:5, 0:lines] = i.end_a[...].astype(F32)
-    pack[4:5, lines : 2 * lines] = i.end_b[...].astype(F32)
-    for index in range(regions):
-        first = 2 * lines + index * cap
-        pack[4:5, first : first + cap] = i.conv[0, index : index + 1, :].astype(F32)
-    fault = i.fault_node[...] - lax.axis_index("region") * nreg
-    fault = jnp.where((fault >= 0) & (fault < nreg), fault, -1)
-    pack[4:5, points : points + scen] = fault.astype(F32)
+
+
+def pair_body(count, i, o):
+    for k in range(count):
+        target = getattr(o, PAIR + str(k))
+        target[0], target[1] = i.even[k], i.odd[k]
 
 
 def sources(amp, phase):
@@ -204,26 +215,47 @@
     return amp * jnp.cos(OMEGA * instant + phase)
 
 
-def rows_body(sizes, i, o, place, zcat, source_rows):
+def rows_body(sizes, i, o, taken, source_rows):
     nreg, nblk, lines, regions, cap, scen = sizes
     blk = LANES
     width = regions * cap
     points = 2 * lines + width
     whole = points + blk
-    whole_row = i.pack[4:5, 0:whole]
-    row = whole_row.astype(jnp.int32)
-    o.row[...] = row
+    here = lax.axis_index("region")
+    groups = [jnp.bitwise_xor(here, away) for away in range(regions)]
+    i.ready("end_a", "end_b", "conv", "fault_node")
+    o.row[...] = jnp.full((1, whole), -1, jnp.int32)
+    o.row[:, 0:lines] = i.end_a[...]
+    o.row[:, lines : 2 * lines] = i.end_b[...]
+    for away in range(regions):
+        first = 2 * lines + away * cap
+        o.row[:, first : first + cap] = i.conv[0, pl.ds(groups[away], 1), :]
+    fault = i.fault_node[...] - here * nreg
+    o.row[:, points : points + scen] = jnp.where((fault >= 0) & (fault < nreg), fault, -1)
+    row = o.row[...]
+    whole_row = row.astype(F32)
     column = jnp.transpose(jnp.broadcast_to(whole_row, (blk, whole))).astype(jnp.int32)
-    here = (column & 127) == iota((whole, blk), 1)
-    o.mark[...] = jnp.where(here, (column >> 7).astype(F32), -1.0).astype(BF16)
-    for k in range(nblk):
-        place[:, k * blk : (k + 1) * blk] = owned(o.mark[...], k)
-    i.ready("inv")
-    z_high, z_low = split2(i.inv[...].reshape(nreg, blk))
-    zcat[:, 0:blk] = z_high
-    zcat[:, blk:] = z_low
-    o.rows[...] = dot(place[...], zcat[...]).astype(BF16)
-    source = sources(i.pack[0:1, :], i.pack[1:2, :])
+    inside = (column & 127) == iota((whole, blk), 1)
+    o.mark[...] = jnp.where(inside, (column >> 7).astype(F32), -1.0).astype(BF16)
+    o.fault_mark[...] = o.mark[points : points + scen, :].astype(F32)
+    i.ready("list_a", "list_b", "list_conv", "list_fault", "inv")
+    for p in range(points + scen):
+        if p < lines:
+            node = i.list_a[0, p]
+        elif p < 2 * lines:
+            node = i.list_b[0, p - lines]
+        elif p < points:
+            away, place = divmod(p - 2 * lines, cap)
+            node = jnp.maximum(i.list_conv[0, groups[away], place], 0)
+        else:
+            node = jnp.clip(i.list_fault[0, p - points] - here * nreg, 0, nreg - 1)
+        taken[p : p + 1, :] = i.inv[pl.ds(node, 1), :]
+    taken[points + scen :, :] = jnp.zeros((blk - scen, blk), F32)
+    high, low = split2(jnp.where(column >= 0, taken[...], 0.0))
+    o.rows[:, :blk] = high
+    o.rows[:, blk:] = low
+    i.ready("amp", "phase", "fault_step", "fault_cond")
+    source = sources(i.amp[...], i.phase[...])
     for k in range(nblk):
         source_rows[k * STEPS : (k + 1) * STEPS, :] = source[:, k * blk : (k + 1) * blk]
     spread = product3(source_rows[...], o.rows[:, :blk], o.rows[:, blk:], NT)
@@ -244,8 +276,8 @@
         axis=1,
         keepdims=True,
     )
-    cond = as_column(i.pack[3:4, 0:scen], scen)
-    closes = as_column(i.pack[2:3, 0:scen], scen)
+    cond = as_column(i.fault_cond[...], scen)
+    closes = as_column(i.fault_step[...].astype(F32), scen)
     ratio = cond / (1.0 + cond * self_imp)
     o.fault_ratio[...] = jnp.where(
         closes <= iota((scen, blk), 1).astype(F32), jnp.broadcast_to(ratio, (scen, blk)), 0.0
@@ -316,8 +348,8 @@
         for row in range(6):
             pieces = []
             for j in range(width // LANES):
-                one = i.recv[2 * j][scen + row : scen + row + 1, :]
-                two = i.recv[2 * j + 1][scen + row : scen + row + 1, :]
+                one = i.recv[j][0, scen + row : scen + row + 1, :]
+                two = i.recv[j][1, scen + row : scen + row + 1, :]
                 pieces.append(jnp.where(low, one, pltpu.roll(two, cap, 1)))
             params.append(jnp.concatenate(pieces, axis=1))
     else:
@@ -333,7 +365,7 @@
         if packed:
             ups, downs = [], []
             for j in range(width // LANES):
-                one, two = i.recv[2 * j][:scen], i.recv[2 * j + 1][:scen]
+                one, two = i.recv[j][0, :scen], i.recv[j][1, :scen]
                 ups.append(jnp.where(low, one, pltpu.roll(two, cap, 1)))
                 downs.append(jnp.where(low, pltpu.roll(one, cap, 1), two))
             first, second = jnp.concatenate(ups, axis=1), jnp.concatenate(downs, axis=1)
@@ -402,11 +434,16 @@
         o.current[...] = current
     else:
         half = scen // 2
+        region = lax.axis_index("region")
         for j in range(width // LANES):
             mine = current[:, j * LANES : (j + 1) * LANES]
             top, bottom = mine[:half], mine[half:]
-            o.current[2 * j] = jnp.where(low, top, pltpu.roll(bottom, cap, 1))
-            o.current[2 * j + 1] = jnp.where(low, pltpu.roll(top, cap, 1), bottom)
+            pieces = (
+                jnp.where(low, top, pltpu.roll(bottom, cap, 1)),
+                jnp.where(low, pltpu.roll(top, cap, 1), bottom),
+            )
+            for k in range(2):
+                o.current[jnp.bitwise_xor(region, 2 * j + k)] = pieces[k]
 
 
 def full_body(sizes, pair, i, o):
@@ -414,27 +451,38 @@
     blk = LANES
     t0 = 2 * pair
     fault_z = i.fault_z[...]
-    fault_blk = owner_of(i.mark[points : points + scen, :])
+    fault_blk = owner_of(i.fault_mark[...])
     x = i.x[...]
     coef = i.coef[...]
-    i.ready("inv")
     if pair:
-        all_base = i.base
-    else:
-        all_base = o.base
-        source = sources(i.pack[0:1, :], i.pack[1:2, :])
+        known = i
+    else:
+        known = o
+        mark = i.mark[:points].astype(F32)
+        node = jnp.where(mark >= 0.0, mark * blk + iota((points, blk), 1).astype(F32), -1.0)
+        node = jnp.max(node, axis=1, keepdims=True)
+        o.column[...] = jnp.broadcast_to(node, (points, blk)).astype(jnp.int32)
+        i.ready("inv", "amp", "phase")
         for k in range(nblk):
             here = slice(k * blk, (k + 1) * blk)
-            o.base[:, here] = product3(source[:, here], *split2(i.inv[k]))
+            o.zcat[here, :blk], o.zcat[here, blk:] = split2(i.inv[k])
+        source = sources(i.amp[...], i.phase[...])
+        for k in range(nblk):
+            here = slice(k * blk, (k + 1) * blk)
+            o.base[:, here] = product3(source[:, here], o.zcat[here, :blk], o.zcat[here, blk:])
+    lane = iota((points, blk), 1)
     for k in range(0, nblk, WIDE):
-        mine = jnp.concatenate([owned(i.mark[:points], k + j) for j in range(WIDE)], axis=1)
+        mine = jnp.concatenate(
+            [onehot(known.column[...] == lane + (k + j) * blk) for j in range(WIDE)], axis=1
+        )
         both = dot(x, mine)
         inject = both[: 2 * scen] + both[2 * scen :]
         for j in range(WIDE):
             here = slice((k + j) * blk, (k + j + 1) * blk)
-            volts = product3(inject[:, j * blk : (j + 1) * blk], *split2(i.inv[k + j]))
+            z = known.zcat[here, :]
+            volts = product3(inject[:, j * blk : (j + 1) * blk], z[:, :blk], z[:, blk:])
             base = [
-                jnp.broadcast_to(all_base[t0 + m : t0 + m + 1, here], (scen, blk))
+                jnp.broadcast_to(known.base[t0 + m : t0 + m + 1, here], (scen, blk))
                 for m in range(2)
             ]
             zcol = jnp.where(fault_blk == k + j, fault_z, 0.0)
@@ -448,12 +496,15 @@
                 o.volts[:, here] = volts[scen:]
 
 
-def finish_body(sizes, i, o):
-    regions, cap, scen, group, count, packed = sizes
+def rms_body(scen, count, i, o):
     parts = [i.parts[k][...] for k in range(count)]
     while len(parts) > 1:
         parts = [parts[k] + parts[k + 1] for k in range(0, len(parts), 2)]
     o.rms[...] = jnp.sqrt(parts[0] / (scen * count * STEPS) + EPS)
+
+
+def settle_body(sizes, i, o):
+    regions, cap, scen, group, packed = sizes
     slots = i.slots[...]
     if packed:
         half = scen // 2
@@ -507,68 +558,85 @@
     packed = 2 * cap == LANES
     half = scen + 8
 
-    send_shape = (regions, half, LANES) if packed else (half, regions * 2 * cap)
+    amp, phase = src_amp.reshape(1, nreg), src_phase.reshape(1, nreg)
+    if packed:
+        slot_outs = dict.fromkeys(("even", "odd"), ((regions // 2, half, LANES), F32))
+    else:
+        slot_outs = dict(send=((half, regions * 2 * cap), F32))
     head = call(
-        functools.partial(start_body, (regions, cap, half, scen, group, maxd, lines, nreg)),
+        functools.partial(start_body, (regions, cap, half, scen, group, maxd)),
         "start",
         {},
-        {},
-        hbm_outs=dict(
-            send=(send_shape, F32), into=((2, scen, lines), F32), pack=((8, nreg), F32)
+        dict(into=((2, scen, lines), F32), **slot_outs),
+        hbm=dict(
+            slots=recv_slot, par=conv_par, state=conv_state, hist=hist_ua, delay=line_delay
         ),
-        limit=VMEM,
-        hbm=dict(
-            slots=recv_slot,
-            par=conv_par,
-            state=conv_state,
-            hist=hist_ua,
-            delay=line_delay,
-            end_a=line_a,
-            end_b=line_b,
-            conv=send_node,
-            amp=src_amp.reshape(1, nreg),
-            phase=src_phase.reshape(1, nreg),
-            fault_node=fault_node.reshape(1, scen),
-            fault_step=fault_step.reshape(1, scen),
-            fault_cond=fault_cond.reshape(1, scen),
-        ),
-    )
-    send = head.send
+    )
     if packed:
-        recv = lax.all_to_all(send, "region", split_axis=0, concat_axis=0, tiled=True)
-    else:
-        send = send.reshape(half, 2, regions, cap).transpose(2, 1, 0, 3)
-        recv = lax.all_to_all(send, "region", split_axis=0, concat_axis=0, tiled=True)
-        recv = recv.transpose(1, 2, 0, 3).reshape(2, half, width)
+        even, odd = head.even, head.odd
+    else:
+        slots = head.send.reshape(half, 2, regions, cap).transpose(2, 1, 0, 3)
+        even, odd = slots[0::2], slots[1::2]
+    odd = mirrored(odd, "region", 1)
     into = head.into
     far_in = shifted(into, "region", 1)
+    if packed:
+        shape = ((2, half, LANES), F32)
+        couples = call(
+            functools.partial(pair_body, regions // 2),
+            "couple",
+            dict(even=even, odd=odd),
+            {PAIR + str(k): shape for k in range(regions // 2)},
+        )
+        couples = [getattr(couples, PAIR + str(k)) for k in range(regions // 2)]
+    else:
+        couples = [jnp.stack([even[k], odd[k]]) for k in range(regions // 2)]
+    recv = couples[:1]
+    for k in range(1, regions // 2):
+        recv.append(mirrored(couples[k], "region", 2 * k))
+    if not packed:
+        recv = jnp.concatenate(recv, axis=0).transpose(1, 2, 0, 3).reshape(2, half, width)
 
     whole = points + blk
     model = call(
         functools.partial(rows_body, (nreg, nblk, lines, regions, cap, scen)),
         "rows",
-        dict(pack=head.pack),
+        {},
         dict(
             row=((1, whole), jnp.int32),
             mark=((whole, blk), BF16),
+            fault_mark=((scen, blk), F32),
             rows=((whole, 2 * blk), BF16),
             base_p=((STEPS, points), F32),
             fault_z=((scen, blk), F32),
             fault_base=((scen, blk), F32),
             fault_ratio=((scen, blk), F32),
         ),
-        hbm=dict(inv=inv_blocks),
+        hbm=dict(
+            end_a=line_a,
+            end_b=line_b,
+            conv=send_node,
+            fault_node=fault_node.reshape(1, scen),
+            list_a=line_a,
+            list_b=line_b,
+            list_conv=send_node,
+            list_fault=fault_node.reshape(1, scen),
+            inv=inv_blocks.reshape(nreg, blk),
+            amp=amp,
+            phase=phase,
+            fault_step=fault_step.reshape(1, scen),
+            fault_cond=fault_cond.reshape(1, scen),
+        ),
+        scalar=("list_a", "list_b", "list_conv", "list_fault"),
         scratch=(
-            pltpu.VMEM((whole, nreg), BF16),
-            pltpu.VMEM((nreg, 2 * blk), BF16),
+            pltpu.VMEM((whole, blk), F32),
             pltpu.VMEM((STEPS * nblk, blk), F32),
         ),
-        limit=VMEM - ROOM,
         cost=(4e9, 2e7),
     )
     wave = ((2, scen, lines), F32)
     mades, backs, carry = {}, {}, {}
-    squares = swap_near = swap_far = sent = base = None
+    squares = swap_near = swap_far = sent = shared = None
     for pair in range(STEPS // 2):
         t0 = 2 * pair
         final = t0 + 2 >= STEPS
@@ -640,47 +708,59 @@
             if packed:
                 returned = lax.all_to_all(current, "region", split_axis=0, concat_axis=0, tiled=True)
             else:
-                current = current.reshape(scen, regions, cap).transpose(1, 0, 2)
+                order = jnp.bitwise_xor(lax.axis_index("region"), jnp.arange(regions))
+                current = current.reshape(scen, regions, cap).transpose(1, 0, 2)[order]
                 returned = lax.all_to_all(current, "region", split_axis=0, concat_axis=0, tiled=True)
                 returned = returned.transpose(1, 0, 2).reshape(scen, width)
         ins = dict(
             x=made.x,
             coef=made.coef,
-            mark=model.mark,
+            fault_mark=model.fault_mark,
             fault_z=model.fault_z,
         )
         if pair:
-            ins.update(squares=squares, base=base)
+            ins.update(squares=squares, **shared)
         else:
-            ins.update(pack=head.pack)
+            ins.update(mark=model.mark)
         outs = dict(squares=((1, nreg), F32))
         if final:
             outs.update(volts=((scen, nreg), F32))
         if not pair:
-            outs.update(base=((STEPS, nreg), F32))
+            outs.update(
+                base=((STEPS, nreg), F32),
+                column=((points, blk), jnp.int32),
+                zcat=((nreg, 2 * blk), BF16),
+            )
         full = call(
             functools.partial(full_body, (nblk, points, scen), pair),
             "full",
             ins,
             outs,
-            hbm=dict(inv=inv_blocks),
+            hbm={} if pair else dict(inv=inv_blocks, amp=amp, phase=phase),
             cost=(4e9, 1e7),
         )
         squares = full.squares
         if not pair:
-            base = full.base
+            shared = dict(base=full.base, column=full.column, zcat=full.zcat)
 
     parts = [squares]
     for offset in range(1, count):
         pairs = [(source, source ^ offset) for source in range(count)]
         parts.append(lax.ppermute(squares, "scen", pairs))
+    settled = call(
+        functools.partial(settle_body, (regions, cap, scen, group, packed)),
+        "settle",
+        dict(slots=recv_slot, recv=returned, volts=full.volts),
+        dict(current=((scen, group), F32)),
+        relays=dict(volts=((scen, nreg), F32)),
+    )
     tail = call(
-        functools.partial(finish_body, (regions, cap, scen, group, count, packed)),
-        "finish",
-        dict(slots=recv_slot, recv=returned, parts=parts),
-        dict(rms=((1, nreg), F32), current=((scen, group), F32)),
-    )
-    return full.volts, tail.current, tail.rms.reshape(nreg)
+        functools.partial(rms_body, scen, count),
+        "rms",
+        dict(parts=parts),
+        dict(rms=((1, nreg), F32)),
+    )
+    return settled.volts, settled.current, tail.rms.reshape(nreg)
 
 
 def solution(mesh):

time: 61.8 us -> 60.3 us (0.976)
  waiting for transfers between devices: 6.5 us -> 10.3 us
  local copies, waits for them, and re-layouts: 2.34 us -> 0.03 us
  Pallas kernels: 29.2 us -> 27.5 us
  starting transfers between devices: 22.5 us -> 21.2 us
    ppermute x0 -> x4, starting transfers between devices: none -> 7.77 us  [mirrored(): lax.ppermute(value, axis, [(source, source ^ offset) for source in range(...]
    all_to_all x1 -> x0, starting transfers between devices: 7.29 us -> none  [per_device(): lax.all_to_all(send, 'region', split_axis=0, concat_axis=0, tiled=True)]
    ppermute x0 -> x4, waiting for transfers between devices: none -> 4.36 us  [mirrored(): lax.ppermute(value, axis, [(source, source ^ offset) for source in range(...]
    unnamed x22 -> x12, local copies, waits for them, and re-layouts: 2.34 us -> 0.03 us
    ppermute x1, starting transfers between devices: 2.02 us -> 0.07 us  [shifted(): return lax.ppermute(value, axis, pairs)]
    pallas_call x11 -> x13, Pallas kernels: 29.2 us -> 27.5 us  [call(): pl.pallas_call(kernel, name=name, out_shape=[jax.ShapeDtypeStruct(*shape)...]
  transfers between devices with their start and end apart: 12 -> 15, of which waited for: 8 -> 7; matrix products, arithmetic and copies ran while one was open for 0% -> 0% of each run, Pallas kernels for 32% -> 30%
where the time goes in v3:
time: 60.3 us; the launch traced here: 60 us
  Pallas kernels  27.5 us (46%)
  starting transfers between devices  21.2 us (35%)
  waiting for transfers between devices  10.3 us (17%)
  between operations  0.96 us (2%)
    pallas_call x13, Pallas kernels, call(): pl.pallas_call(kernel, name=name, out_shape=[jax.ShapeDtypeStruct(*shape)...  27.5 us
    ppermute x6, starting transfers between devices, swapped(): return lax.ppermute(value, axis, pairs)  8.14 us
    ppermute x4, starting transfers between devices, mirrored(): lax.ppermute(value, axis, [(source, source ^ offset) for source in range(...  7.77 us
    ppermute x4, waiting for transfers between devices, mirrored(): lax.ppermute(value, axis, [(source, source ^ offset) for source in range(...  4.36 us
    ppermute x6, waiting for transfers between devices, swapped(): return lax.ppermute(value, axis, pairs)  3.99 us
    all_to_all x1, starting transfers between devices, per_device(): lax.all_to_all(current, 'region', split_axis=0, concat_axis=0, tiled=True)  3.35 us
    ppermute x3, starting transfers between devices, per_device(): parts.append(lax.ppermute(squares, 'scen', pairs))  1.92 us
    ppermute x3, waiting for transfers between devices, per_device(): parts.append(lax.ppermute(squares, 'scen', pairs))  1.91 us
  transfers between devices with their start and end apart: 15, of which 7 were waited for; matrix products, arithmetic and copies ran while one was open for 0% of the time, Pallas kernels for 30%

profile of v3, /device:TPU:0, one launch (start us, length us, event | category | flops | bytes accessed | tf_op | source)
XLA Modules:
  0.0 60.0 jit_solution(4884668565727822424)
XLA Ops:
  0.6 1.2 %start.1 = (f32[2,32,256]{2,1,0:T(8,128)S(1)}, f32[4,40,128]{2,1,0:T(8,128)S(1)}, f32[4,40,128]{2,1,0:T(8,128)S(1)}) custom-call(s32[1,128]{1,0:T(1,128)} %refs_1_.13, f32[6,128]{1,0:T(8,128)} %refs_1_.8, f32[2,32,128]{2,1,0:T(8,128)} %refs_2_.3, f32[1,6,32,256]{3,2,1,0:T(8,128)} %refs_8_.3, s32[1,256]{1,0:T(1,128)} %refs_6_.3), custom_call_target="tpu_custom_call" | custom-call | flops 1000000000 | bytes 4000000 | tf_op jit(solution)/shard_map/start/pallas_call | solution.py:108
  1.9 3.0 %collective-permute-start.1 = (f32[4,40,128]{2,1,0:T(8,128)S(1)}, f32[4,40,128]{2,1,0:T(8,128)S(1)}, u32[]{:S(2)}, u32[]{:S(2)}) collective-permute-start(f32[4,40,128]{2,1,0:T(8,128)S(1)} %get-tuple-element.62), channel_id=1, source_target_pairs={{0,4},{4,0},{8,12},{12,8},{16,20},{20,16},{24,28},{28,24},{1,5},{5... | collective-permute-start | bytes 245768 | tf_op jit(solution)/shard_map/ppermute | solution.py:32
  5.0 2.4 %collective-permute-done.1.refs_1_ = f32[4,40,128]{2,1,0:T(8,128)S(1)} collective-permute-done((f32[4,40,128]{2,1,0:T(8,128)S(1)}, f32[4,40,128]{2,1,0:T(8,128)S(1)}, u32[]{:S(2)}, u32[]{:S(2)}) %collective-permute-start.1) | collective-permute-done | bytes 81952 | tf_op jit(solution)/shard_map/ppermute | solution.py:32
  7.4 2.1 %collective-permute-start.2 = (f32[2,40,128]{2,1,0:T(8,128)S(1)}, f32[2,40,128]{2,1,0:T(8,128)S(1)}, u32[]{:S(2)}, u32[]{:S(2)}) collective-permute-start(f32[2,40,128]{2,1,0:T(8,128)S(1)} %get-tuple-element.64), channel_id=1, source_target_pairs={{0,8},{4,12},{8,0},{12,4},{16,24},{20,28},{24,16},{28,20},{1,9},{5... | collective-permute-start | bytes 122888 | tf_op jit(solution)/shard_map/ppermute | solution.py:32
  9.5 2.6 %collective-permute-start.3 = (f32[2,40,128]{2,1,0:T(8,128)S(1)}, f32[2,40,128]{2,1,0:T(8,128)S(1)}, u32[]{:S(2)}, u32[]{:S(2)}) collective-permute-start(f32[2,40,128]{2,1,0:T(8,128)S(1)} %get-tuple-element.65), channel_id=1, source_target_pairs={{0,16},{4,20},{8,24},{12,28},{16,0},{20,4},{24,8},{28,12},{1,17},{... | collective-permute-start | bytes 122888 | tf_op jit(solution)/shard_map/ppermute | solution.py:32
  12.2 3.7 %rows.1 = (s32[1,1152]{1,0:T(1,128)S(1)}, bf16[1152,128]{1,0:T(8,128)(2,1)S(1)}, f32[32,128]{1,0:T(8,128)S(1)}, bf16[1152,256]{1,0:T(8,128)(2,1)S(1)}, f32[8,102...) custom-call(s32[1,256]{1,0:T(1,128)} %refs_4_.3, s32[1,256]{1,0:T(1,128)} %refs_5_.3, ...), custom_call_target="tpu_custom_call" | custom-call | flops 4000000000 | bytes 20000000 | tf_op jit(solution)/shard_map/rows/pallas_call | solution.py:108
  15.9 2.0 %collective-permute-done.4.refs_13_.refs_17_.refs_18_.refs_16_ = f32[2,40,128]{2,1,0:T(8,128)S(1)} collective-permute-done((f32[2,40,128]{2,1,0:T(8,128)S(1)}, f32[2,40,128]{2,1,0:T(8,128)S(1)}, u32[]{:S(2)}, u32[]{:S(2)}) %collective-permute-start.4) | collective-permute-done | bytes 40992 | tf_op jit(solution)/shard_map/ppermute | solution.py:32
  17.9 2.4 %advance.4 = (bf16[128,1024]{1,0:T(8,128)(2,1)S(1)}, f32[64,128]{1,0:T(8,128)S(1)}, f32[2,32,256]{2,1,0:T(8,128)S(1)}, f32[2,32,256]{2,1,0:T(8,128)S(1)}, f32[2,...) custom-call(f32[1,256]{1,0:T(1,128)S(1)} %copy-done.2, ...), custom_call_target="tpu_custom_call" | custom-call | flops 1000000000 | bytes 4000000 | tf_op jit(solution)/shard_map/advance/pallas_call | solution.py:108
  20.4 3.3 %collective-permute-start.5 = (f32[2,32,256]{2,1,0:T(8,128)S(1)}, f32[2,32,256]{2,1,0:T(8,128)S(1)}, u32[]{:S(2)}, u32[]{:S(2)}) collective-permute-start(f32[2,32,256]{2,1,0:T(8,128)S(1)} %get-tuple-element.75), channel_id=1, source_target_pairs={{4,8},{8,4},{12,16},{16,12},{20,24},{24,20},{28,0},{0,28},{5,9},{9... | collective-permute-start | bytes 196616 | tf_op jit(solution)/shard_map/ppermute | solution.py:41
  23.7 4.9 %full.4 = (f32[1,3072]{1,0:T(1,128)S(1)}, f32[8,3072]{1,0:T(8,128)S(1)}, s32[1024,128]{1,0:T(8,128)S(1)}, bf16[3072,256]{1,0:T(8,128)(2,1)S(1)}) custom-call(f32[64,128]{1,0:T(8,128)S(1)} %get-tuple-element.91.refs_0_, f32[32,128]{1,0:T(8,128)S(1)} %get-tuple-element.92.refs_1_.refs_3_, f32[32,128]{1,0:T(8,128)S(1)} %get-tuple-element.93.refs_2_.refs_4_, ...), custom_call_target="tpu_custom_call" | custom-call | flops 4000000000 | bytes 10000000 | tf_op jit(solution)/shard_map/full/pallas_call | solution.py:108
  28.6 1.2 %advance.5 = (bf16[128,1024]{1,0:T(8,128)(2,1)S(1)}, f32[64,128]{1,0:T(8,128)S(1)}, f32[2,32,256]{2,1,0:T(8,128)S(1)}, f32[2,32,256]{2,1,0:T(8,128)S(1)}, f32[2,...) custom-call(f32[1,256]{1,0:T(1,128)S(1)} %copy-done.2, ...), custom_call_target="tpu_custom_call" | custom-call | flops 1000000000 | bytes 4000000 | tf_op jit(solution)/shard_map/advance/pallas_call | solution.py:108
  29.8 2.1 %collective-permute-start.7 = (f32[2,32,256]{2,1,0:T(8,128)S(1)}, f32[2,32,256]{2,1,0:T(8,128)S(1)}, u32[]{:S(2)}, u32[]{:S(2)}) collective-permute-start(f32[2,32,256]{2,1,0:T(8,128)S(1)} %get-tuple-element.82), channel_id=1, source_target_pairs={{4,8},{8,4},{12,16},{16,12},{20,24},{24,20},{28,0},{0,28},{5,9},{9... | collective-permute-start | bytes 196616 | tf_op jit(solution)/shard_map/ppermute | solution.py:41
  32.0 2.9 %full.5.refs_5_ = f32[1,3072]{1,0:T(1,128)S(1)} custom-call(f32[8,3072]{1,0:T(8,128)S(1)} %get-tuple-element.95.refs_0_, f32[64,128]{1,0:T(8,128)S(1)} %get-tuple-element.99.refs_1_, s32[1024,128]{1,0:T(8,128)S(1)} %get-tuple-element.97.refs_2_, f32[32,128]{1,0:T(8,128)S(1)} %get-tuple-element.92.refs_1_.refs_3_, ...), custom_call_target="tpu_custom_call" | custom-call | flops 4000000000 | bytes 10000000 | tf_op jit(solution)/shard_map/full/pallas_call | solution.py:108
  34.8 2.0 %collective-permute-done.7.refs_21_ = f32[2,32,256]{2,1,0:T(8,128)S(1)} collective-permute-done((f32[2,32,256]{2,1,0:T(8,128)S(1)}, f32[2,32,256]{2,1,0:T(8,128)S(1)}, u32[]{:S(2)}, u32[]{:S(2)}) %collective-permute-start.7) | collective-permute-done | bytes 65568 | tf_op jit(solution)/shard_map/ppermute | solution.py:41
  36.8 1.8 %advance.6 = (bf16[128,1024]{1,0:T(8,128)(2,1)S(1)}, f32[64,128]{1,0:T(8,128)S(1)}, f32[2,32,256]{2,1,0:T(8,128)S(1)}, f32[2,32,256]{2,1,0:T(8,128)S(1)}, f32[2,...) custom-call(f32[1,256]{1,0:T(1,128)S(1)} %copy-done.2, ...), custom_call_target="tpu_custom_call" | custom-call | flops 1000000000 | bytes 4000000 | tf_op jit(solution)/shard_map/advance/pallas_call | solution.py:108
  38.6 2.7 %collective-permute-start.9 = (f32[2,32,256]{2,1,0:T(8,128)S(1)}, f32[2,32,256]{2,1,0:T(8,128)S(1)}, u32[]{:S(2)}, u32[]{:S(2)}) collective-permute-start(f32[2,32,256]{2,1,0:T(8,128)S(1)} %get-tuple-element.88), channel_id=1, source_target_pairs={{4,8},{8,4},{12,16},{16,12},{20,24},{24,20},{28,0},{0,28},{5,9},{9... | collective-permute-start | bytes 196616 | tf_op jit(solution)/shard_map/ppermute | solution.py:41
  41.3 3.0 %full.6.refs_5_ = f32[1,3072]{1,0:T(1,128)S(1)} custom-call(f32[8,3072]{1,0:T(8,128)S(1)} %get-tuple-element.95.refs_0_, f32[64,128]{1,0:T(8,128)S(1)} %get-tuple-element.98.refs_1_, s32[1024,128]{1,0:T(8,128)S(1)} %get-tuple-element.97.refs_2_, f32[32,128]{1,0:T(8,128)S(1)} %get-tuple-element.92.refs_1_.refs_3_, ...), custom_call_target="tpu_custom_call" | custom-call | flops 4000000000 | bytes 10000000 | tf_op jit(solution)/shard_map/full/pallas_call | solution.py:108
  44.3 1.4 %collective-permute-done.9.refs_19_ = f32[2,32,256]{2,1,0:T(8,128)S(1)} collective-permute-done((f32[2,32,256]{2,1,0:T(8,128)S(1)}, f32[2,32,256]{2,1,0:T(8,128)S(1)}, u32[]{:S(2)}, u32[]{:S(2)}) %collective-permute-start.9) | collective-permute-done | bytes 65568 | tf_op jit(solution)/shard_map/ppermute | solution.py:41
  46.3 1.5 %advance.7 = (bf16[128,1024]{1,0:T(8,128)(2,1)S(1)}, f32[64,128]{1,0:T(8,128)S(1)}, f32[8,16,128]{2,1,0:T(8,128)}) custom-call(f32[1,256]{1,0:T(1,128)S(1)} %copy-done.2, f32[1,256]{1,0:T(1,128)S(1)} %copy-done.3, f32[2,32,256]{2,1,0:T(8,128)S(1)} %get-tuple-element.77.refs_2_, f32[2,32,256]{2,1,0:T(8,128)S(1)} %get-tuple-element.84.refs_3_, ...), custom_call_target="tpu_custom_call" | custom-call | flops 1000000000 | bytes 4000000 | tf_op jit(solution)/shard_map/advance/pallas_call | solution.py:108
  47.8 3.4 %all-to-all-start = ((f32[8,16,128]{2,1,0:T(8,128)}), f32[8,16,128]{2,1,0:T(8,128)S(1)}, u32[]{:S(2)}, u32[]{:S(2)}) async-start(f32[8,16,128]{2,1,0:T(8,128)} %get-tuple-element.90), calls=%async_computation | async-start | bytes 131072 | tf_op jit(solution)/shard_map/all_to_all | solution.py:709
  51.2 2.8 %full.7 = (f32[1,3072]{1,0:T(1,128)S(1)}, f32[32,3072]{1,0:T(8,128)S(1)}) custom-call(f32[8,3072]{1,0:T(8,128)S(1)} %get-tuple-element.95.refs_0_, f32[64,128]{1,0:T(8,128)S(1)} %get-tuple-element.96.refs_1_, s32[1024,128]{1,0:T(8,128)S(1)} %get-tuple-element.97.refs_2_, f32[32,128]{1,0:T(8,128)S(1)} %get-tuple-element.92.refs_1_.refs_3_, ...), custom_call_target="tpu_custom_call" | custom-call | flops 4000000000 | bytes 10000000 | tf_op jit(solution)/shard_map/full/pallas_call | solution.py:108
  54.1 1.6 %collective-permute-start.12 = (f32[1,3072]{1,0:T(1,128)S(1)}, f32[1,3072]{1,0:T(1,128)S(1)}, u32[]{:S(2)}, u32[]{:S(2)}) collective-permute-start(f32[1,3072]{1,0:T(1,128)S(1)} %get-tuple-element.108.refs_0_), channel_id=1, source_target_pairs={{0,2},{1,3},{2,0},{3,1},{4,6},{5,7},{6,4},{7,5},{8,10},{9,11},{10,... | collective-permute-start | bytes 36872 | tf_op jit(solution)/shard_map/ppermute | solution.py:749
  55.9 1.3 %collective-permute-done.13.refs_3_ = f32[1,3072]{1,0:T(1,128)S(1)} collective-permute-done((f32[1,3072]{1,0:T(1,128)S(1)}, f32[1,3072]{1,0:T(1,128)S(1)}, u32[]{:S(2)}, u32[]{:S(2)}) %collective-permute-start.13) | collective-permute-done | bytes 12320 | tf_op jit(solution)/shard_map/ppermute | solution.py:749
  58.5 1.4 %settle.1 = (f32[32,128]{1,0:T(8,128)}, f32[32,3072]{1,0:T(8,128)}) custom-call(f32[8,16,128]{2,1,0:T(8,128)S(1)} %all-to-all-done.refs_0_, s32[1,128]{1,0:T(1,128)S(1)} %copy-done.5, f32[32,3072]{1,0:T(8,128)S(1)} %get-tuple-element.105.refs_2_), custom_call_target="tpu_custom_call" | custom-call | flops 1000000000 | bytes 4000000 | tf_op jit(solution)/shard_map/settle/pallas_call | solution.py:108
  (31 shorter events, 2.4 us)
Async XLA Ops:
  1.9 5.5 %collective-permute-start.1 = (f32[4,40,128]{2,1,0:T(8,128)S(1)}, f32[4,40,128]{2,1,0:T(8,128)S(1)}, u32[]{:S(2)}, u32[]{:S(2)}) collective-permute-start(f32[4,40,128]{2,1,0:T(8,128)S(1)} %get-tuple-element.62), channel_id=1, source_target_pairs={{0,4},{4,0},{8,12},{12,8},{16,20},{20,16},{24,28},{28,24},{1,5},{5... | collective-permute-start | bytes 245768 | tf_op jit(solution)/shard_map/ppermute | solution.py:32
  4.9 11.0 %collective-permute-start = (f32[2,32,256]{2,1,0:T(8,128)S(1)}, f32[2,32,256]{2,1,0:T(8,128)S(1)}, u32[]{:S(2)}, u32[]{:S(2)}) collective-permute-start(f32[2,32,256]{2,1,0:T(8,128)S(1)} %get-tuple-element.57.refs_10_), channel_id=1, source_target_pairs={{0,4},{4,8},{8,12},{12,16},{16,20},{20,24},{24,28},{28,0},{1,5},{5... | collective-permute-start | bytes 196616 | tf_op jit(solution)/shard_map/ppermute | solution.py:27
  7.4 8.5 %collective-permute-start.2 = (f32[2,40,128]{2,1,0:T(8,128)S(1)}, f32[2,40,128]{2,1,0:T(8,128)S(1)}, u32[]{:S(2)}, u32[]{:S(2)}) collective-permute-start(f32[2,40,128]{2,1,0:T(8,128)S(1)} %get-tuple-element.64), channel_id=1, source_target_pairs={{0,8},{4,12},{8,0},{12,4},{16,24},{20,28},{24,16},{28,20},{1,9},{5... | collective-permute-start | bytes 122888 | tf_op jit(solution)/shard_map/ppermute | solution.py:32
  9.5 6.4 %collective-permute-start.3 = (f32[2,40,128]{2,1,0:T(8,128)S(1)}, f32[2,40,128]{2,1,0:T(8,128)S(1)}, u32[]{:S(2)}, u32[]{:S(2)}) collective-permute-start(f32[2,40,128]{2,1,0:T(8,128)S(1)} %get-tuple-element.65), channel_id=1, source_target_pairs={{0,16},{4,20},{8,24},{12,28},{16,0},{20,4},{24,8},{28,12},{1,17},{... | collective-permute-start | bytes 122888 | tf_op jit(solution)/shard_map/ppermute | solution.py:32
  12.1 5.8 %collective-permute-start.4 = (f32[2,40,128]{2,1,0:T(8,128)S(1)}, f32[2,40,128]{2,1,0:T(8,128)S(1)}, u32[]{:S(2)}, u32[]{:S(2)}) collective-permute-start(f32[2,40,128]{2,1,0:T(8,128)S(1)} %get-tuple-element.66), channel_id=1, source_target_pairs={{0,24},{4,28},{8,16},{12,20},{16,8},{20,12},{24,0},{28,4},{1,25},{... | collective-permute-start | bytes 122888 | tf_op jit(solution)/shard_map/ppermute | solution.py:32
  12.1 5.8 %copy-start = (f32[1,6,32,256]{3,2,1,0:T(8,128)S(1)}, f32[1,6,32,256]{3,2,1,0:T(8,128)}, u32[]{:S(2)}) copy-start(f32[1,6,32,256]{3,2,1,0:T(8,128)} %refs_9_.3) | copy-start | bytes 589828
  12.1 5.8 %copy-start.1 = (f32[1,6,32,256]{3,2,1,0:T(8,128)S(1)}, f32[1,6,32,256]{3,2,1,0:T(8,128)}, u32[]{:S(2)}) copy-start(f32[1,6,32,256]{3,2,1,0:T(8,128)} %refs_8_.3) | copy-start | bytes 589828
  12.1 5.8 %copy-start.2 = (f32[1,256]{1,0:T(1,128)S(1)}, f32[1,256]{1,0:T(1,128)}, u32[]{:S(2)}) copy-start(f32[1,256]{1,0:T(1,128)} %refs_0_.11) | copy-start | bytes 3076
  12.1 5.8 %copy-start.3 = (f32[1,256]{1,0:T(1,128)S(1)}, f32[1,256]{1,0:T(1,128)}, u32[]{:S(2)}) copy-start(f32[1,256]{1,0:T(1,128)} %refs_1_.12) | copy-start | bytes 3076
  12.1 5.8 %copy-start.4 = (s32[1,256]{1,0:T(1,128)S(1)}, s32[1,256]{1,0:T(1,128)}, u32[]{:S(2)}) copy-start(s32[1,256]{1,0:T(1,128)} %refs_6_.3) | copy-start | bytes 3076
  20.4 8.2 %collective-permute-start.5 = (f32[2,32,256]{2,1,0:T(8,128)S(1)}, f32[2,32,256]{2,1,0:T(8,128)S(1)}, u32[]{:S(2)}, u32[]{:S(2)}) collective-permute-start(f32[2,32,256]{2,1,0:T(8,128)S(1)} %get-tuple-element.75), channel_id=1, source_target_pairs={{4,8},{8,4},{12,16},{16,12},{20,24},{24,20},{28,0},{0,28},{5,9},{9... | collective-permute-start | bytes 196616 | tf_op jit(solution)/shard_map/ppermute | solution.py:41
  23.7 4.9 %collective-permute-start.6 = (f32[2,32,256]{2,1,0:T(8,128)S(1)}, f32[2,32,256]{2,1,0:T(8,128)S(1)}, u32[]{:S(2)}, u32[]{:S(2)}) collective-permute-start(f32[2,32,256]{2,1,0:T(8,128)S(1)} %get-tuple-element.76), channel_id=1, source_target_pairs={{0,4},{4,0},{8,12},{12,8},{16,20},{20,16},{24,28},{28,24},{1,5},{5... | collective-permute-start | bytes 196616 | tf_op jit(solution)/shard_map/ppermute | solution.py:41
  29.8 7.1 %collective-permute-start.7 = (f32[2,32,256]{2,1,0:T(8,128)S(1)}, f32[2,32,256]{2,1,0:T(8,128)S(1)}, u32[]{:S(2)}, u32[]{:S(2)}) collective-permute-start(f32[2,32,256]{2,1,0:T(8,128)S(1)} %get-tuple-element.82), channel_id=1, source_target_pairs={{4,8},{8,4},{12,16},{16,12},{20,24},{24,20},{28,0},{0,28},{5,9},{9... | collective-permute-start | bytes 196616 | tf_op jit(solution)/shard_map/ppermute | solution.py:41
  31.9 5.0 %collective-permute-start.8 = (f32[2,32,256]{2,1,0:T(8,128)S(1)}, f32[2,32,256]{2,1,0:T(8,128)S(1)}, u32[]{:S(2)}, u32[]{:S(2)}) collective-permute-start(f32[2,32,256]{2,1,0:T(8,128)S(1)} %get-tuple-element.83), channel_id=1, source_target_pairs={{0,4},{4,0},{8,12},{12,8},{16,20},{20,16},{24,28},{28,24},{1,5},{5... | collective-permute-start | bytes 196616 | tf_op jit(solution)/shard_map/ppermute | solution.py:41
  38.6 7.1 %collective-permute-start.9 = (f32[2,32,256]{2,1,0:T(8,128)S(1)}, f32[2,32,256]{2,1,0:T(8,128)S(1)}, u32[]{:S(2)}, u32[]{:S(2)}) collective-permute-start(f32[2,32,256]{2,1,0:T(8,128)S(1)} %get-tuple-element.88), channel_id=1, source_target_pairs={{4,8},{8,4},{12,16},{16,12},{20,24},{24,20},{28,0},{0,28},{5,9},{9... | collective-permute-start | bytes 196616 | tf_op jit(solution)/shard_map/ppermute | solution.py:41
  41.3 5.0 %collective-permute-start.10 = (f32[2,32,256]{2,1,0:T(8,128)S(1)}, f32[2,32,256]{2,1,0:T(8,128)S(1)}, u32[]{:S(2)}, u32[]{:S(2)}) collective-permute-start(f32[2,32,256]{2,1,0:T(8,128)S(1)} %get-tuple-element.89), channel_id=1, source_target_pairs={{0,4},{4,0},{8,12},{12,8},{16,20},{20,16},{24,28},{28,24},{1,5},{5... | collective-permute-start | bytes 196616 | tf_op jit(solution)/shard_map/ppermute | solution.py:41
  47.8 10.6 %all-to-all-start = ((f32[8,16,128]{2,1,0:T(8,128)}), f32[8,16,128]{2,1,0:T(8,128)S(1)}, u32[]{:S(2)}, u32[]{:S(2)}) async-start(f32[8,16,128]{2,1,0:T(8,128)} %get-tuple-element.90), calls=%async_computation | async-start | bytes 131072 | tf_op jit(solution)/shard_map/all_to_all | solution.py:709
  54.0 4.5 %copy-start.5 = (s32[1,128]{1,0:T(1,128)S(1)}, s32[1,128]{1,0:T(1,128)}, u32[]{:S(2)}) copy-start(s32[1,128]{1,0:T(1,128)} %refs_1_.13) | copy-start | bytes 1540
  54.0 3.2 %collective-permute-start.13 = (f32[1,3072]{1,0:T(1,128)S(1)}, f32[1,3072]{1,0:T(1,128)S(1)}, u32[]{:S(2)}, u32[]{:S(2)}) collective-permute-start(f32[1,3072]{1,0:T(1,128)S(1)} %get-tuple-element.108.refs_0_), channel_id=1, source_target_pairs={{0,3},{1,2},{2,1},{3,0},{4,7},{5,6},{6,5},{7,4},{8,11},{9,10},{10,... | collective-permute-start | bytes 36872 | tf_op jit(solution)/shard_map/ppermute | solution.py:749
  54.1 3.8 %collective-permute-start.12 = (f32[1,3072]{1,0:T(1,128)S(1)}, f32[1,3072]{1,0:T(1,128)S(1)}, u32[]{:S(2)}, u32[]{:S(2)}) collective-permute-start(f32[1,3072]{1,0:T(1,128)S(1)} %get-tuple-element.108.refs_0_), channel_id=1, source_target_pairs={{0,2},{1,3},{2,0},{3,1},{4,6},{5,7},{6,4},{7,5},{8,10},{9,11},{10,... | collective-permute-start | bytes 36872 | tf_op jit(solution)/shard_map/ppermute | solution.py:749
  55.7 2.2 %collective-permute-start.11 = (f32[1,3072]{1,0:T(1,128)S(1)}, f32[1,3072]{1,0:T(1,128)S(1)}, u32[]{:S(2)}, u32[]{:S(2)}) collective-permute-start(f32[1,3072]{1,0:T(1,128)S(1)} %get-tuple-element.108.refs_0_), channel_id=1, source_target_pairs={{0,1},{1,0},{2,3},{3,2},{4,5},{5,4},{6,7},{7,6},{8,9},{9,8},{10,11... | collective-permute-start | bytes 36872 | tf_op jit(solution)/shard_map/ppermute | solution.py:749

commit v4 on v3

--- a/solution.py
+++ b/solution.py
@@ -221,8 +221,8 @@
     width = regions * cap
     points = 2 * lines + width
     whole = points + blk
-    here = lax.axis_index("region")
-    groups = [jnp.bitwise_xor(here, away) for away in range(regions)]
+    region = lax.axis_index("region")
+    groups = [jnp.bitwise_xor(region, away) for away in range(regions)]
     i.ready("end_a", "end_b", "conv", "fault_node")
     o.row[...] = jnp.full((1, whole), -1, jnp.int32)
     o.row[:, 0:lines] = i.end_a[...]
@@ -230,7 +230,7 @@
     for away in range(regions):
         first = 2 * lines + away * cap
         o.row[:, first : first + cap] = i.conv[0, pl.ds(groups[away], 1), :]
-    fault = i.fault_node[...] - here * nreg
+    fault = i.fault_node[...] - region * nreg
     o.row[:, points : points + scen] = jnp.where((fault >= 0) & (fault < nreg), fault, -1)
     row = o.row[...]
     whole_row = row.astype(F32)
@@ -238,6 +238,7 @@
     inside = (column & 127) == iota((whole, blk), 1)
     o.mark[...] = jnp.where(inside, (column >> 7).astype(F32), -1.0).astype(BF16)
     o.fault_mark[...] = o.mark[points : points + scen, :].astype(F32)
+    o.column[...] = column[:points]
     i.ready("list_a", "list_b", "list_conv", "list_fault", "inv")
     for p in range(points + scen):
         if p < lines:
@@ -248,7 +249,7 @@
             away, place = divmod(p - 2 * lines, cap)
             node = jnp.maximum(i.list_conv[0, groups[away], place], 0)
         else:
-            node = jnp.clip(i.list_fault[0, p - points] - here * nreg, 0, nreg - 1)
+            node = jnp.clip(i.list_fault[0, p - points] - region * nreg, 0, nreg - 1)
         taken[p : p + 1, :] = i.inv[pl.ds(node, 1), :]
     taken[points + scen :, :] = jnp.zeros((blk - scen, blk), F32)
     high, low = split2(jnp.where(column >= 0, taken[...], 0.0))
@@ -257,7 +258,11 @@
     i.ready("amp", "phase", "fault_step", "fault_cond")
     source = sources(i.amp[...], i.phase[...])
     for k in range(nblk):
-        source_rows[k * STEPS : (k + 1) * STEPS, :] = source[:, k * blk : (k + 1) * blk]
+        here = slice(k * blk, (k + 1) * blk)
+        source_rows[k * STEPS : (k + 1) * STEPS, :] = source[:, here]
+        z_high, z_low = split2(i.inv[here, :])
+        o.zcat[here, :blk], o.zcat[here, blk:] = z_high, z_low
+        o.base[:, here] = product3(source[:, here], z_high, z_low)
     spread = product3(source_rows[...], o.rows[:, :blk], o.rows[:, blk:], NT)
     row_blk = row >> 7
     at_points = jnp.zeros((STEPS, whole), F32)
@@ -343,13 +348,14 @@
         between_body(points, scen, i, o)
     live = i.row[:, 2 * lines : 2 * lines + width] >= 0
     if packed:
+        recv = i.recv[::-1]
         low = iota((1, LANES), 1) < cap
         params = []
         for row in range(6):
             pieces = []
             for j in range(width // LANES):
-                one = i.recv[j][0, scen + row : scen + row + 1, :]
-                two = i.recv[j][1, scen + row : scen + row + 1, :]
+                one = recv[j][0, scen + row : scen + row + 1, :]
+                two = recv[j][1, scen + row : scen + row + 1, :]
                 pieces.append(jnp.where(low, one, pltpu.roll(two, cap, 1)))
             params.append(jnp.concatenate(pieces, axis=1))
     else:
@@ -365,7 +371,7 @@
         if packed:
             ups, downs = [], []
             for j in range(width // LANES):
-                one, two = i.recv[j][0, :scen], i.recv[j][1, :scen]
+                one, two = recv[j][0, :scen], recv[j][1, :scen]
                 ups.append(jnp.where(low, one, pltpu.roll(two, cap, 1)))
                 downs.append(jnp.where(low, pltpu.roll(one, cap, 1), two))
             first, second = jnp.concatenate(ups, axis=1), jnp.concatenate(downs, axis=1)
@@ -421,10 +427,11 @@
             sides.append(line[:, lines:])
             if hasattr(o, "out"):
                 o.out[j] = made[t0 + j]
-    if hasattr(o, "into"):
+    if sides:
         for j in range(2):
             onward = pick(out, delays, t0 + 2 + j, maxd)
-            o.into[j] = onward
+            if hasattr(o, "into"):
+                o.into[j] = onward
             o.swap_near[j] = jnp.where(even, onward, sides[j])
             o.swap_far[j] = jnp.where(even, sides[j], onward)
     if hasattr(o, "state"):
@@ -454,35 +461,19 @@
     fault_blk = owner_of(i.fault_mark[...])
     x = i.x[...]
     coef = i.coef[...]
-    if pair:
-        known = i
-    else:
-        known = o
-        mark = i.mark[:points].astype(F32)
-        node = jnp.where(mark >= 0.0, mark * blk + iota((points, blk), 1).astype(F32), -1.0)
-        node = jnp.max(node, axis=1, keepdims=True)
-        o.column[...] = jnp.broadcast_to(node, (points, blk)).astype(jnp.int32)
-        i.ready("inv", "amp", "phase")
-        for k in range(nblk):
-            here = slice(k * blk, (k + 1) * blk)
-            o.zcat[here, :blk], o.zcat[here, blk:] = split2(i.inv[k])
-        source = sources(i.amp[...], i.phase[...])
-        for k in range(nblk):
-            here = slice(k * blk, (k + 1) * blk)
-            o.base[:, here] = product3(source[:, here], o.zcat[here, :blk], o.zcat[here, blk:])
     lane = iota((points, blk), 1)
     for k in range(0, nblk, WIDE):
         mine = jnp.concatenate(
-            [onehot(known.column[...] == lane + (k + j) * blk) for j in range(WIDE)], axis=1
+            [onehot(i.column[...] == lane + (k + j) * blk) for j in range(WIDE)], axis=1
         )
         both = dot(x, mine)
         inject = both[: 2 * scen] + both[2 * scen :]
         for j in range(WIDE):
             here = slice((k + j) * blk, (k + j + 1) * blk)
-            z = known.zcat[here, :]
+            z = i.zcat[here, :]
             volts = product3(inject[:, j * blk : (j + 1) * blk], z[:, :blk], z[:, blk:])
             base = [
-                jnp.broadcast_to(known.base[t0 + m : t0 + m + 1, here], (scen, blk))
+                jnp.broadcast_to(i.base[t0 + m : t0 + m + 1, here], (scen, blk))
                 for m in range(2)
             ]
             zcol = jnp.where(fault_blk == k + j, fault_z, 0.0)
@@ -496,15 +487,16 @@
                 o.volts[:, here] = volts[scen:]
 
 
-def rms_body(scen, count, i, o):
+def place_body(i, o):
+    o.done[...] = jnp.zeros((1, LANES), F32)
+
+
+def finish_body(sizes, i, o):
+    regions, cap, scen, group, count, packed = sizes
     parts = [i.parts[k][...] for k in range(count)]
     while len(parts) > 1:
         parts = [parts[k] + parts[k + 1] for k in range(0, len(parts), 2)]
     o.rms[...] = jnp.sqrt(parts[0] / (scen * count * STEPS) + EPS)
-
-
-def settle_body(sizes, i, o):
-    regions, cap, scen, group, packed = sizes
     slots = i.slots[...]
     if packed:
         half = scen // 2
@@ -594,8 +586,9 @@
     recv = couples[:1]
     for k in range(1, regions // 2):
         recv.append(mirrored(couples[k], "region", 2 * k))
+    recv.reverse()
     if not packed:
-        recv = jnp.concatenate(recv, axis=0).transpose(1, 2, 0, 3).reshape(2, half, width)
+        recv = jnp.concatenate(recv[::-1], axis=0).transpose(1, 2, 0, 3).reshape(2, half, width)
 
     whole = points + blk
     model = call(
@@ -606,6 +599,9 @@
             row=((1, whole), jnp.int32),
             mark=((whole, blk), BF16),
             fault_mark=((scen, blk), F32),
+            column=((points, blk), jnp.int32),
+            zcat=((nreg, 2 * blk), BF16),
+            base=((STEPS, nreg), F32),
             rows=((whole, 2 * blk), BF16),
             base_p=((STEPS, points), F32),
             fault_z=((scen, blk), F32),
@@ -636,7 +632,7 @@
     )
     wave = ((2, scen, lines), F32)
     mades, backs, carry = {}, {}, {}
-    squares = swap_near = swap_far = sent = shared = None
+    squares = swap_near = swap_far = sent = None
     for pair in range(STEPS // 2):
         t0 = 2 * pair
         final = t0 + 2 >= STEPS
@@ -669,12 +665,11 @@
             outs.update(
                 swap_far=wave,
                 swap_near=wave,
-                into=wave,
                 state=((2, scen, width), F32),
                 current=((scen, width), F32),
             )
             if t0 + 4 < STEPS:
-                outs.update(out=wave)
+                outs.update(out=wave, into=wave)
             if pair:
                 outs.update(back=wave)
             else:
@@ -695,7 +690,9 @@
         if not pair:
             matrix = made
         if not final:
-            sent, into = into, made.into
+            sent = into
+            if t0 + 4 < STEPS:
+                into = made.into
             swap_far = swapped(made.swap_far, "region", 1)
             swap_near = swapped(made.swap_near, "region", 0)
             if t0 + 4 < STEPS:
@@ -717,50 +714,42 @@
             coef=made.coef,
             fault_mark=model.fault_mark,
             fault_z=model.fault_z,
+            column=model.column,
+            zcat=model.zcat,
+            base=model.base,
         )
         if pair:
-            ins.update(squares=squares, **shared)
-        else:
-            ins.update(mark=model.mark)
+            ins.update(squares=squares)
         outs = dict(squares=((1, nreg), F32))
         if final:
             outs.update(volts=((scen, nreg), F32))
-        if not pair:
-            outs.update(
-                base=((STEPS, nreg), F32),
-                column=((points, blk), jnp.int32),
-                zcat=((nreg, 2 * blk), BF16),
-            )
         full = call(
             functools.partial(full_body, (nblk, points, scen), pair),
             "full",
             ins,
             outs,
-            hbm={} if pair else dict(inv=inv_blocks, amp=amp, phase=phase),
             cost=(4e9, 1e7),
         )
         squares = full.squares
-        if not pair:
-            shared = dict(base=full.base, column=full.column, zcat=full.zcat)
 
     parts = [squares]
     for offset in range(1, count):
         pairs = [(source, source ^ offset) for source in range(count)]
         parts.append(lax.ppermute(squares, "scen", pairs))
-    settled = call(
-        functools.partial(settle_body, (regions, cap, scen, group, packed)),
-        "settle",
-        dict(slots=recv_slot, recv=returned, volts=full.volts),
-        dict(current=((scen, group), F32)),
+    placed = call(
+        place_body,
+        "place",
+        dict(volts=full.volts),
+        dict(done=((1, LANES), F32)),
         relays=dict(volts=((scen, nreg), F32)),
     )
     tail = call(
-        functools.partial(rms_body, scen, count),
-        "rms",
-        dict(parts=parts),
-        dict(rms=((1, nreg), F32)),
-    )
-    return settled.volts, settled.current, tail.rms.reshape(nreg)
+        functools.partial(finish_body, (regions, cap, scen, group, count, packed)),
+        "finish",
+        dict(slots=recv_slot, recv=returned, parts=parts, after=placed.done),
+        dict(rms=((1, nreg), F32), current=((scen, group), F32)),
+    )
+    return placed.volts, tail.current, tail.rms.reshape(nreg)
 
 
 def solution(mesh):

time: 60.3 us -> 58.9 us (0.977)
  Pallas kernels: 27.5 us -> 24.8 us
  starting transfers between devices: 21.2 us -> 23.8 us
  waiting for transfers between devices: 10.3 us -> 9.28 us
    pallas_call x13, Pallas kernels: 27.5 us -> 24.8 us  [call(): pl.pallas_call(kernel, name=name, out_shape=[jax.ShapeDtypeStruct(*shape)...]
    ppermute x4, waiting for transfers between devices: 4.36 us -> 2.48 us  [mirrored(): lax.ppermute(value, axis, [(source, source ^ offset) for source in range(...]
    ppermute x6, starting transfers between devices: 8.14 us -> 9.97 us  [swapped(): return lax.ppermute(value, axis, pairs)]
    ppermute x6, waiting for transfers between devices: 3.99 us -> 5.42 us  [swapped(): return lax.ppermute(value, axis, pairs)]
    ppermute x3, waiting for transfers between devices: 1.91 us -> 1.15 us  [per_device(): parts.append(lax.ppermute(squares, 'scen', pairs))]
    all_to_all x1, starting transfers between devices: 3.35 us -> 3.97 us  [per_device(): lax.all_to_all(current, 'region', split_axis=0, concat_axis=0, tiled=True)]
  transfers between devices with their start and end apart: 15 -> 15, of which waited for: 7 -> 9; matrix products, arithmetic and copies ran while one was open for 0% -> 0% of each run, Pallas kernels for 30% -> 28%
where the time goes in v4:
time: 58.9 us; the launch traced here: 58.7 us
  Pallas kernels  24.8 us (42%)
  starting transfers between devices  23.8 us (40%)
  waiting for transfers between devices  9.28 us (16%)
  between operations  0.78 us (1%)
    pallas_call x13, Pallas kernels, call(): pl.pallas_call(kernel, name=name, out_shape=[jax.ShapeDtypeStruct(*shape)...  24.8 us
    ppermute x6, starting transfers between devices, swapped(): return lax.ppermute(value, axis, pairs)  9.97 us
    ppermute x4, starting transfers between devices, mirrored(): lax.ppermute(value, axis, [(source, source ^ offset) for source in range(...  7.85 us
    ppermute x6, waiting for transfers between devices, swapped(): return lax.ppermute(value, axis, pairs)  5.42 us
    all_to_all x1, starting transfers between devices, per_device(): lax.all_to_all(current, 'region', split_axis=0, concat_axis=0, tiled=True)  3.97 us
    ppermute x4, waiting for transfers between devices, mirrored(): lax.ppermute(value, axis, [(source, source ^ offset) for source in range(...  2.48 us
    ppermute x3, starting transfers between devices, per_device(): parts.append(lax.ppermute(squares, 'scen', pairs))  1.92 us
  transfers between devices with their start and end apart: 15, of which 9 were waited for; matrix products, arithmetic and copies ran while one was open for 0% of the time, Pallas kernels for 28%

profile of v4, /device:TPU:0, one launch (start us, length us, event | category | flops | bytes accessed | tf_op | source)
XLA Modules:
  0.0 58.7 jit_solution(13833971498333313425)
XLA Ops:
  0.6 1.2 %start.1 = (f32[2,32,256]{2,1,0:T(8,128)S(1)}, f32[4,40,128]{2,1,0:T(8,128)S(1)}, f32[4,40,128]{2,1,0:T(8,128)S(1)}) custom-call(s32[1,128]{1,0:T(1,128)} %refs_6_.5, f32[6,128]{1,0:T(8,128)} %refs_1_.7, f32[2,32,128]{2,1,0:T(8,128)} %refs_2_.3, f32[1,6,32,256]{3,2,1,0:T(8,128)} %refs_8_.3, s32[1,256]{1,0:T(1,128)} %refs_6_.4), custom_call_target="tpu_custom_call" | custom-call | flops 1000000000 | bytes 4000000 | tf_op jit(solution)/shard_map/start/pallas_call | solution.py:108
  1.9 3.0 %collective-permute-start.1 = (f32[4,40,128]{2,1,0:T(8,128)S(1)}, f32[4,40,128]{2,1,0:T(8,128)S(1)}, u32[]{:S(2)}, u32[]{:S(2)}) collective-permute-start(f32[4,40,128]{2,1,0:T(8,128)S(1)} %get-tuple-element.64), channel_id=1, source_target_pairs={{0,4},{4,0},{8,12},{12,8},{16,20},{20,16},{24,28},{28,24},{1,5},{5... | collective-permute-start | bytes 245768 | tf_op jit(solution)/shard_map/ppermute | solution.py:32
  5.0 2.4 %collective-permute-done.1.refs_1_ = f32[4,40,128]{2,1,0:T(8,128)S(1)} collective-permute-done((f32[4,40,128]{2,1,0:T(8,128)S(1)}, f32[4,40,128]{2,1,0:T(8,128)S(1)}, u32[]{:S(2)}, u32[]{:S(2)}) %collective-permute-start.1) | collective-permute-done | bytes 81952 | tf_op jit(solution)/shard_map/ppermute | solution.py:32
  7.4 4.2 %collective-permute-start.2 = (f32[2,40,128]{2,1,0:T(8,128)S(1)}, f32[2,40,128]{2,1,0:T(8,128)S(1)}, u32[]{:S(2)}, u32[]{:S(2)}) collective-permute-start(f32[2,40,128]{2,1,0:T(8,128)S(1)} %get-tuple-element.65), channel_id=1, source_target_pairs={{0,24},{4,28},{8,16},{12,20},{16,8},{20,12},{24,0},{28,4},{1,25},{... | collective-permute-start | bytes 122888 | tf_op jit(solution)/shard_map/ppermute | solution.py:32
  11.6 0.6 %collective-permute-start.4 = (f32[2,40,128]{2,1,0:T(8,128)S(1)}, f32[2,40,128]{2,1,0:T(8,128)S(1)}, u32[]{:S(2)}, u32[]{:S(2)}) collective-permute-start(f32[2,40,128]{2,1,0:T(8,128)S(1)} %get-tuple-element.67), channel_id=1, source_target_pairs={{0,8},{4,12},{8,0},{12,4},{16,24},{20,28},{24,16},{28,20},{1,9},{5... | collective-permute-start | bytes 122888 | tf_op jit(solution)/shard_map/ppermute | solution.py:32
  12.2 4.1 %rows.1 = (s32[1,1152]{1,0:T(1,128)S(1)}, bf16[1152,128]{1,0:T(8,128)(2,1)S(1)}, f32[32,128]{1,0:T(8,128)S(1)}, s32[1024,128]{1,0:T(8,128)S(1)}, bf16[3072,256]{...) custom-call(s32[1,256]{1,0:T(1,128)} %refs_4_.3, ...), custom_call_target="tpu_custom_call" | custom-call | flops 4000000000 | bytes 20000000 | tf_op jit(solution)/shard_map/rows/pallas_call | solution.py:108
  16.5 2.4 %advance.4 = (bf16[128,1024]{1,0:T(8,128)(2,1)S(1)}, f32[64,128]{1,0:T(8,128)S(1)}, f32[2,32,256]{2,1,0:T(8,128)S(1)}, f32[2,32,256]{2,1,0:T(8,128)S(1)}, f32[2,...) custom-call(f32[1,256]{1,0:T(1,128)S(1)} %copy-done.2, ...), custom_call_target="tpu_custom_call" | custom-call | flops 1000000000 | bytes 4000000 | tf_op jit(solution)/shard_map/advance/pallas_call | solution.py:108
  18.9 5.1 %collective-permute-start.5 = (f32[2,32,256]{2,1,0:T(8,128)S(1)}, f32[2,32,256]{2,1,0:T(8,128)S(1)}, u32[]{:S(2)}, u32[]{:S(2)}) collective-permute-start(f32[2,32,256]{2,1,0:T(8,128)S(1)} %get-tuple-element.77), channel_id=1, source_target_pairs={{4,8},{8,4},{12,16},{16,12},{20,24},{24,20},{28,0},{0,28},{5,9},{9... | collective-permute-start | bytes 196616 | tf_op jit(solution)/shard_map/ppermute | solution.py:41
  24.1 2.8 %full.4.refs_5_ = f32[1,3072]{1,0:T(1,128)S(1)} custom-call(f32[8,3072]{1,0:T(8,128)S(1)} %get-tuple-element.57.refs_0_, f32[64,128]{1,0:T(8,128)S(1)} %get-tuple-element.98.refs_1_, s32[1024,128]{1,0:T(8,128)S(1)} %get-tuple-element.93.refs_2_, f32[32,128]{1,0:T(8,128)S(1)} %get-tuple-element.94.refs_3_, f32[32,128]{1,0:T(8,128)S(1)} %get-tuple-element.95.refs_4_, ...), custom_call_target="tpu_custom_call" | custom-call | flops 4000000000 | bytes 10000000 | tf_op jit(solution)/shard_map/full/pallas_call | solution.py:108
  26.9 1.4 %collective-permute-done.6.refs_21_ = f32[2,32,256]{2,1,0:T(8,128)S(1)} collective-permute-done((f32[2,32,256]{2,1,0:T(8,128)S(1)}, f32[2,32,256]{2,1,0:T(8,128)S(1)}, u32[]{:S(2)}, u32[]{:S(2)}) %collective-permute-start.6) | collective-permute-done | bytes 65568 | tf_op jit(solution)/shard_map/ppermute | solution.py:41
  28.3 1.2 %advance.5 = (bf16[128,1024]{1,0:T(8,128)(2,1)S(1)}, f32[64,128]{1,0:T(8,128)S(1)}, f32[2,32,256]{2,1,0:T(8,128)S(1)}, f32[2,32,256]{2,1,0:T(8,128)S(1)}, f32[2,...) custom-call(f32[1,256]{1,0:T(1,128)S(1)} %copy-done.2, ...), custom_call_target="tpu_custom_call" | custom-call | flops 1000000000 | bytes 4000000 | tf_op jit(solution)/shard_map/advance/pallas_call | solution.py:108
  29.5 2.8 %collective-permute-start.7 = (f32[2,32,256]{2,1,0:T(8,128)S(1)}, f32[2,32,256]{2,1,0:T(8,128)S(1)}, u32[]{:S(2)}, u32[]{:S(2)}) collective-permute-start(f32[2,32,256]{2,1,0:T(8,128)S(1)} %get-tuple-element.84), channel_id=1, source_target_pairs={{4,8},{8,4},{12,16},{16,12},{20,24},{24,20},{28,0},{0,28},{5,9},{9... | collective-permute-start | bytes 196616 | tf_op jit(solution)/shard_map/ppermute | solution.py:41
  32.3 2.9 %full.5.refs_5_ = f32[1,3072]{1,0:T(1,128)S(1)} custom-call(f32[8,3072]{1,0:T(8,128)S(1)} %get-tuple-element.57.refs_0_, f32[64,128]{1,0:T(8,128)S(1)} %get-tuple-element.97.refs_1_, s32[1024,128]{1,0:T(8,128)S(1)} %get-tuple-element.93.refs_2_, f32[32,128]{1,0:T(8,128)S(1)} %get-tuple-element.94.refs_3_, f32[32,128]{1,0:T(8,128)S(1)} %get-tuple-element.95.refs_4_, ...), custom_call_target="tpu_custom_call" | custom-call | flops 4000000000 | bytes 10000000 | tf_op jit(solution)/shard_map/full/pallas_call | solution.py:108
  35.1 1.5 %collective-permute-done.7.refs_21_ = f32[2,32,256]{2,1,0:T(8,128)S(1)} collective-permute-done((f32[2,32,256]{2,1,0:T(8,128)S(1)}, f32[2,32,256]{2,1,0:T(8,128)S(1)}, u32[]{:S(2)}, u32[]{:S(2)}) %collective-permute-start.7) | collective-permute-done | bytes 65568 | tf_op jit(solution)/shard_map/ppermute | solution.py:41
  37.2 1.2 %advance.6 = (bf16[128,1024]{1,0:T(8,128)(2,1)S(1)}, f32[64,128]{1,0:T(8,128)S(1)}, f32[2,32,256]{2,1,0:T(8,128)S(1)}, f32[2,32,256]{2,1,0:T(8,128)S(1)}, f32[2,...) custom-call(f32[1,256]{1,0:T(1,128)S(1)} %copy-done.2, f32[1,256]{1,0:T(1,128)S(1)} %copy-done.3, ...), custom_call_target="tpu_custom_call" | custom-call | flops 1000000000 | bytes 4000000 | tf_op jit(solution)/shard_map/advance/pallas_call | solution.py:108
  38.4 2.1 %collective-permute-start.9 = (f32[2,32,256]{2,1,0:T(8,128)S(1)}, f32[2,32,256]{2,1,0:T(8,128)S(1)}, u32[]{:S(2)}, u32[]{:S(2)}) collective-permute-start(f32[2,32,256]{2,1,0:T(8,128)S(1)} %get-tuple-element.90), channel_id=1, source_target_pairs={{4,8},{8,4},{12,16},{16,12},{20,24},{24,20},{28,0},{0,28},{5,9},{9... | collective-permute-start | bytes 196616 | tf_op jit(solution)/shard_map/ppermute | solution.py:41
  40.5 3.0 %full.6.refs_5_ = f32[1,3072]{1,0:T(1,128)S(1)} custom-call(f32[8,3072]{1,0:T(8,128)S(1)} %get-tuple-element.57.refs_0_, f32[64,128]{1,0:T(8,128)S(1)} %get-tuple-element.96.refs_1_, s32[1024,128]{1,0:T(8,128)S(1)} %get-tuple-element.93.refs_2_, f32[32,128]{1,0:T(8,128)S(1)} %get-tuple-element.94.refs_3_, f32[32,128]{1,0:T(8,128)S(1)} %get-tuple-element.95.refs_4_, ...), custom_call_target="tpu_custom_call" | custom-call | flops 4000000000 | bytes 10000000 | tf_op jit(solution)/shard_map/full/pallas_call | solution.py:108
  43.5 1.9 %collective-permute-done.9.refs_19_ = f32[2,32,256]{2,1,0:T(8,128)S(1)} collective-permute-done((f32[2,32,256]{2,1,0:T(8,128)S(1)}, f32[2,32,256]{2,1,0:T(8,128)S(1)}, u32[]{:S(2)}, u32[]{:S(2)}) %collective-permute-start.9) | collective-permute-done | bytes 65568 | tf_op jit(solution)/shard_map/ppermute | solution.py:41
  45.5 1.5 %advance.7 = (bf16[128,1024]{1,0:T(8,128)(2,1)S(1)}, f32[64,128]{1,0:T(8,128)S(1)}, f32[8,16,128]{2,1,0:T(8,128)}) custom-call(f32[1,256]{1,0:T(1,128)S(1)} %copy-done.2, f32[1,256]{1,0:T(1,128)S(1)} %copy-done.3, f32[2,32,256]{2,1,0:T(8,128)S(1)} %get-tuple-element.79.refs_2_, f32[2,32,256]{2,1,0:T(8,128)S(1)} %get-tuple-element.86.refs_3_, ...), custom_call_target="tpu_custom_call" | custom-call | flops 1000000000 | bytes 4000000 | tf_op jit(solution)/shard_map/advance/pallas_call | solution.py:108
  47.0 4.0 %all-to-all-start = ((f32[8,16,128]{2,1,0:T(8,128)}), f32[8,16,128]{2,1,0:T(8,128)S(1)}, u32[]{:S(2)}, u32[]{:S(2)}) async-start(f32[8,16,128]{2,1,0:T(8,128)} %get-tuple-element.108), calls=%async_computation | async-start | bytes 131072 | tf_op jit(solution)/shard_map/all_to_all | solution.py:706
  50.9 2.8 %full.7 = (f32[1,3072]{1,0:T(1,128)S(1)}, f32[32,3072]{1,0:T(8,128)S(1)}) custom-call(f32[8,3072]{1,0:T(8,128)S(1)} %get-tuple-element.57.refs_0_, f32[64,128]{1,0:T(8,128)S(1)} %get-tuple-element.92.refs_1_, s32[1024,128]{1,0:T(8,128)S(1)} %get-tuple-element.93.refs_2_, f32[32,128]{1,0:T(8,128)S(1)} %get-tuple-element.94.refs_3_, ...), custom_call_target="tpu_custom_call" | custom-call | flops 4000000000 | bytes 10000000 | tf_op jit(solution)/shard_map/full/pallas_call | solution.py:108
  53.8 1.6 %collective-permute-start.12 = (f32[1,3072]{1,0:T(1,128)S(1)}, f32[1,3072]{1,0:T(1,128)S(1)}, u32[]{:S(2)}, u32[]{:S(2)}) collective-permute-start(f32[1,3072]{1,0:T(1,128)S(1)} %get-tuple-element.107.refs_1_), channel_id=1, source_target_pairs={{0,2},{1,3},{2,0},{3,1},{4,6},{5,7},{6,4},{7,5},{8,10},{9,11},{10,... | collective-permute-start | bytes 36872 | tf_op jit(solution)/shard_map/ppermute | solution.py:738
  55.7 0.8 %place.1 = (f32[1,128]{1,0:T(1,128)S(1)}, f32[32,3072]{1,0:T(8,128)}) custom-call(f32[32,3072]{1,0:T(8,128)S(1)} %get-tuple-element.104.refs_0_), custom_call_target="tpu_custom_call" | custom-call | flops 1000000000 | bytes 4000000 | tf_op jit(solution)/shard_map/place/pallas_call | solution.py:108
  57.8 0.8 %finish.1 = (f32[1,3072]{1,0:T(1,128)}, f32[32,128]{1,0:T(8,128)}) custom-call(f32[1,128]{1,0:T(1,128)S(1)} %get-tuple-element.106.refs_0_, f32[1,3072]{1,0:T(1,128)S(1)} %get-tuple-element.107.refs_1_, f32[1,3072]{1,0:T(1,128)S(1)} %collective-permute-done.11.refs_2_, f32[1,3072]{1,0:T(1,128)S(1)} %collective-permute-done.12.refs_3_, ...), custom_call_target="tpu_custom_call" | custom-call | flops 1000000000 | bytes 4000000 | tf_op jit(solution)/shard_map/finish/pallas_call | solution.py:108
  (31 shorter events, 2.6 us)
Async XLA Ops:
  1.9 5.5 %collective-permute-start.1 = (f32[4,40,128]{2,1,0:T(8,128)S(1)}, f32[4,40,128]{2,1,0:T(8,128)S(1)}, u32[]{:S(2)}, u32[]{:S(2)}) collective-permute-start(f32[4,40,128]{2,1,0:T(8,128)S(1)} %get-tuple-element.64), channel_id=1, source_target_pairs={{0,4},{4,0},{8,12},{12,8},{16,20},{20,16},{24,28},{28,24},{1,5},{5... | collective-permute-start | bytes 245768 | tf_op jit(solution)/shard_map/ppermute | solution.py:32
  4.9 11.4 %collective-permute-start = (f32[2,32,256]{2,1,0:T(8,128)S(1)}, f32[2,32,256]{2,1,0:T(8,128)S(1)}, u32[]{:S(2)}, u32[]{:S(2)}) collective-permute-start(f32[2,32,256]{2,1,0:T(8,128)S(1)} %get-tuple-element.59.refs_10_), channel_id=1, source_target_pairs={{0,4},{4,8},{8,12},{12,16},{16,20},{20,24},{24,28},{28,0},{1,5},{5... | collective-permute-start | bytes 196616 | tf_op jit(solution)/shard_map/ppermute | solution.py:27
  7.4 9.0 %collective-permute-start.2 = (f32[2,40,128]{2,1,0:T(8,128)S(1)}, f32[2,40,128]{2,1,0:T(8,128)S(1)}, u32[]{:S(2)}, u32[]{:S(2)}) collective-permute-start(f32[2,40,128]{2,1,0:T(8,128)S(1)} %get-tuple-element.65), channel_id=1, source_target_pairs={{0,24},{4,28},{8,16},{12,20},{16,8},{20,12},{24,0},{28,4},{1,25},{... | collective-permute-start | bytes 122888 | tf_op jit(solution)/shard_map/ppermute | solution.py:32
  11.5 4.9 %collective-permute-start.3 = (f32[2,40,128]{2,1,0:T(8,128)S(1)}, f32[2,40,128]{2,1,0:T(8,128)S(1)}, u32[]{:S(2)}, u32[]{:S(2)}) collective-permute-start(f32[2,40,128]{2,1,0:T(8,128)S(1)} %get-tuple-element.66), channel_id=1, source_target_pairs={{0,16},{4,20},{8,24},{12,28},{16,0},{20,4},{24,8},{28,12},{1,17},{... | collective-permute-start | bytes 122888 | tf_op jit(solution)/shard_map/ppermute | solution.py:32
  11.6 4.9 %collective-permute-start.4 = (f32[2,40,128]{2,1,0:T(8,128)S(1)}, f32[2,40,128]{2,1,0:T(8,128)S(1)}, u32[]{:S(2)}, u32[]{:S(2)}) collective-permute-start(f32[2,40,128]{2,1,0:T(8,128)S(1)} %get-tuple-element.67), channel_id=1, source_target_pairs={{0,8},{4,12},{8,0},{12,4},{16,24},{20,28},{24,16},{28,20},{1,9},{5... | collective-permute-start | bytes 122888 | tf_op jit(solution)/shard_map/ppermute | solution.py:32
  12.2 4.3 %copy-start = (f32[1,6,32,256]{3,2,1,0:T(8,128)S(1)}, f32[1,6,32,256]{3,2,1,0:T(8,128)}, u32[]{:S(2)}) copy-start(f32[1,6,32,256]{3,2,1,0:T(8,128)} %refs_9_.3) | copy-start | bytes 589828
  12.2 4.3 %copy-start.1 = (f32[1,6,32,256]{3,2,1,0:T(8,128)S(1)}, f32[1,6,32,256]{3,2,1,0:T(8,128)}, u32[]{:S(2)}) copy-start(f32[1,6,32,256]{3,2,1,0:T(8,128)} %refs_8_.3) | copy-start | bytes 589828
  12.2 4.3 %copy-start.2 = (f32[1,256]{1,0:T(1,128)S(1)}, f32[1,256]{1,0:T(1,128)}, u32[]{:S(2)}) copy-start(f32[1,256]{1,0:T(1,128)} %refs_0_.11) | copy-start | bytes 3076
  12.2 4.3 %copy-start.3 = (f32[1,256]{1,0:T(1,128)S(1)}, f32[1,256]{1,0:T(1,128)}, u32[]{:S(2)}) copy-start(f32[1,256]{1,0:T(1,128)} %refs_1_.11) | copy-start | bytes 3076
  12.2 4.3 %copy-start.4 = (s32[1,256]{1,0:T(1,128)S(1)}, s32[1,256]{1,0:T(1,128)}, u32[]{:S(2)}) copy-start(s32[1,256]{1,0:T(1,128)} %refs_6_.4) | copy-start | bytes 3076
  18.9 8.0 %collective-permute-start.5 = (f32[2,32,256]{2,1,0:T(8,128)S(1)}, f32[2,32,256]{2,1,0:T(8,128)S(1)}, u32[]{:S(2)}, u32[]{:S(2)}) collective-permute-start(f32[2,32,256]{2,1,0:T(8,128)S(1)} %get-tuple-element.77), channel_id=1, source_target_pairs={{4,8},{8,4},{12,16},{16,12},{20,24},{24,20},{28,0},{0,28},{5,9},{9... | collective-permute-start | bytes 196616 | tf_op jit(solution)/shard_map/ppermute | solution.py:41
  24.0 4.3 %collective-permute-start.6 = (f32[2,32,256]{2,1,0:T(8,128)S(1)}, f32[2,32,256]{2,1,0:T(8,128)S(1)}, u32[]{:S(2)}, u32[]{:S(2)}) collective-permute-start(f32[2,32,256]{2,1,0:T(8,128)S(1)} %get-tuple-element.78), channel_id=1, source_target_pairs={{0,4},{4,0},{8,12},{12,8},{16,20},{20,16},{24,28},{28,24},{1,5},{5... | collective-permute-start | bytes 196616 | tf_op jit(solution)/shard_map/ppermute | solution.py:41
  29.5 7.1 %collective-permute-start.7 = (f32[2,32,256]{2,1,0:T(8,128)S(1)}, f32[2,32,256]{2,1,0:T(8,128)S(1)}, u32[]{:S(2)}, u32[]{:S(2)}) collective-permute-start(f32[2,32,256]{2,1,0:T(8,128)S(1)} %get-tuple-element.84), channel_id=1, source_target_pairs={{4,8},{8,4},{12,16},{16,12},{20,24},{24,20},{28,0},{0,28},{5,9},{9... | collective-permute-start | bytes 196616 | tf_op jit(solution)/shard_map/ppermute | solution.py:41
  32.3 5.0 %collective-permute-start.8 = (f32[2,32,256]{2,1,0:T(8,128)S(1)}, f32[2,32,256]{2,1,0:T(8,128)S(1)}, u32[]{:S(2)}, u32[]{:S(2)}) collective-permute-start(f32[2,32,256]{2,1,0:T(8,128)S(1)} %get-tuple-element.85), channel_id=1, source_target_pairs={{0,4},{4,0},{8,12},{12,8},{16,20},{20,16},{24,28},{28,24},{1,5},{5... | collective-permute-start | bytes 196616 | tf_op jit(solution)/shard_map/ppermute | solution.py:41
  38.4 7.0 %collective-permute-start.9 = (f32[2,32,256]{2,1,0:T(8,128)S(1)}, f32[2,32,256]{2,1,0:T(8,128)S(1)}, u32[]{:S(2)}, u32[]{:S(2)}) collective-permute-start(f32[2,32,256]{2,1,0:T(8,128)S(1)} %get-tuple-element.90), channel_id=1, source_target_pairs={{4,8},{8,4},{12,16},{16,12},{20,24},{24,20},{28,0},{0,28},{5,9},{9... | collective-permute-start | bytes 196616 | tf_op jit(solution)/shard_map/ppermute | solution.py:41
  40.5 5.0 %collective-permute-start.10 = (f32[2,32,256]{2,1,0:T(8,128)S(1)}, f32[2,32,256]{2,1,0:T(8,128)S(1)}, u32[]{:S(2)}, u32[]{:S(2)}) collective-permute-start(f32[2,32,256]{2,1,0:T(8,128)S(1)} %get-tuple-element.91), channel_id=1, source_target_pairs={{0,4},{4,0},{8,12},{12,8},{16,20},{20,16},{24,28},{28,24},{1,5},{5... | collective-permute-start | bytes 196616 | tf_op jit(solution)/shard_map/ppermute | solution.py:41
  47.0 10.9 %all-to-all-start = ((f32[8,16,128]{2,1,0:T(8,128)}), f32[8,16,128]{2,1,0:T(8,128)S(1)}, u32[]{:S(2)}, u32[]{:S(2)}) async-start(f32[8,16,128]{2,1,0:T(8,128)} %get-tuple-element.108), calls=%async_computation | async-start | bytes 131072 | tf_op jit(solution)/shard_map/all_to_all | solution.py:706
  53.8 4.1 %copy-start.5 = (s32[1,128]{1,0:T(1,128)S(1)}, s32[1,128]{1,0:T(1,128)}, u32[]{:S(2)}) copy-start(s32[1,128]{1,0:T(1,128)} %refs_6_.5) | copy-start | bytes 1540
  53.8 3.2 %collective-permute-start.13 = (f32[1,3072]{1,0:T(1,128)S(1)}, f32[1,3072]{1,0:T(1,128)S(1)}, u32[]{:S(2)}, u32[]{:S(2)}) collective-permute-start(f32[1,3072]{1,0:T(1,128)S(1)} %get-tuple-element.107.refs_1_), channel_id=1, source_target_pairs={{0,3},{1,2},{2,1},{3,0},{4,7},{5,6},{6,5},{7,4},{8,11},{9,10},{10,... | collective-permute-start | bytes 36872 | tf_op jit(solution)/shard_map/ppermute | solution.py:738
  53.8 3.8 %collective-permute-start.12 = (f32[1,3072]{1,0:T(1,128)S(1)}, f32[1,3072]{1,0:T(1,128)S(1)}, u32[]{:S(2)}, u32[]{:S(2)}) collective-permute-start(f32[1,3072]{1,0:T(1,128)S(1)} %get-tuple-element.107.refs_1_), channel_id=1, source_target_pairs={{0,2},{1,3},{2,0},{3,1},{4,6},{5,7},{6,4},{7,5},{8,10},{9,11},{10,... | collective-permute-start | bytes 36872 | tf_op jit(solution)/shard_map/ppermute | solution.py:738
  55.4 2.2 %collective-permute-start.11 = (f32[1,3072]{1,0:T(1,128)S(1)}, f32[1,3072]{1,0:T(1,128)S(1)}, u32[]{:S(2)}, u32[]{:S(2)}) collective-permute-start(f32[1,3072]{1,0:T(1,128)S(1)} %get-tuple-element.107.refs_1_), channel_id=1, source_target_pairs={{0,1},{1,0},{2,3},{3,2},{4,5},{5,4},{6,7},{7,6},{8,9},{9,8},{10,11... | collective-permute-start | bytes 36872 | tf_op jit(solution)/shard_map/ppermute | solution.py:738

commit v5 on v4

--- a/solution.py
+++ b/solution.py
@@ -215,7 +215,7 @@
     return amp * jnp.cos(OMEGA * instant + phase)
 
 
-def rows_body(sizes, i, o, taken, source_rows):
+def tables_body(sizes, i, o):
     nreg, nblk, lines, regions, cap, scen = sizes
     blk = LANES
     width = regions * cap
@@ -238,7 +238,25 @@
     inside = (column & 127) == iota((whole, blk), 1)
     o.mark[...] = jnp.where(inside, (column >> 7).astype(F32), -1.0).astype(BF16)
     o.fault_mark[...] = o.mark[points : points + scen, :].astype(F32)
-    o.column[...] = column[:points]
+    o.column[...] = column
+    i.ready("amp", "phase", "inv")
+    source = sources(i.amp[...], i.phase[...])
+    for k in range(nblk):
+        here = slice(k * blk, (k + 1) * blk)
+        o.source_rows[k * STEPS : (k + 1) * STEPS, :] = source[:, here]
+        z_high, z_low = split2(i.inv[here, :])
+        o.zcat[here, :blk], o.zcat[here, blk:] = z_high, z_low
+        o.base[:, here] = product3(source[:, here], z_high, z_low)
+
+
+def rows_body(sizes, i, o, taken):
+    nreg, nblk, lines, regions, cap, scen = sizes
+    blk = LANES
+    points = 2 * lines + regions * cap
+    whole = points + blk
+    region = lax.axis_index("region")
+    groups = [jnp.bitwise_xor(region, away) for away in range(regions)]
+    row, column = i.row[...], i.column[...]
     i.ready("list_a", "list_b", "list_conv", "list_fault", "inv")
     for p in range(points + scen):
         if p < lines:
@@ -255,15 +273,8 @@
     high, low = split2(jnp.where(column >= 0, taken[...], 0.0))
     o.rows[:, :blk] = high
     o.rows[:, blk:] = low
-    i.ready("amp", "phase", "fault_step", "fault_cond")
-    source = sources(i.amp[...], i.phase[...])
-    for k in range(nblk):
-        here = slice(k * blk, (k + 1) * blk)
-        source_rows[k * STEPS : (k + 1) * STEPS, :] = source[:, here]
-        z_high, z_low = split2(i.inv[here, :])
-        o.zcat[here, :blk], o.zcat[here, blk:] = z_high, z_low
-        o.base[:, here] = product3(source[:, here], z_high, z_low)
-    spread = product3(source_rows[...], o.rows[:, :blk], o.rows[:, blk:], NT)
+    i.ready("fault_step", "fault_cond")
+    spread = product3(i.source_rows[...], o.rows[:, :blk], o.rows[:, blk:], NT)
     row_blk = row >> 7
     at_points = jnp.zeros((STEPS, whole), F32)
     for k in range(nblk):
@@ -464,7 +475,7 @@
     lane = iota((points, blk), 1)
     for k in range(0, nblk, WIDE):
         mine = jnp.concatenate(
-            [onehot(i.column[...] == lane + (k + j) * blk) for j in range(WIDE)], axis=1
+            [onehot(i.column[:points, :] == lane + (k + j) * blk) for j in range(WIDE)], axis=1
         )
         both = dot(x, mine)
         inject = both[: 2 * scen] + both[2 * scen :]
@@ -571,13 +582,40 @@
         even, odd = slots[0::2], slots[1::2]
     odd = mirrored(odd, "region", 1)
     into = head.into
-    far_in = shifted(into, "region", 1)
+    whole = points + blk
+    inv_flat = inv_blocks.reshape(nreg, blk)
+    tables = call(
+        functools.partial(tables_body, (nreg, nblk, lines, regions, cap, scen)),
+        "tables",
+        {},
+        dict(
+            row=((1, whole), jnp.int32),
+            mark=((whole, blk), BF16),
+            fault_mark=((scen, blk), F32),
+            column=((whole, blk), jnp.int32),
+            zcat=((nreg, 2 * blk), BF16),
+            base=((STEPS, nreg), F32),
+            source_rows=((STEPS * nblk, blk), F32),
+        ),
+        hbm=dict(
+            end_a=line_a,
+            end_b=line_b,
+            conv=send_node,
+            fault_node=fault_node.reshape(1, scen),
+            inv=inv_flat,
+            amp=amp,
+            phase=phase,
+        ),
+        cost=(4e9, 2e7),
+    )
+    later, fault_mark = lax.optimization_barrier((into, tables.fault_mark))
+    far_in = shifted(later, "region", 1)
     if packed:
         shape = ((2, half, LANES), F32)
         couples = call(
             functools.partial(pair_body, regions // 2),
             "couple",
-            dict(even=even, odd=odd),
+            dict(even=even, odd=odd, after=fault_mark),
             {PAIR + str(k): shape for k in range(regions // 2)},
         )
         couples = [getattr(couples, PAIR + str(k)) for k in range(regions // 2)]
@@ -590,18 +628,11 @@
     if not packed:
         recv = jnp.concatenate(recv[::-1], axis=0).transpose(1, 2, 0, 3).reshape(2, half, width)
 
-    whole = points + blk
     model = call(
         functools.partial(rows_body, (nreg, nblk, lines, regions, cap, scen)),
         "rows",
-        {},
+        dict(row=tables.row, column=tables.column, source_rows=tables.source_rows),
         dict(
-            row=((1, whole), jnp.int32),
-            mark=((whole, blk), BF16),
-            fault_mark=((scen, blk), F32),
-            column=((points, blk), jnp.int32),
-            zcat=((nreg, 2 * blk), BF16),
-            base=((STEPS, nreg), F32),
             rows=((whole, 2 * blk), BF16),
             base_p=((STEPS, points), F32),
             fault_z=((scen, blk), F32),
@@ -609,27 +640,19 @@
             fault_ratio=((scen, blk), F32),
         ),
         hbm=dict(
-            end_a=line_a,
-            end_b=line_b,
-            conv=send_node,
-            fault_node=fault_node.reshape(1, scen),
             list_a=line_a,
             list_b=line_b,
             list_conv=send_node,
             list_fault=fault_node.reshape(1, scen),
-            inv=inv_blocks.reshape(nreg, blk),
-            amp=amp,
-            phase=phase,
+            inv=inv_flat,
             fault_step=fault_step.reshape(1, scen),
             fault_cond=fault_cond.reshape(1, scen),
         ),
         scalar=("list_a", "list_b", "list_conv", "list_fault"),
-        scratch=(
-            pltpu.VMEM((whole, blk), F32),
-            pltpu.VMEM((STEPS * nblk, blk), F32),
-        ),
+        scratch=(pltpu.VMEM((whole, blk), F32),),
         cost=(4e9, 2e7),
     )
+
     wave = ((2, scen, lines), F32)
     mades, backs, carry = {}, {}, {}
     squares = swap_near = swap_far = sent = None
@@ -649,11 +672,11 @@
         if t0 - maxd < 0:
             ins.update(hist_b=hist_ub)
         if pair:
-            ins.update(swap_near=swap_near, swap_far=swap_far, into_prev=sent, row=model.row)
+            ins.update(swap_near=swap_near, swap_far=swap_far, into_prev=sent, row=tables.row)
             ins.update(m_high=matrix.m_high, m_low=matrix.m_low, fault_p=matrix.fault_p)
         else:
             ins.update(far_in=far_in)
-            ins.update(row=model.row, mark=model.mark, rows=model.rows)
+            ins.update(row=tables.row, mark=tables.mark, rows=model.rows)
         first = max(0, pair - 3)
         ins.update(backs={k: v for k, v in backs.items() if k >= first})
         if not final:
@@ -712,11 +735,11 @@
         ins = dict(
             x=made.x,
             coef=made.coef,
-            fault_mark=model.fault_mark,
+            fault_mark=tables.fault_mark,
             fault_z=model.fault_z,
-            column=model.column,
-            zcat=model.zcat,
-            base=model.base,
+            column=tables.column,
+            zcat=tables.zcat,
+            base=tables.base,
         )
         if pair:
             ins.update(squares=squares)

time: 58.9 us -> 57.9 us (0.983)
  Pallas kernels: 24.8 us -> 26.3 us
  waiting for transfers between devices: 9.28 us -> 7.95 us
  starting transfers between devices: 23.8 us -> 22.5 us
    ppermute x4, waiting for transfers between devices: 2.48 us -> 0.97 us  [mirrored(): lax.ppermute(value, axis, [(source, source ^ offset) for source in range(...]
    pallas_call x13 -> x14, Pallas kernels: 24.8 us -> 26.3 us  [call(): pl.pallas_call(kernel, name=name, out_shape=[jax.ShapeDtypeStruct(*shape)...]
    ppermute x6, starting transfers between devices: 9.97 us -> 8.74 us  [swapped(): return lax.ppermute(value, axis, pairs)]
  transfers between devices with their start and end apart: 15 -> 15, of which waited for: 9 -> 10; matrix products, arithmetic and copies ran while one was open for 0% -> 0% of each run, Pallas kernels for 28% -> 31%
where the time goes in v5:
time: 57.9 us; the launch traced here: 57.6 us
  Pallas kernels  26.3 us (45%)
  starting transfers between devices  22.5 us (39%)
  waiting for transfers between devices  7.95 us (14%)
  between operations  0.79 us (1%)
    pallas_call x14, Pallas kernels, call(): pl.pallas_call(kernel, name=name, out_shape=[jax.ShapeDtypeStruct(*shape)...  26.3 us
    ppermute x6, starting transfers between devices, swapped(): return lax.ppermute(value, axis, pairs)  8.74 us
    ppermute x4, starting transfers between devices, mirrored(): lax.ppermute(value, axis, [(source, source ^ offset) for source in range(...  7.85 us
    ppermute x6, waiting for transfers between devices, swapped(): return lax.ppermute(value, axis, pairs)  5.59 us
    all_to_all x1, starting transfers between devices, per_device(): lax.all_to_all(current, 'region', split_axis=0, concat_axis=0, tiled=True)  3.96 us
    ppermute x3, starting transfers between devices, per_device(): parts.append(lax.ppermute(squares, 'scen', pairs))  1.92 us
  transfers between devices with their start and end apart: 15, of which 10 were waited for; matrix products, arithmetic and copies ran while one was open for 0% of the time, Pallas kernels for 31%

profile of v5, /device:TPU:0, one launch (start us, length us, event | category | flops | bytes accessed | tf_op | source)
XLA Modules:
  0.0 57.6 jit_solution(10332629633117054752)
XLA Ops:
  0.6 1.2 %start.1 = (f32[2,32,256]{2,1,0:T(8,128)S(1)}, f32[4,40,128]{2,1,0:T(8,128)S(1)}, f32[4,40,128]{2,1,0:T(8,128)S(1)}) custom-call(s32[1,128]{1,0:T(1,128)} %refs_6_.3, f32[6,128]{1,0:T(8,128)} %refs_1_.7, f32[2,32,128]{2,1,0:T(8,128)} %refs_2_.3, f32[1,6,32,256]{3,2,1,0:T(8,128)} %refs_8_.3, s32[1,256]{1,0:T(1,128)} %refs_6_.2), custom_call_target="tpu_custom_call" | custom-call | flops 1000000000 | bytes 4000000 | tf_op jit(solution)/shard_map/start/pallas_call | solution.py:108
  1.9 3.0 %collective-permute-start.1 = (f32[4,40,128]{2,1,0:T(8,128)S(1)}, f32[4,40,128]{2,1,0:T(8,128)S(1)}, u32[]{:S(2)}, u32[]{:S(2)}) collective-permute-start(f32[4,40,128]{2,1,0:T(8,128)S(1)} %get-tuple-element.73), channel_id=1, source_target_pairs={{0,4},{4,0},{8,12},{12,8},{16,20},{20,16},{24,28},{28,24},{1,5},{5... | collective-permute-start | bytes 245768 | tf_op jit(solution)/shard_map/ppermute | solution.py:32
  4.9 2.3 %tables.1 = (s32[1,1152]{1,0:T(1,128)S(1)}, bf16[1152,128]{1,0:T(8,128)(2,1)S(1)}, f32[32,128]{1,0:T(8,128)S(1)}, s32[1152,128]{1,0:T(8,128)S(1)}, bf16[3072,256...) custom-call(s32[1,256]{1,0:T(1,128)} %refs_3_.3, s32[1,256]{1,0:T(1,128)} %refs_4_.3, ...), custom_call_target="tpu_custom_call" | custom-call | flops 4000000000 | bytes 20000000 | tf_op jit(solution)/shard_map/tables/pallas_call | solution.py:108
  7.4 4.2 %collective-permute-start.2 = (f32[2,40,128]{2,1,0:T(8,128)S(1)}, f32[2,40,128]{2,1,0:T(8,128)S(1)}, u32[]{:S(2)}, u32[]{:S(2)}) collective-permute-start(f32[2,40,128]{2,1,0:T(8,128)S(1)} %get-tuple-element.74), channel_id=1, source_target_pairs={{0,24},{4,28},{8,16},{12,20},{16,8},{20,12},{24,0},{28,4},{1,25},{... | collective-permute-start | bytes 122888 | tf_op jit(solution)/shard_map/ppermute | solution.py:32
  12.2 3.3 %rows.1 = (bf16[1152,256]{1,0:T(8,128)(2,1)S(1)}, f32[8,1024]{1,0:T(8,128)S(1)}, f32[32,128]{1,0:T(8,128)S(1)}, f32[32,128]{1,0:T(8,128)S(1)}, f32[32,128]{1,0:T(8,128)S(1)}) custom-call(s32[1152,128]{1,0:T(8,128)S(1)} %get-tuple-element.61.refs_0_.refs_2_, s32[1,1152]{1,0:T(1,128)S(1)} %get-tuple-element.62.refs_1_.refs_14_.refs_18_.refs_19_.refs_17_, ...), custom_call_target="tpu_custom_call" | custom-call | flops 4000000000 | bytes 20000000 | tf_op jit(solution)/shard_map/rows/pallas_call | solution.py:108
  15.6 0.9 %collective-permute-done.3.refs_11_.refs_15_.refs_16_.refs_14_ = f32[2,40,128]{2,1,0:T(8,128)S(1)} collective-permute-done((f32[2,40,128]{2,1,0:T(8,128)S(1)}, f32[2,40,128]{2,1,0:T(8,128)S(1)}, u32[]{:S(2)}, u32[]{:S(2)}) %collective-permute-start.3) | collective-permute-done | bytes 40992 | tf_op jit(solution)/shard_map/ppermute | solution.py:32
  16.5 2.4 %advance.4 = (bf16[128,1024]{1,0:T(8,128)(2,1)S(1)}, f32[64,128]{1,0:T(8,128)S(1)}, f32[2,32,256]{2,1,0:T(8,128)S(1)}, f32[2,32,256]{2,1,0:T(8,128)S(1)}, f32[2,...) custom-call(f32[1,256]{1,0:T(1,128)S(1)} %copy-done.2, ...), custom_call_target="tpu_custom_call" | custom-call | flops 1000000000 | bytes 4000000 | tf_op jit(solution)/shard_map/advance/pallas_call | solution.py:108
  18.9 3.9 %collective-permute-start.5 = (f32[2,32,256]{2,1,0:T(8,128)S(1)}, f32[2,32,256]{2,1,0:T(8,128)S(1)}, u32[]{:S(2)}, u32[]{:S(2)}) collective-permute-start(f32[2,32,256]{2,1,0:T(8,128)S(1)} %get-tuple-element.85), channel_id=1, source_target_pairs={{4,8},{8,4},{12,16},{16,12},{20,24},{24,20},{28,0},{0,28},{5,9},{9... | collective-permute-start | bytes 196616 | tf_op jit(solution)/shard_map/ppermute | solution.py:41
  22.8 2.8 %full.4.refs_5_ = f32[1,3072]{1,0:T(1,128)S(1)} custom-call(f32[8,3072]{1,0:T(8,128)S(1)} %get-tuple-element.60.refs_0_, f32[64,128]{1,0:T(8,128)S(1)} %get-tuple-element.104.refs_1_, s32[1152,128]{1,0:T(8,128)S(1)} %get-tuple-element.61.refs_0_.refs_2_, f32[32,128]{1,0:T(8,128)S(1)} %get-tuple-element.71.refs_0_.refs_3_, ...), custom_call_target="tpu_custom_call" | custom-call | flops 4000000000 | bytes 10000000 | tf_op jit(solution)/shard_map/full/pallas_call | solution.py:108
  26.0 1.1 %collective-permute-done.6.refs_21_ = f32[2,32,256]{2,1,0:T(8,128)S(1)} collective-permute-done((f32[2,32,256]{2,1,0:T(8,128)S(1)}, f32[2,32,256]{2,1,0:T(8,128)S(1)}, u32[]{:S(2)}, u32[]{:S(2)}) %collective-permute-start.6) | collective-permute-done | bytes 65568 | tf_op jit(solution)/shard_map/ppermute | solution.py:41
  27.1 1.2 %advance.5 = (bf16[128,1024]{1,0:T(8,128)(2,1)S(1)}, f32[64,128]{1,0:T(8,128)S(1)}, f32[2,32,256]{2,1,0:T(8,128)S(1)}, f32[2,32,256]{2,1,0:T(8,128)S(1)}, f32[2,...) custom-call(f32[1,256]{1,0:T(1,128)S(1)} %copy-done.2, ...), custom_call_target="tpu_custom_call" | custom-call | flops 1000000000 | bytes 4000000 | tf_op jit(solution)/shard_map/advance/pallas_call | solution.py:108
  28.3 2.8 %collective-permute-start.7 = (f32[2,32,256]{2,1,0:T(8,128)S(1)}, f32[2,32,256]{2,1,0:T(8,128)S(1)}, u32[]{:S(2)}, u32[]{:S(2)}) collective-permute-start(f32[2,32,256]{2,1,0:T(8,128)S(1)} %get-tuple-element.92), channel_id=1, source_target_pairs={{4,8},{8,4},{12,16},{16,12},{20,24},{24,20},{28,0},{0,28},{5,9},{9... | collective-permute-start | bytes 196616 | tf_op jit(solution)/shard_map/ppermute | solution.py:41
  31.0 2.9 %full.5.refs_5_ = f32[1,3072]{1,0:T(1,128)S(1)} custom-call(f32[8,3072]{1,0:T(8,128)S(1)} %get-tuple-element.60.refs_0_, f32[64,128]{1,0:T(8,128)S(1)} %get-tuple-element.103.refs_1_, s32[1152,128]{1,0:T(8,128)S(1)} %get-tuple-element.61.refs_0_.refs_2_, f32[32,128]{1,0:T(8,128)S(1)} %get-tuple-element.71.refs_0_.refs_3_, ...), custom_call_target="tpu_custom_call" | custom-call | flops 4000000000 | bytes 10000000 | tf_op jit(solution)/shard_map/full/pallas_call | solution.py:108
  33.9 1.5 %collective-permute-done.7.refs_21_ = f32[2,32,256]{2,1,0:T(8,128)S(1)} collective-permute-done((f32[2,32,256]{2,1,0:T(8,128)S(1)}, f32[2,32,256]{2,1,0:T(8,128)S(1)}, u32[]{:S(2)}, u32[]{:S(2)}) %collective-permute-start.7) | collective-permute-done | bytes 65568 | tf_op jit(solution)/shard_map/ppermute | solution.py:41
  36.0 1.2 %advance.6 = (bf16[128,1024]{1,0:T(8,128)(2,1)S(1)}, f32[64,128]{1,0:T(8,128)S(1)}, f32[2,32,256]{2,1,0:T(8,128)S(1)}, f32[2,32,256]{2,1,0:T(8,128)S(1)}, f32[2,...) custom-call(f32[1,256]{1,0:T(1,128)S(1)} %copy-done.2, f32[1,256]{1,0:T(1,128)S(1)} %copy-done.3, ...), custom_call_target="tpu_custom_call" | custom-call | flops 1000000000 | bytes 4000000 | tf_op jit(solution)/shard_map/advance/pallas_call | solution.py:108
  37.2 2.1 %collective-permute-start.9 = (f32[2,32,256]{2,1,0:T(8,128)S(1)}, f32[2,32,256]{2,1,0:T(8,128)S(1)}, u32[]{:S(2)}, u32[]{:S(2)}) collective-permute-start(f32[2,32,256]{2,1,0:T(8,128)S(1)} %get-tuple-element.98), channel_id=1, source_target_pairs={{4,8},{8,4},{12,16},{16,12},{20,24},{24,20},{28,0},{0,28},{5,9},{9... | collective-permute-start | bytes 196616 | tf_op jit(solution)/shard_map/ppermute | solution.py:41
  39.3 2.9 %full.6.refs_5_ = f32[1,3072]{1,0:T(1,128)S(1)} custom-call(f32[8,3072]{1,0:T(8,128)S(1)} %get-tuple-element.60.refs_0_, f32[64,128]{1,0:T(8,128)S(1)} %get-tuple-element.102.refs_1_, s32[1152,128]{1,0:T(8,128)S(1)} %get-tuple-element.61.refs_0_.refs_2_, f32[32,128]{1,0:T(8,128)S(1)} %get-tuple-element.71.refs_0_.refs_3_, ...), custom_call_target="tpu_custom_call" | custom-call | flops 4000000000 | bytes 10000000 | tf_op jit(solution)/shard_map/full/pallas_call | solution.py:108
  42.1 2.1 %collective-permute-done.9.refs_19_ = f32[2,32,256]{2,1,0:T(8,128)S(1)} collective-permute-done((f32[2,32,256]{2,1,0:T(8,128)S(1)}, f32[2,32,256]{2,1,0:T(8,128)S(1)}, u32[]{:S(2)}, u32[]{:S(2)}) %collective-permute-start.9) | collective-permute-done | bytes 65568 | tf_op jit(solution)/shard_map/ppermute | solution.py:41
  44.2 1.7 %advance.7 = (bf16[128,1024]{1,0:T(8,128)(2,1)S(1)}, f32[64,128]{1,0:T(8,128)S(1)}, f32[8,16,128]{2,1,0:T(8,128)}) custom-call(f32[1,256]{1,0:T(1,128)S(1)} %copy-done.2, f32[1,256]{1,0:T(1,128)S(1)} %copy-done.3, f32[2,32,256]{2,1,0:T(8,128)S(1)} %get-tuple-element.87.refs_2_, f32[2,32,256]{2,1,0:T(8,128)S(1)} %get-tuple-element.94.refs_3_, ...), custom_call_target="tpu_custom_call" | custom-call | flops 1000000000 | bytes 4000000 | tf_op jit(solution)/shard_map/advance/pallas_call | solution.py:108
  45.9 4.0 %all-to-all-start = ((f32[8,16,128]{2,1,0:T(8,128)}), f32[8,16,128]{2,1,0:T(8,128)S(1)}, u32[]{:S(2)}, u32[]{:S(2)}) async-start(f32[8,16,128]{2,1,0:T(8,128)} %get-tuple-element.114), calls=%async_computation | async-start | bytes 131072 | tf_op jit(solution)/shard_map/all_to_all | solution.py:729
  49.9 2.8 %full.7 = (f32[1,3072]{1,0:T(1,128)S(1)}, f32[32,3072]{1,0:T(8,128)S(1)}) custom-call(f32[8,3072]{1,0:T(8,128)S(1)} %get-tuple-element.60.refs_0_, f32[64,128]{1,0:T(8,128)S(1)} %get-tuple-element.100.refs_1_, s32[1152,128]{1,0:T(8,128)S(1)} %get-tuple-element.61.refs_0_.refs_2_, f32[32,128]{1,0:T(8,128)S(1)} %get-tuple-element.71.refs_0_.refs_3_, ...), custom_call_target="tpu_custom_call" | custom-call | flops 4000000000 | bytes 10000000 | tf_op jit(solution)/shard_map/full/pallas_call | solution.py:108
  52.8 1.6 %collective-permute-start.12 = (f32[1,3072]{1,0:T(1,128)S(1)}, f32[1,3072]{1,0:T(1,128)S(1)}, u32[]{:S(2)}, u32[]{:S(2)}) collective-permute-start(f32[1,3072]{1,0:T(1,128)S(1)} %get-tuple-element.113.refs_1_), channel_id=1, source_target_pairs={{0,2},{1,3},{2,0},{3,1},{4,6},{5,7},{6,4},{7,5},{8,10},{9,11},{10,... | collective-permute-start | bytes 36872 | tf_op jit(solution)/shard_map/ppermute | solution.py:761
  54.6 0.8 %place.1 = (f32[1,128]{1,0:T(1,128)S(1)}, f32[32,3072]{1,0:T(8,128)}) custom-call(f32[32,3072]{1,0:T(8,128)S(1)} %get-tuple-element.110.refs_0_), custom_call_target="tpu_custom_call" | custom-call | flops 1000000000 | bytes 4000000 | tf_op jit(solution)/shard_map/place/pallas_call | solution.py:108
  56.8 0.8 %finish.1 = (f32[1,3072]{1,0:T(1,128)}, f32[32,128]{1,0:T(8,128)}) custom-call(f32[1,128]{1,0:T(1,128)S(1)} %get-tuple-element.112.refs_0_, f32[1,3072]{1,0:T(1,128)S(1)} %get-tuple-element.113.refs_1_, f32[1,3072]{1,0:T(1,128)S(1)} %collective-permute-done.11.refs_2_, f32[1,3072]{1,0:T(1,128)S(1)} %collective-permute-done.12.refs_3_, ...), custom_call_target="tpu_custom_call" | custom-call | flops 1000000000 | bytes 4000000 | tf_op jit(solution)/shard_map/finish/pallas_call | solution.py:108
  (32 shorter events, 3.5 us)
Async XLA Ops:
  1.9 5.5 %collective-permute-start.1 = (f32[4,40,128]{2,1,0:T(8,128)S(1)}, f32[4,40,128]{2,1,0:T(8,128)S(1)}, u32[]{:S(2)}, u32[]{:S(2)}) collective-permute-start(f32[4,40,128]{2,1,0:T(8,128)S(1)} %get-tuple-element.73), channel_id=1, source_target_pairs={{0,4},{4,0},{8,12},{12,8},{16,20},{20,16},{24,28},{28,24},{1,5},{5... | collective-permute-start | bytes 245768 | tf_op jit(solution)/shard_map/ppermute | solution.py:32
  7.2 8.3 %collective-permute-start = (f32[2,32,256]{2,1,0:T(8,128)S(1)}, f32[2,32,256]{2,1,0:T(8,128)S(1)}, u32[]{:S(2)}, u32[]{:S(2)}) collective-permute-start(f32[2,32,256]{2,1,0:T(8,128)S(1)} %get-tuple-element.67.refs_10_), channel_id=1, source_target_pairs={{0,4},{4,8},{8,12},{12,16},{16,20},{20,24},{24,28},{28,0},{1,5},{5... | collective-permute-start | bytes 196616 | tf_op jit(solution)/shard_map/ppermute | solution.py:27
  7.4 8.2 %collective-permute-start.2 = (f32[2,40,128]{2,1,0:T(8,128)S(1)}, f32[2,40,128]{2,1,0:T(8,128)S(1)}, u32[]{:S(2)}, u32[]{:S(2)}) collective-permute-start(f32[2,40,128]{2,1,0:T(8,128)S(1)} %get-tuple-element.74), channel_id=1, source_target_pairs={{0,24},{4,28},{8,16},{12,20},{16,8},{20,12},{24,0},{28,4},{1,25},{... | collective-permute-start | bytes 122888 | tf_op jit(solution)/shard_map/ppermute | solution.py:32
  11.5 4.9 %collective-permute-start.3 = (f32[2,40,128]{2,1,0:T(8,128)S(1)}, f32[2,40,128]{2,1,0:T(8,128)S(1)}, u32[]{:S(2)}, u32[]{:S(2)}) collective-permute-start(f32[2,40,128]{2,1,0:T(8,128)S(1)} %get-tuple-element.75), channel_id=1, source_target_pairs={{0,16},{4,20},{8,24},{12,28},{16,0},{20,4},{24,8},{28,12},{1,17},{... | collective-permute-start | bytes 122888 | tf_op jit(solution)/shard_map/ppermute | solution.py:32
  11.6 4.9 %collective-permute-start.4 = (f32[2,40,128]{2,1,0:T(8,128)S(1)}, f32[2,40,128]{2,1,0:T(8,128)S(1)}, u32[]{:S(2)}, u32[]{:S(2)}) collective-permute-start(f32[2,40,128]{2,1,0:T(8,128)S(1)} %get-tuple-element.76), channel_id=1, source_target_pairs={{0,8},{4,12},{8,0},{12,4},{16,24},{20,28},{24,16},{28,20},{1,9},{5... | collective-permute-start | bytes 122888 | tf_op jit(solution)/shard_map/ppermute | solution.py:32
  12.2 4.3 %copy-start = (f32[1,6,32,256]{3,2,1,0:T(8,128)S(1)}, f32[1,6,32,256]{3,2,1,0:T(8,128)}, u32[]{:S(2)}) copy-start(f32[1,6,32,256]{3,2,1,0:T(8,128)} %refs_9_.3) | copy-start | bytes 589828
  12.2 4.3 %copy-start.1 = (f32[1,6,32,256]{3,2,1,0:T(8,128)S(1)}, f32[1,6,32,256]{3,2,1,0:T(8,128)}, u32[]{:S(2)}) copy-start(f32[1,6,32,256]{3,2,1,0:T(8,128)} %refs_8_.3) | copy-start | bytes 589828
  12.2 4.3 %copy-start.2 = (f32[1,256]{1,0:T(1,128)S(1)}, f32[1,256]{1,0:T(1,128)}, u32[]{:S(2)}) copy-start(f32[1,256]{1,0:T(1,128)} %refs_0_.11) | copy-start | bytes 3076
  12.2 4.3 %copy-start.3 = (f32[1,256]{1,0:T(1,128)S(1)}, f32[1,256]{1,0:T(1,128)}, u32[]{:S(2)}) copy-start(f32[1,256]{1,0:T(1,128)} %refs_1_.11) | copy-start | bytes 3076
  12.2 4.3 %copy-start.4 = (s32[1,256]{1,0:T(1,128)S(1)}, s32[1,256]{1,0:T(1,128)}, u32[]{:S(2)}) copy-start(s32[1,256]{1,0:T(1,128)} %refs_6_.2) | copy-start | bytes 3076
  18.9 7.0 %collective-permute-start.5 = (f32[2,32,256]{2,1,0:T(8,128)S(1)}, f32[2,32,256]{2,1,0:T(8,128)S(1)}, u32[]{:S(2)}, u32[]{:S(2)}) collective-permute-start(f32[2,32,256]{2,1,0:T(8,128)S(1)} %get-tuple-element.85), channel_id=1, source_target_pairs={{4,8},{8,4},{12,16},{16,12},{20,24},{24,20},{28,0},{0,28},{5,9},{9... | collective-permute-start | bytes 196616 | tf_op jit(solution)/shard_map/ppermute | solution.py:41
  22.8 4.3 %collective-permute-start.6 = (f32[2,32,256]{2,1,0:T(8,128)S(1)}, f32[2,32,256]{2,1,0:T(8,128)S(1)}, u32[]{:S(2)}, u32[]{:S(2)}) collective-permute-start(f32[2,32,256]{2,1,0:T(8,128)S(1)} %get-tuple-element.86), channel_id=1, source_target_pairs={{0,4},{4,0},{8,12},{12,8},{16,20},{20,16},{24,28},{28,24},{1,5},{5... | collective-permute-start | bytes 196616 | tf_op jit(solution)/shard_map/ppermute | solution.py:41
  28.3 7.1 %collective-permute-start.7 = (f32[2,32,256]{2,1,0:T(8,128)S(1)}, f32[2,32,256]{2,1,0:T(8,128)S(1)}, u32[]{:S(2)}, u32[]{:S(2)}) collective-permute-start(f32[2,32,256]{2,1,0:T(8,128)S(1)} %get-tuple-element.92), channel_id=1, source_target_pairs={{4,8},{8,4},{12,16},{16,12},{20,24},{24,20},{28,0},{0,28},{5,9},{9... | collective-permute-start | bytes 196616 | tf_op jit(solution)/shard_map/ppermute | solution.py:41
  31.0 5.0 %collective-permute-start.8 = (f32[2,32,256]{2,1,0:T(8,128)S(1)}, f32[2,32,256]{2,1,0:T(8,128)S(1)}, u32[]{:S(2)}, u32[]{:S(2)}) collective-permute-start(f32[2,32,256]{2,1,0:T(8,128)S(1)} %get-tuple-element.93), channel_id=1, source_target_pairs={{0,4},{4,0},{8,12},{12,8},{16,20},{20,16},{24,28},{28,24},{1,5},{5... | collective-permute-start | bytes 196616 | tf_op jit(solution)/shard_map/ppermute | solution.py:41
  37.2 7.1 %collective-permute-start.9 = (f32[2,32,256]{2,1,0:T(8,128)S(1)}, f32[2,32,256]{2,1,0:T(8,128)S(1)}, u32[]{:S(2)}, u32[]{:S(2)}) collective-permute-start(f32[2,32,256]{2,1,0:T(8,128)S(1)} %get-tuple-element.98), channel_id=1, source_target_pairs={{4,8},{8,4},{12,16},{16,12},{20,24},{24,20},{28,0},{0,28},{5,9},{9... | collective-permute-start | bytes 196616 | tf_op jit(solution)/shard_map/ppermute | solution.py:41
  39.2 5.0 %collective-permute-start.10 = (f32[2,32,256]{2,1,0:T(8,128)S(1)}, f32[2,32,256]{2,1,0:T(8,128)S(1)}, u32[]{:S(2)}, u32[]{:S(2)}) collective-permute-start(f32[2,32,256]{2,1,0:T(8,128)S(1)} %get-tuple-element.99), channel_id=1, source_target_pairs={{0,4},{4,0},{8,12},{12,8},{16,20},{20,16},{24,28},{28,24},{1,5},{5... | collective-permute-start | bytes 196616 | tf_op jit(solution)/shard_map/ppermute | solution.py:41
  45.9 10.9 %all-to-all-start = ((f32[8,16,128]{2,1,0:T(8,128)}), f32[8,16,128]{2,1,0:T(8,128)S(1)}, u32[]{:S(2)}, u32[]{:S(2)}) async-start(f32[8,16,128]{2,1,0:T(8,128)} %get-tuple-element.114), calls=%async_computation | async-start | bytes 131072 | tf_op jit(solution)/shard_map/all_to_all | solution.py:729
  52.7 4.1 %copy-start.5 = (s32[1,128]{1,0:T(1,128)S(1)}, s32[1,128]{1,0:T(1,128)}, u32[]{:S(2)}) copy-start(s32[1,128]{1,0:T(1,128)} %refs_6_.3) | copy-start | bytes 1540
  52.7 3.2 %collective-permute-start.13 = (f32[1,3072]{1,0:T(1,128)S(1)}, f32[1,3072]{1,0:T(1,128)S(1)}, u32[]{:S(2)}, u32[]{:S(2)}) collective-permute-start(f32[1,3072]{1,0:T(1,128)S(1)} %get-tuple-element.113.refs_1_), channel_id=1, source_target_pairs={{0,3},{1,2},{2,1},{3,0},{4,7},{5,6},{6,5},{7,4},{8,11},{9,10},{10,... | collective-permute-start | bytes 36872 | tf_op jit(solution)/shard_map/ppermute | solution.py:761
  52.8 3.8 %collective-permute-start.12 = (f32[1,3072]{1,0:T(1,128)S(1)}, f32[1,3072]{1,0:T(1,128)S(1)}, u32[]{:S(2)}, u32[]{:S(2)}) collective-permute-start(f32[1,3072]{1,0:T(1,128)S(1)} %get-tuple-element.113.refs_1_), channel_id=1, source_target_pairs={{0,2},{1,3},{2,0},{3,1},{4,6},{5,7},{6,4},{7,5},{8,10},{9,11},{10,... | collective-permute-start | bytes 36872 | tf_op jit(solution)/shard_map/ppermute | solution.py:761
  54.4 2.2 %collective-permute-start.11 = (f32[1,3072]{1,0:T(1,128)S(1)}, f32[1,3072]{1,0:T(1,128)S(1)}, u32[]{:S(2)}, u32[]{:S(2)}) collective-permute-start(f32[1,3072]{1,0:T(1,128)S(1)} %get-tuple-element.113.refs_1_), channel_id=1, source_target_pairs={{0,1},{1,0},{2,3},{3,2},{4,5},{5,4},{6,7},{7,6},{8,9},{9,8},{10,11... | collective-permute-start | bytes 36872 | tf_op jit(solution)/shard_map/ppermute | solution.py:761

commit v6 on v5

--- a/solution.py
+++ b/solution.py
@@ -298,6 +298,7 @@
     o.fault_ratio[...] = jnp.where(
         closes <= iota((scen, blk), 1).astype(F32), jnp.broadcast_to(ratio, (scen, blk)), 0.0
     )
+    between_body(points, scen, Space(row=i.row, mark=i.mark, rows=o.rows), o)
 
 
 def between_body(points, scen, i, o):
@@ -354,9 +355,7 @@
         return i.made[t // 2][t % 2]
 
     points = 2 * lines + width
-    known = i if pair else o
-    if not pair:
-        between_body(points, scen, i, o)
+    known = i
     live = i.row[:, 2 * lines : 2 * lines + width] >= 0
     if packed:
         recv = i.recv[::-1]
@@ -631,13 +630,21 @@
     model = call(
         functools.partial(rows_body, (nreg, nblk, lines, regions, cap, scen)),
         "rows",
-        dict(row=tables.row, column=tables.column, source_rows=tables.source_rows),
+        dict(
+            row=tables.row,
+            mark=tables.mark,
+            column=tables.column,
+            source_rows=tables.source_rows,
+        ),
         dict(
             rows=((whole, 2 * blk), BF16),
             base_p=((STEPS, points), F32),
             fault_z=((scen, blk), F32),
             fault_base=((scen, blk), F32),
             fault_ratio=((scen, blk), F32),
+            m_high=((points, points), BF16),
+            m_low=((points, points), BF16),
+            fault_p=((scen, points), F32),
         ),
         hbm=dict(
             list_a=line_a,
@@ -665,6 +672,9 @@
             admit=line_yc,
             recv=recv,
             base_p=model.base_p,
+            m_high=model.m_high,
+            m_low=model.m_low,
+            fault_p=model.fault_p,
             fault_base=model.fault_base,
             fault_ratio=model.fault_ratio,
             **carry,
@@ -673,10 +683,9 @@
             ins.update(hist_b=hist_ub)
         if pair:
             ins.update(swap_near=swap_near, swap_far=swap_far, into_prev=sent, row=tables.row)
-            ins.update(m_high=matrix.m_high, m_low=matrix.m_low, fault_p=matrix.fault_p)
         else:
             ins.update(far_in=far_in)
-            ins.update(row=tables.row, mark=tables.mark, rows=model.rows)
+            ins.update(row=tables.row)
         first = max(0, pair - 3)
         ins.update(backs={k: v for k, v in backs.items() if k >= first})
         if not final:
@@ -695,12 +704,6 @@
                 outs.update(out=wave, into=wave)
             if pair:
                 outs.update(back=wave)
-            else:
-                outs.update(
-                    m_high=((points, points), BF16),
-                    m_low=((points, points), BF16),
-                    fault_p=((scen, points), F32),
-                )
         else:
             shape = (regions, scen // 2, LANES) if packed else (scen, width)
             outs.update(current=(shape, F32))
@@ -710,8 +713,6 @@
             ins,
             outs,
         )
-        if not pair:
-            matrix = made
         if not final:
             sent = into
             if t0 + 4 < STEPS:

time: 57.9 us -> 57.8 us (level)
  starting transfers between devices: 22.5 us -> 23.4 us
  waiting for transfers between devices: 7.95 us -> 7.06 us
    ppermute x4, waiting for transfers between devices: 0.97 us -> 0.08 us  [mirrored(): lax.ppermute(value, axis, [(source, source ^ offset) for source in range(...]
    ppermute x6, starting transfers between devices: 8.74 us -> 9.6 us  [swapped(): return lax.ppermute(value, axis, pairs)]
  transfers between devices with their start and end apart: 15 -> 15, of which waited for: 10 -> 8; matrix products, arithmetic and copies ran while one was open for 0% -> 0% of each run, Pallas kernels for 31% -> 33%
where the time goes in v6:
time: 57.8 us; the launch traced here: 57.5 us
  Pallas kernels  26.2 us (45%)
  starting transfers between devices  23.4 us (40%)
  waiting for transfers between devices  7.06 us (12%)
  between operations  0.82 us (1%)
    pallas_call x14, Pallas kernels, call(): pl.pallas_call(kernel, name=name, out_shape=[jax.ShapeDtypeStruct(*shape)...  26.2 us
    ppermute x6, starting transfers between devices, swapped(): return lax.ppermute(value, axis, pairs)  9.6 us
    ppermute x4, starting transfers between devices, mirrored(): lax.ppermute(value, axis, [(source, source ^ offset) for source in range(...  7.85 us
    ppermute x6, waiting for transfers between devices, swapped(): return lax.ppermute(value, axis, pairs)  5.58 us
    all_to_all x1, starting transfers between devices, per_device(): lax.all_to_all(current, 'region', split_axis=0, concat_axis=0, tiled=True)  3.96 us
    ppermute x3, starting transfers between devices, per_device(): parts.append(lax.ppermute(squares, 'scen', pairs))  1.92 us
  transfers between devices with their start and end apart: 15, of which 8 were waited for; matrix products, arithmetic and copies ran while one was open for 0% of the time, Pallas kernels for 33%

profile of v6, /device:TPU:0, one launch (start us, length us, event | category | flops | bytes accessed | tf_op | source)
XLA Modules:
  0.0 57.5 jit_solution(1241685151935520555)
XLA Ops:
  0.6 1.2 %start.1 = (f32[2,32,256]{2,1,0:T(8,128)S(1)}, f32[4,40,128]{2,1,0:T(8,128)S(1)}, f32[4,40,128]{2,1,0:T(8,128)S(1)}) custom-call(s32[1,128]{1,0:T(1,128)} %refs_6_.5, f32[6,128]{1,0:T(8,128)} %refs_1_.7, f32[2,32,128]{2,1,0:T(8,128)} %refs_2_.3, f32[1,6,32,256]{3,2,1,0:T(8,128)} %refs_8_.3, s32[1,256]{1,0:T(1,128)} %refs_6_.4), custom_call_target="tpu_custom_call" | custom-call | flops 1000000000 | bytes 4000000 | tf_op jit(solution)/shard_map/start/pallas_call | solution.py:108
  1.9 3.0 %collective-permute-start.1 = (f32[4,40,128]{2,1,0:T(8,128)S(1)}, f32[4,40,128]{2,1,0:T(8,128)S(1)}, u32[]{:S(2)}, u32[]{:S(2)}) collective-permute-start(f32[4,40,128]{2,1,0:T(8,128)S(1)} %get-tuple-element.75), channel_id=1, source_target_pairs={{0,4},{4,0},{8,12},{12,8},{16,20},{20,16},{24,28},{28,24},{1,5},{5... | collective-permute-start | bytes 245768 | tf_op jit(solution)/shard_map/ppermute | solution.py:32
  4.9 2.3 %tables.1 = (s32[1,1152]{1,0:T(1,128)S(1)}, bf16[1152,128]{1,0:T(8,128)(2,1)S(1)}, f32[32,128]{1,0:T(8,128)S(1)}, s32[1152,128]{1,0:T(8,128)S(1)}, bf16[3072,256...) custom-call(s32[1,256]{1,0:T(1,128)} %refs_4_.3, s32[1,256]{1,0:T(1,128)} %refs_5_.2, ...), custom_call_target="tpu_custom_call" | custom-call | flops 4000000000 | bytes 20000000 | tf_op jit(solution)/shard_map/tables/pallas_call | solution.py:108
  7.4 4.2 %collective-permute-start.2 = (f32[2,40,128]{2,1,0:T(8,128)S(1)}, f32[2,40,128]{2,1,0:T(8,128)S(1)}, u32[]{:S(2)}, u32[]{:S(2)}) collective-permute-start(f32[2,40,128]{2,1,0:T(8,128)S(1)} %get-tuple-element.76), channel_id=1, source_target_pairs={{0,24},{4,28},{8,16},{12,20},{16,8},{20,12},{24,0},{28,4},{1,25},{... | collective-permute-start | bytes 122888 | tf_op jit(solution)/shard_map/ppermute | solution.py:32
  11.6 0.6 %collective-permute-start.4 = (f32[2,40,128]{2,1,0:T(8,128)S(1)}, f32[2,40,128]{2,1,0:T(8,128)S(1)}, u32[]{:S(2)}, u32[]{:S(2)}) collective-permute-start(f32[2,40,128]{2,1,0:T(8,128)S(1)} %get-tuple-element.78), channel_id=1, source_target_pairs={{0,8},{4,12},{8,0},{12,4},{16,24},{20,28},{24,16},{28,20},{1,9},{5... | collective-permute-start | bytes 122888 | tf_op jit(solution)/shard_map/ppermute | solution.py:32
  12.2 4.4 %rows.1 = (bf16[1152,256]{1,0:T(8,128)(2,1)}, f32[8,1024]{1,0:T(8,128)S(1)}, f32[32,128]{1,0:T(8,128)S(1)}, f32[32,128]{1,0:T(8,128)S(1)}, f32[32,128]{1,0:T(8,1...) custom-call(s32[1152,128]{1,0:T(8,128)S(1)} %get-tuple-element.60.refs_0_.refs_2_, ...), custom_call_target="tpu_custom_call" | custom-call | flops 4000000000 | bytes 20000000 | tf_op jit(solution)/shard_map/rows/pallas_call | solution.py:108
  16.7 1.2 %advance.4 = (bf16[128,1024]{1,0:T(8,128)(2,1)S(1)}, f32[64,128]{1,0:T(8,128)S(1)}, f32[2,32,256]{2,1,0:T(8,128)S(1)}, f32[2,32,256]{2,1,0:T(8,128)S(1)}, f32[2,...) custom-call(f32[1,256]{1,0:T(1,128)S(1)} %copy-done.2, ...), custom_call_target="tpu_custom_call" | custom-call | flops 1000000000 | bytes 4000000 | tf_op jit(solution)/shard_map/advance/pallas_call | solution.py:108
  17.9 4.7 %collective-permute-start.5 = (f32[2,32,256]{2,1,0:T(8,128)S(1)}, f32[2,32,256]{2,1,0:T(8,128)S(1)}, u32[]{:S(2)}, u32[]{:S(2)}) collective-permute-start(f32[2,32,256]{2,1,0:T(8,128)S(1)} %get-tuple-element.83), channel_id=1, source_target_pairs={{4,8},{8,4},{12,16},{16,12},{20,24},{24,20},{28,0},{0,28},{5,9},{9... | collective-permute-start | bytes 196616 | tf_op jit(solution)/shard_map/ppermute | solution.py:41
  22.6 2.8 %full.4.refs_5_ = f32[1,3072]{1,0:T(1,128)S(1)} custom-call(f32[8,3072]{1,0:T(8,128)S(1)} %get-tuple-element.59.refs_0_, f32[64,128]{1,0:T(8,128)S(1)} %get-tuple-element.102.refs_1_, s32[1152,128]{1,0:T(8,128)S(1)} %get-tuple-element.60.refs_0_.refs_2_, f32[32,128]{1,0:T(8,128)S(1)} %get-tuple-element.73.refs_0_.refs_3_, ...), custom_call_target="tpu_custom_call" | custom-call | flops 4000000000 | bytes 10000000 | tf_op jit(solution)/shard_map/full/pallas_call | solution.py:108
  25.5 1.4 %collective-permute-done.6.refs_21_ = f32[2,32,256]{2,1,0:T(8,128)S(1)} collective-permute-done((f32[2,32,256]{2,1,0:T(8,128)S(1)}, f32[2,32,256]{2,1,0:T(8,128)S(1)}, u32[]{:S(2)}, u32[]{:S(2)}) %collective-permute-start.6) | collective-permute-done | bytes 65568 | tf_op jit(solution)/shard_map/ppermute | solution.py:41
  26.9 1.2 %advance.5 = (bf16[128,1024]{1,0:T(8,128)(2,1)S(1)}, f32[64,128]{1,0:T(8,128)S(1)}, f32[2,32,256]{2,1,0:T(8,128)S(1)}, f32[2,32,256]{2,1,0:T(8,128)S(1)}, f32[2,...) custom-call(f32[1,256]{1,0:T(1,128)S(1)} %copy-done.2, ...), custom_call_target="tpu_custom_call" | custom-call | flops 1000000000 | bytes 4000000 | tf_op jit(solution)/shard_map/advance/pallas_call | solution.py:108
  28.1 2.8 %collective-permute-start.7 = (f32[2,32,256]{2,1,0:T(8,128)S(1)}, f32[2,32,256]{2,1,0:T(8,128)S(1)}, u32[]{:S(2)}, u32[]{:S(2)}) collective-permute-start(f32[2,32,256]{2,1,0:T(8,128)S(1)} %get-tuple-element.90), channel_id=1, source_target_pairs={{4,8},{8,4},{12,16},{16,12},{20,24},{24,20},{28,0},{0,28},{5,9},{9... | collective-permute-start | bytes 196616 | tf_op jit(solution)/shard_map/ppermute | solution.py:41
  30.9 2.9 %full.5.refs_5_ = f32[1,3072]{1,0:T(1,128)S(1)} custom-call(f32[8,3072]{1,0:T(8,128)S(1)} %get-tuple-element.59.refs_0_, f32[64,128]{1,0:T(8,128)S(1)} %get-tuple-element.101.refs_1_, s32[1152,128]{1,0:T(8,128)S(1)} %get-tuple-element.60.refs_0_.refs_2_, f32[32,128]{1,0:T(8,128)S(1)} %get-tuple-element.73.refs_0_.refs_3_, ...), custom_call_target="tpu_custom_call" | custom-call | flops 4000000000 | bytes 10000000 | tf_op jit(solution)/shard_map/full/pallas_call | solution.py:108
  33.7 1.5 %collective-permute-done.7.refs_21_ = f32[2,32,256]{2,1,0:T(8,128)S(1)} collective-permute-done((f32[2,32,256]{2,1,0:T(8,128)S(1)}, f32[2,32,256]{2,1,0:T(8,128)S(1)}, u32[]{:S(2)}, u32[]{:S(2)}) %collective-permute-start.7) | collective-permute-done | bytes 65568 | tf_op jit(solution)/shard_map/ppermute | solution.py:41
  35.8 1.2 %advance.6 = (bf16[128,1024]{1,0:T(8,128)(2,1)S(1)}, f32[64,128]{1,0:T(8,128)S(1)}, f32[2,32,256]{2,1,0:T(8,128)S(1)}, f32[2,32,256]{2,1,0:T(8,128)S(1)}, f32[2,...) custom-call(f32[1,256]{1,0:T(1,128)S(1)} %copy-done.2, f32[1,256]{1,0:T(1,128)S(1)} %copy-done.3, ...), custom_call_target="tpu_custom_call" | custom-call | flops 1000000000 | bytes 4000000 | tf_op jit(solution)/shard_map/advance/pallas_call | solution.py:108
  37.0 2.1 %collective-permute-start.9 = (f32[2,32,256]{2,1,0:T(8,128)S(1)}, f32[2,32,256]{2,1,0:T(8,128)S(1)}, u32[]{:S(2)}, u32[]{:S(2)}) collective-permute-start(f32[2,32,256]{2,1,0:T(8,128)S(1)} %get-tuple-element.96), channel_id=1, source_target_pairs={{4,8},{8,4},{12,16},{16,12},{20,24},{24,20},{28,0},{0,28},{5,9},{9... | collective-permute-start | bytes 196616 | tf_op jit(solution)/shard_map/ppermute | solution.py:41
  39.1 2.9 %full.6.refs_5_ = f32[1,3072]{1,0:T(1,128)S(1)} custom-call(f32[8,3072]{1,0:T(8,128)S(1)} %get-tuple-element.59.refs_0_, f32[64,128]{1,0:T(8,128)S(1)} %get-tuple-element.100.refs_1_, s32[1152,128]{1,0:T(8,128)S(1)} %get-tuple-element.60.refs_0_.refs_2_, f32[32,128]{1,0:T(8,128)S(1)} %get-tuple-element.73.refs_0_.refs_3_, ...), custom_call_target="tpu_custom_call" | custom-call | flops 4000000000 | bytes 10000000 | tf_op jit(solution)/shard_map/full/pallas_call | solution.py:108
  42.0 2.1 %collective-permute-done.9.refs_19_ = f32[2,32,256]{2,1,0:T(8,128)S(1)} collective-permute-done((f32[2,32,256]{2,1,0:T(8,128)S(1)}, f32[2,32,256]{2,1,0:T(8,128)S(1)}, u32[]{:S(2)}, u32[]{:S(2)}) %collective-permute-start.9) | collective-permute-done | bytes 65568 | tf_op jit(solution)/shard_map/ppermute | solution.py:41
  44.1 1.7 %advance.7 = (bf16[128,1024]{1,0:T(8,128)(2,1)S(1)}, f32[64,128]{1,0:T(8,128)S(1)}, f32[8,16,128]{2,1,0:T(8,128)}) custom-call(f32[1,256]{1,0:T(1,128)S(1)} %copy-done.2, f32[1,256]{1,0:T(1,128)S(1)} %copy-done.3, f32[2,32,256]{2,1,0:T(8,128)S(1)} %get-tuple-element.85.refs_2_, f32[2,32,256]{2,1,0:T(8,128)S(1)} %get-tuple-element.92.refs_3_, ...), custom_call_target="tpu_custom_call" | custom-call | flops 1000000000 | bytes 4000000 | tf_op jit(solution)/shard_map/advance/pallas_call | solution.py:108
  45.8 4.0 %all-to-all-start = ((f32[8,16,128]{2,1,0:T(8,128)}), f32[8,16,128]{2,1,0:T(8,128)S(1)}, u32[]{:S(2)}, u32[]{:S(2)}) async-start(f32[8,16,128]{2,1,0:T(8,128)} %get-tuple-element.112), calls=%async_computation | async-start | bytes 131072 | tf_op jit(solution)/shard_map/all_to_all | solution.py:730
  49.7 2.8 %full.7 = (f32[1,3072]{1,0:T(1,128)S(1)}, f32[32,3072]{1,0:T(8,128)S(1)}) custom-call(f32[8,3072]{1,0:T(8,128)S(1)} %get-tuple-element.59.refs_0_, f32[64,128]{1,0:T(8,128)S(1)} %get-tuple-element.98.refs_1_, s32[1152,128]{1,0:T(8,128)S(1)} %get-tuple-element.60.refs_0_.refs_2_, f32[32,128]{1,0:T(8,128)S(1)} %get-tuple-element.73.refs_0_.refs_3_, ...), custom_call_target="tpu_custom_call" | custom-call | flops 4000000000 | bytes 10000000 | tf_op jit(solution)/shard_map/full/pallas_call | solution.py:108
  52.6 1.6 %collective-permute-start.12 = (f32[1,3072]{1,0:T(1,128)S(1)}, f32[1,3072]{1,0:T(1,128)S(1)}, u32[]{:S(2)}, u32[]{:S(2)}) collective-permute-start(f32[1,3072]{1,0:T(1,128)S(1)} %get-tuple-element.111.refs_1_), channel_id=1, source_target_pairs={{0,2},{1,3},{2,0},{3,1},{4,6},{5,7},{6,4},{7,5},{8,10},{9,11},{10,... | collective-permute-start | bytes 36872 | tf_op jit(solution)/shard_map/ppermute | solution.py:762
  54.5 0.8 %place.1 = (f32[1,128]{1,0:T(1,128)S(1)}, f32[32,3072]{1,0:T(8,128)}) custom-call(f32[32,3072]{1,0:T(8,128)S(1)} %get-tuple-element.108.refs_0_), custom_call_target="tpu_custom_call" | custom-call | flops 1000000000 | bytes 4000000 | tf_op jit(solution)/shard_map/place/pallas_call | solution.py:108
  56.7 0.8 %finish.1 = (f32[1,3072]{1,0:T(1,128)}, f32[32,128]{1,0:T(8,128)}) custom-call(f32[1,128]{1,0:T(1,128)S(1)} %get-tuple-element.110.refs_0_, f32[1,3072]{1,0:T(1,128)S(1)} %get-tuple-element.111.refs_1_, f32[1,3072]{1,0:T(1,128)S(1)} %collective-permute-done.11.refs_2_, f32[1,3072]{1,0:T(1,128)S(1)} %collective-permute-done.12.refs_3_, ...), custom_call_target="tpu_custom_call" | custom-call | flops 1000000000 | bytes 4000000 | tf_op jit(solution)/shard_map/finish/pallas_call | solution.py:108
  (32 shorter events, 2.6 us)
Async XLA Ops:
  1.9 5.5 %collective-permute-start.1 = (f32[4,40,128]{2,1,0:T(8,128)S(1)}, f32[4,40,128]{2,1,0:T(8,128)S(1)}, u32[]{:S(2)}, u32[]{:S(2)}) collective-permute-start(f32[4,40,128]{2,1,0:T(8,128)S(1)} %get-tuple-element.75), channel_id=1, source_target_pairs={{0,4},{4,0},{8,12},{12,8},{16,20},{20,16},{24,28},{28,24},{1,5},{5... | collective-permute-start | bytes 245768 | tf_op jit(solution)/shard_map/ppermute | solution.py:32
  7.2 9.4 %collective-permute-start = (f32[2,32,256]{2,1,0:T(8,128)S(1)}, f32[2,32,256]{2,1,0:T(8,128)S(1)}, u32[]{:S(2)}, u32[]{:S(2)}) collective-permute-start(f32[2,32,256]{2,1,0:T(8,128)S(1)} %get-tuple-element.67.refs_10_), channel_id=1, source_target_pairs={{0,4},{4,8},{8,12},{12,16},{16,20},{20,24},{24,28},{28,0},{1,5},{5... | collective-permute-start | bytes 196616 | tf_op jit(solution)/shard_map/ppermute | solution.py:27
  7.4 9.3 %collective-permute-start.2 = (f32[2,40,128]{2,1,0:T(8,128)S(1)}, f32[2,40,128]{2,1,0:T(8,128)S(1)}, u32[]{:S(2)}, u32[]{:S(2)}) collective-permute-start(f32[2,40,128]{2,1,0:T(8,128)S(1)} %get-tuple-element.76), channel_id=1, source_target_pairs={{0,24},{4,28},{8,16},{12,20},{16,8},{20,12},{24,0},{28,4},{1,25},{... | collective-permute-start | bytes 122888 | tf_op jit(solution)/shard_map/ppermute | solution.py:32
  11.5 5.1 %collective-permute-start.3 = (f32[2,40,128]{2,1,0:T(8,128)S(1)}, f32[2,40,128]{2,1,0:T(8,128)S(1)}, u32[]{:S(2)}, u32[]{:S(2)}) collective-permute-start(f32[2,40,128]{2,1,0:T(8,128)S(1)} %get-tuple-element.77), channel_id=1, source_target_pairs={{0,16},{4,20},{8,24},{12,28},{16,0},{20,4},{24,8},{28,12},{1,17},{... | collective-permute-start | bytes 122888 | tf_op jit(solution)/shard_map/ppermute | solution.py:32
  11.6 5.1 %collective-permute-start.4 = (f32[2,40,128]{2,1,0:T(8,128)S(1)}, f32[2,40,128]{2,1,0:T(8,128)S(1)}, u32[]{:S(2)}, u32[]{:S(2)}) collective-permute-start(f32[2,40,128]{2,1,0:T(8,128)S(1)} %get-tuple-element.78), channel_id=1, source_target_pairs={{0,8},{4,12},{8,0},{12,4},{16,24},{20,28},{24,16},{28,20},{1,9},{5... | collective-permute-start | bytes 122888 | tf_op jit(solution)/shard_map/ppermute | solution.py:32
  12.2 4.5 %copy-start = (f32[1,6,32,256]{3,2,1,0:T(8,128)S(1)}, f32[1,6,32,256]{3,2,1,0:T(8,128)}, u32[]{:S(2)}) copy-start(f32[1,6,32,256]{3,2,1,0:T(8,128)} %refs_9_.5) | copy-start | bytes 589828
  12.2 4.5 %copy-start.1 = (f32[1,6,32,256]{3,2,1,0:T(8,128)S(1)}, f32[1,6,32,256]{3,2,1,0:T(8,128)}, u32[]{:S(2)}) copy-start(f32[1,6,32,256]{3,2,1,0:T(8,128)} %refs_8_.3) | copy-start | bytes 589828
  12.2 4.5 %copy-start.2 = (f32[1,256]{1,0:T(1,128)S(1)}, f32[1,256]{1,0:T(1,128)}, u32[]{:S(2)}) copy-start(f32[1,256]{1,0:T(1,128)} %refs_0_.11) | copy-start | bytes 3076
  12.2 4.5 %copy-start.3 = (f32[1,256]{1,0:T(1,128)S(1)}, f32[1,256]{1,0:T(1,128)}, u32[]{:S(2)}) copy-start(f32[1,256]{1,0:T(1,128)} %refs_1_.11) | copy-start | bytes 3076
  12.2 4.5 %copy-start.4 = (s32[1,256]{1,0:T(1,128)S(1)}, s32[1,256]{1,0:T(1,128)}, u32[]{:S(2)}) copy-start(s32[1,256]{1,0:T(1,128)} %refs_6_.4) | copy-start | bytes 3076
  17.9 7.6 %collective-permute-start.5 = (f32[2,32,256]{2,1,0:T(8,128)S(1)}, f32[2,32,256]{2,1,0:T(8,128)S(1)}, u32[]{:S(2)}, u32[]{:S(2)}) collective-permute-start(f32[2,32,256]{2,1,0:T(8,128)S(1)} %get-tuple-element.83), channel_id=1, source_target_pairs={{4,8},{8,4},{12,16},{16,12},{20,24},{24,20},{28,0},{0,28},{5,9},{9... | collective-permute-start | bytes 196616 | tf_op jit(solution)/shard_map/ppermute | solution.py:41
  22.6 4.3 %collective-permute-start.6 = (f32[2,32,256]{2,1,0:T(8,128)S(1)}, f32[2,32,256]{2,1,0:T(8,128)S(1)}, u32[]{:S(2)}, u32[]{:S(2)}) collective-permute-start(f32[2,32,256]{2,1,0:T(8,128)S(1)} %get-tuple-element.84), channel_id=1, source_target_pairs={{0,4},{4,0},{8,12},{12,8},{16,20},{20,16},{24,28},{28,24},{1,5},{5... | collective-permute-start | bytes 196616 | tf_op jit(solution)/shard_map/ppermute | solution.py:41
  28.1 7.1 %collective-permute-start.7 = (f32[2,32,256]{2,1,0:T(8,128)S(1)}, f32[2,32,256]{2,1,0:T(8,128)S(1)}, u32[]{:S(2)}, u32[]{:S(2)}) collective-permute-start(f32[2,32,256]{2,1,0:T(8,128)S(1)} %get-tuple-element.90), channel_id=1, source_target_pairs={{4,8},{8,4},{12,16},{16,12},{20,24},{24,20},{28,0},{0,28},{5,9},{9... | collective-permute-start | bytes 196616 | tf_op jit(solution)/shard_map/ppermute | solution.py:41
  30.9 5.0 %collective-permute-start.8 = (f32[2,32,256]{2,1,0:T(8,128)S(1)}, f32[2,32,256]{2,1,0:T(8,128)S(1)}, u32[]{:S(2)}, u32[]{:S(2)}) collective-permute-start(f32[2,32,256]{2,1,0:T(8,128)S(1)} %get-tuple-element.91), channel_id=1, source_target_pairs={{0,4},{4,0},{8,12},{12,8},{16,20},{20,16},{24,28},{28,24},{1,5},{5... | collective-permute-start | bytes 196616 | tf_op jit(solution)/shard_map/ppermute | solution.py:41
  37.0 7.1 %collective-permute-start.9 = (f32[2,32,256]{2,1,0:T(8,128)S(1)}, f32[2,32,256]{2,1,0:T(8,128)S(1)}, u32[]{:S(2)}, u32[]{:S(2)}) collective-permute-start(f32[2,32,256]{2,1,0:T(8,128)S(1)} %get-tuple-element.96), channel_id=1, source_target_pairs={{4,8},{8,4},{12,16},{16,12},{20,24},{24,20},{28,0},{0,28},{5,9},{9... | collective-permute-start | bytes 196616 | tf_op jit(solution)/shard_map/ppermute | solution.py:41
  39.1 5.0 %collective-permute-start.10 = (f32[2,32,256]{2,1,0:T(8,128)S(1)}, f32[2,32,256]{2,1,0:T(8,128)S(1)}, u32[]{:S(2)}, u32[]{:S(2)}) collective-permute-start(f32[2,32,256]{2,1,0:T(8,128)S(1)} %get-tuple-element.97), channel_id=1, source_target_pairs={{0,4},{4,0},{8,12},{12,8},{16,20},{20,16},{24,28},{28,24},{1,5},{5... | collective-permute-start | bytes 196616 | tf_op jit(solution)/shard_map/ppermute | solution.py:41
  45.8 10.9 %all-to-all-start = ((f32[8,16,128]{2,1,0:T(8,128)}), f32[8,16,128]{2,1,0:T(8,128)S(1)}, u32[]{:S(2)}, u32[]{:S(2)}) async-start(f32[8,16,128]{2,1,0:T(8,128)} %get-tuple-element.112), calls=%async_computation | async-start | bytes 131072 | tf_op jit(solution)/shard_map/all_to_all | solution.py:730
  52.6 4.1 %copy-start.5 = (s32[1,128]{1,0:T(1,128)S(1)}, s32[1,128]{1,0:T(1,128)}, u32[]{:S(2)}) copy-start(s32[1,128]{1,0:T(1,128)} %refs_6_.5) | copy-start | bytes 1540
  52.6 3.2 %collective-permute-start.13 = (f32[1,3072]{1,0:T(1,128)S(1)}, f32[1,3072]{1,0:T(1,128)S(1)}, u32[]{:S(2)}, u32[]{:S(2)}) collective-permute-start(f32[1,3072]{1,0:T(1,128)S(1)} %get-tuple-element.111.refs_1_), channel_id=1, source_target_pairs={{0,3},{1,2},{2,1},{3,0},{4,7},{5,6},{6,5},{7,4},{8,11},{9,10},{10,... | collective-permute-start | bytes 36872 | tf_op jit(solution)/shard_map/ppermute | solution.py:762
  52.6 3.8 %collective-permute-start.12 = (f32[1,3072]{1,0:T(1,128)S(1)}, f32[1,3072]{1,0:T(1,128)S(1)}, u32[]{:S(2)}, u32[]{:S(2)}) collective-permute-start(f32[1,3072]{1,0:T(1,128)S(1)} %get-tuple-element.111.refs_1_), channel_id=1, source_target_pairs={{0,2},{1,3},{2,0},{3,1},{4,6},{5,7},{6,4},{7,5},{8,10},{9,11},{10,... | collective-permute-start | bytes 36872 | tf_op jit(solution)/shard_map/ppermute | solution.py:762
  54.2 2.2 %collective-permute-start.11 = (f32[1,3072]{1,0:T(1,128)S(1)}, f32[1,3072]{1,0:T(1,128)S(1)}, u32[]{:S(2)}, u32[]{:S(2)}) collective-permute-start(f32[1,3072]{1,0:T(1,128)S(1)} %get-tuple-element.111.refs_1_), channel_id=1, source_target_pairs={{0,1},{1,0},{2,3},{3,2},{4,5},{5,4},{6,7},{7,6},{8,9},{9,8},{10,11... | collective-permute-start | bytes 36872 | tf_op jit(solution)/shard_map/ppermute | solution.py:762
